TPU v7x, 256 devices: a whole 4x4x8 slice. The times are simulated.
256 devices in a mesh: frame: 32 (over z, y_hi, core), head: 8 (over x, y_lo).
Axes of the slice: x: 4, y: 4 (y_hi: 2, y_lo: 2; y = y_hi * 2 + y_lo), z: 8, core: 2. Of those that a mesh axis runs over, the one named last changes fastest.
Arguments:
- queries: bfloat16 [32768, 3072], P(('frame', 'head')), may hold values from -64 to 64, as said below
- key_rows: bfloat16 [32768, 3072], P(('frame', 'head')), may hold values from -64 to 64, as said below
- value_rows: bfloat16 [32768, 3072], P(('frame', 'head')), may hold values from -24 to 24
- block_mask: int32 [256, 256], replicated, may hold values from 0 to 1, as said below
Outputs:
- attended: bfloat16 [32768, 3072], P(('frame', 'head'))
Inputs may be any that keep to these rules, and one draw needn't show every extreme that they name: block_mask holds 0 or 1; every query block attends to all key blocks of its own frame; for two frames two or more apart, the query blocks of one attend to exactly one key block of the other (the same one for all of them), and some query blocks may attend to none of it. queries are finite reals. `key_rows`: keys are finite reals.
All inputs are finite; a program needn't handle non-finite values.
Results may differ from a plain program's by a relative error of at most 0.0037.
Values may be sent and summed in bfloat16 or wider, within the bound.
No kernel may reach another device: no remote copies, remote signals or barrier semaphores. Data moves between devices by JAX's collectives and lax.ppermute only.
A program may use at most 128 MiB of HBM per device.

v0:
```python
import math

import jax
import jax.numpy as jnp
from jax import lax
from jax.sharding import PartitionSpec as P

HDIM = 128
BLOCK = 128
BF = 8


def padded(value, sides, width):
    for axis, dim in sides:
        peers, length = (lax.axis_size(axis), value.shape[dim])
        up = [(i, (i + 1) % peers) for i in range(peers - 1)]
        down = [(j, i) for i, j in up]
        last = lax.slice_in_dim(value, length - width, length, axis=dim)
        first = lax.slice_in_dim(value, 0, width, axis=dim)
        before = lax.ppermute(last, axis, up)
        after = lax.ppermute(first, axis, down)
        value = jnp.concatenate([before, value, after], axis=dim)
    return value


def masked_scores(query_part, key_part, block_rows, score_scale):
    scores = (
        jnp.einsum("thd,uhd->htu", query_part, key_part, preferred_element_type=jnp.float32)
        * score_scale
    )
    heads, rows, cols = scores.shape
    shaped = scores.reshape(heads, rows // BLOCK, BLOCK, cols // BLOCK, BLOCK)
    shaped = jnp.where(block_rows[None, :, None, :, None], shaped, -1e30)
    return shaped.reshape(heads, rows, cols)


def body(queries, key_rows, value_rows, block_mask):
    frame_count = lax.axis_size("frame")
    frame_id = lax.axis_index("frame")
    width_local = queries.shape[1] // lax.axis_size("head")
    head_count = width_local // HDIM
    frame_len = BF * BLOCK
    score_scale = 1.0 / math.sqrt(HDIM)
    query_frame, key_frame, value_frame = (
        lax.all_to_all(queries, "head", split_axis=1, concat_axis=0, tiled=True),
        lax.all_to_all(key_rows, "head", split_axis=1, concat_axis=0, tiled=True),
        lax.all_to_all(value_rows, "head", split_axis=1, concat_axis=0, tiled=True),
    )
    paired = jnp.concatenate([key_frame, value_frame], axis=1)
    beside = padded(paired, (("frame", 0),), frame_len)
    mask_grid = block_mask.reshape(frame_count, BF, frame_count, BF)
    block_ids = jnp.arange(BF, dtype=jnp.int32)
    towards = lax.dynamic_index_in_dim(mask_grid, frame_id, 2, keepdims=False)
    outgoing = jnp.minimum(jnp.sum(jnp.max(towards, axis=1) * block_ids[None, :], axis=1), BF - 1)
    blocks = paired.reshape(BF, BLOCK, 2 * width_local)
    parcel = jnp.take(blocks, outgoing, axis=0)
    distant_kv = lax.all_to_all(parcel, "frame", split_axis=0, concat_axis=0, tiled=True).reshape(
        frame_count * BLOCK, 2 * width_local
    )
    own_rows = lax.dynamic_index_in_dim(mask_grid, frame_id, 0, keepdims=False)
    incoming = jnp.minimum(jnp.sum(jnp.max(own_rows, axis=0) * block_ids[None, :], axis=1), BF - 1)
    padded_rows = jnp.pad(own_rows, ((0, 0), (1, 1), (0, 0)))
    near_mask = lax.dynamic_slice_in_dim(padded_rows, frame_id, 3, 1).reshape(BF, 3 * BF)
    match = (block_ids[None, None, :] == incoming[None, :, None]).astype(jnp.int32)
    far_mask = jnp.sum(own_rows * match, axis=2)
    frame_ids = jnp.arange(frame_count, dtype=jnp.int32)
    distant = (jnp.abs(frame_ids - frame_id) >= 2).astype(jnp.int32)
    far_mask = far_mask * distant[None, :]
    near_on = near_mask > 0
    far_on = far_mask > 0
    joint_on = jnp.concatenate([near_on, far_on], axis=1)
    near_keys = beside[:, :width_local].reshape(3 * frame_len, head_count, HDIM)
    near_values = beside[:, width_local:].reshape(3 * frame_len, head_count, HDIM)
    far_keys = distant_kv[:, :width_local].reshape(frame_count * BLOCK, head_count, HDIM)
    far_values = distant_kv[:, width_local:].reshape(frame_count * BLOCK, head_count, HDIM)
    all_keys = jnp.concatenate([near_keys, far_keys], axis=0)
    all_values = jnp.concatenate([near_values, far_values], axis=0)
    query_heads = query_frame.reshape(frame_len, head_count, HDIM)
    step_blocks = math.gcd(BF, max(1, 256 // BLOCK))
    row_step = step_blocks * BLOCK

    def one_step(step_no):
        row_start = step_no * row_step
        block_start = step_no * step_blocks
        query_part = lax.dynamic_slice_in_dim(query_heads, row_start, row_step, 0)
        rows_on = lax.dynamic_slice_in_dim(joint_on, block_start, step_blocks, 0)
        scores = masked_scores(query_part, all_keys, rows_on, score_scale)
        row_top = jnp.max(scores, axis=2, keepdims=True)
        weights = jnp.exp(scores - row_top)
        denominator = jnp.sum(weights, axis=2)
        summed = jnp.einsum(
            "htu,uhd->thd",
            weights.astype(jnp.bfloat16),
            all_values,
            preferred_element_type=jnp.float32,
        )
        scaled = summed / jnp.transpose(denominator)[:, :, None]
        return scaled.astype(jnp.bfloat16).reshape(row_step, width_local)

    stacked = lax.map(one_step, jnp.arange(BF // step_blocks, dtype=jnp.int32))
    result = stacked.reshape(frame_len, width_local)
    return lax.all_to_all(result, "head", split_axis=0, concat_axis=1, tiled=True)


def solution(mesh):
    placed = (
        P(("frame", "head"), None),
        P(("frame", "head"), None),
        P(("frame", "head"), None),
        P(),
    )
    return jax.shard_map(
        body, mesh=mesh, in_specs=placed, out_specs=P(("frame", "head"), None), check_vma=False
    )
```

profile of v0, /device:TPU:32, one launch (start us, length us, event | category | flops | bytes accessed | tf_op | source)
XLA Modules:
  0.0 439.4 jit_solution(16061372058998671965)
XLA Ops:
  0.0 1.5 copy.65
  1.6 1.2 copy.66
  2.7 5.4 %all-to-all-start.2 = ((bf16[128,8,384]{2,0,1:T(8,128)(2,1)}), bf16[128,8,384]{2,0,1:T(8,128)(2,1)S(1)}, u32[]{:S(2)}, u32[]{:S(2)}) async-start(bf16[128,8,384]{2,0,1:T(8,128)(2,1)} %copy.66), calls=%async_computation.2 | async-start | bytes 1572864 | tf_op jit(solution)/shard_map/all_to_all | solution.py:47
  8.2 1.5 copy.63
  9.7 1.2 copy.64
  10.8 9.7 %all-to-all-done.2 = bf16[128,8,384]{2,0,1:T(8,128)(2,1)S(1)} async-done(((bf16[128,8,384]{2,0,1:T(8,128)(2,1)}), bf16[128,8,384]{2,0,1:T(8,128)(2,1)S(1)}, u32[]{:S(2)}, u32[]{:S(2)}) %all-to-all-start.2) | async-done | bytes 786464 | tf_op jit(solution)/shard_map/all_to_all | solution.py:47
  20.5 3.5 all-to-all-start.1
  24.1 3.6 reshape.114
  27.8 1.2 copy.61
  28.9 1.5 dynamic-slice_reduce_fusion
  30.5 5.2 %all-to-all-done.1 = bf16[128,8,384]{2,0,1:T(8,128)(2,1)S(1)} async-done(((bf16[128,8,384]{2,0,1:T(8,128)(2,1)}), bf16[128,8,384]{2,0,1:T(8,128)(2,1)S(1)}, u32[]{:S(2)}, u32[]{:S(2)}) %all-to-all-start.1) | async-done | bytes 786464 | tf_op jit(solution)/shard_map/all_to_all | solution.py:46
  35.7 4.2 all-to-all-start
  40.1 3.6 gather_fusion
  43.7 6.1 %broadcast_select_fusion = bf16[32,128,768]{2,1,0:T(8,128)(2,1)} fusion(bf16[32,128,768]{2,1,0:T(8,128)(2,1)} %gather_fusion, pred[32]{0:T(512)(128)(4,1)S(1)} %compare_and_fusion), kind=kLoop, calls=%fused_computation.19 | loop fusion | flops 3145728 | bytes 12582944 | tf_op jit(solution)/shard_map/jit(_take)/select_n | solution.py:56
  49.8 1.2 all-to-all-done
  51.1 11.1 %all-to-all-start.3 = ((bf16[32,128,768]{2,1,0:T(8,128)(2,1)}), bf16[32,128,768]{2,1,0:T(8,128)(2,1)}, u32[]{:S(2)}, u32[]{:S(2)}) async-start(bf16[32,128,768]{2,1,0:T(8,128)(2,1)} %broadcast_select_fusion), calls=%async_computation.3 | async-start | bytes 12582912 | tf_op jit(solution)/shard_map/all_to_all | solution.py:57
  62.8 1.3 pad_maximum_fusion.3
  64.0 2.0 collective-permute-start
  66.1 6.1 %collective-permute-start.1 = (bf16[1024,768]{0,1:T(8,128)(2,1)}, bf16[1024,768]{0,1:T(8,128)(2,1)}, u32[]{:S(2)}, u32[]{:S(2)}) collective-permute-start(bf16[1024,768]{0,1:T(8,128)(2,1)} %pad_maximum_fusion.3), channel_id=1, source_target_pairs={{8,0},{16,8},{24,16},{32,24},{40,32},{48,40},{56,48},{64,56},{72,6... | collective-permute-start | bytes 4718600 | tf_op jit(solution)/shard_map/ppermute | solution.py:21
  72.2 0.9 dynamic-slice_reduce_fusion.1
  73.3 1.1 multiply_reduce_fusion
  74.7 1.6 copy.62
  76.3 1.2 reshape.115
  77.6 140.6 %collective-permute-done = bf16[1024,768]{0,1:T(8,128)(2,1)} collective-permute-done((bf16[1024,768]{0,1:T(8,128)(2,1)}, bf16[1024,768]{0,1:T(8,128)(2,1)}, u32[]{:S(2)}, u32[]{:S(2)}) %collective-permute-start) | collective-permute-done | bytes 1572896 | tf_op jit(solution)/shard_map/ppermute | solution.py:20
  218.2 13.0 %pad_maximum_fusion.2 = bf16[3072,768]{0,1:T(8,128)(2,1)S(1)} fusion(bf16[1024,768]{0,1:T(8,128)(2,1)} %collective-permute-done.1, bf16[1024,384]{0,1:T(8,128)(2,1)S(1)} %copy.68, bf16[1024,384]{0,1:T(8,128)(2,1)S(1)} %copy.67, bf16[1024,768]{0,1:T(8,128)(2,1)} %collective-permute-done), kind=kLoop, calls=%fused_computation.22 | loop fusion | flops 18874368 | bytes 9437184 | tf_op jit(solution)/shard_map/concatenate | solution.py:22
  231.1 2.4 fusion.24
  233.6 6.1 %fusion.23 = (bf16[4096,384]{1,0:T(8,128)(2,1)}, bf16[4096,384]{1,0:T(8,128)(2,1)}) fusion(bf16[4096,768]{1,0:T(8,128)(2,1)} %bitcast.17), kind=kLoop, calls=%fused_computation.44 | loop fusion | bytes 12582912 | tf_op jit(solution)/shard_map/slice | solution.py:75
  239.7 3.2 copy.71
  242.9 4.8 %copy.82 = bf16[4096,384]{0,1:T(8,128)(2,1)} copy(bf16[4096,384]{1,0:T(8,128)(2,1)} %get-tuple-element.97) | data formatting | bytes 6291456
  247.7 5.4 %pad_maximum_fusion = bf16[7168,3,128]{0,2,1:T(8,128)(2,1)} fusion(bf16[4096,3,128]{0,2,1:T(8,128)(2,1)} %bitcast.67, bf16[3072,3,128]{0,2,1:T(8,128)(2,1)} %bitcast.69), kind=kLoop, calls=%fused_computation.20 | loop fusion | flops 11010048 | bytes 11010048 | tf_op jit(solution)/shard_map/concatenate | solution.py:76
  253.1 8.3 %copy.73 = bf16[7168,3,128]{2,0,1:T(8,128)(2,1)} copy(bf16[7168,3,128]{0,2,1:T(8,128)(2,1)} %pad_maximum_fusion) | data formatting | bytes 11010048 | tf_op jit(solution)/shard_map/while | solution.py:100
  261.4 4.5 %pad_maximum_fusion.1 = bf16[7168,3,128]{0,2,1:T(8,128)(2,1)} fusion(bf16[4096,3,128]{0,2,1:T(8,128)(2,1)S(1)} %bitcast.66, bf16[3072,3,128]{0,2,1:T(8,128)(2,1)} %bitcast.68), kind=kLoop, calls=%fused_computation.21 | loop fusion | flops 11010048 | bytes 11010048 | tf_op jit(solution)/shard_map/concatenate | solution.py:77
  265.9 158.5 %while.10 = (s32[]{:T(128)}, bf16[4,256,384]{2,1,0:T(8,128)(2,1)}, s32[4]{0:T(128)S(1)}, pred[8,56]{1,0:T(8,128)(4,1)S(1)}, bf16[1024,3,128]{0,2,1:T(8,128)(2,1)...) while((s32[]{:T(128)}, bf16[4,256,384]{2,1,0:T(8,128)(2,1)}, ...), condition=%wide.region_8.9_spmd, body=%wide.region_5.8_spmd.sunk | while | flops 2879322624 | bytes 89276480 | solution.py:100
  267.8 0.9 copy.88
  269.4 11.8 %fusion.36 = (f32[3,256]{1,0:T(4,128)S(1)}, f32[3,256,7168]{2,1,0:T(8,128)}) fusion(pred[256,7168]{1,0:T(8,128)(4,1)S(1)} %bitcast.63, bf16[7168,3,128]{2,0,1:T(8,128)(2,1)} %get-tuple-element.178, bf16[1024,3,128]{0,2,1:T(8,128)(2,1)} %get-tuple-element.177, s32[]{:T(128)S(6)} %select_n.77), kind=kOutput, calls=%fused_computation.3.clone.1 | convolution fusion | flops 1425800448 | bytes 29559812 | tf_op jit(solution)/shard_map/while/body/eval_jaxpr/thd,uhd->htu/dot_general | solution.py:28
  281.2 10.9 %fusion.37 = f32[3,256]{1,0:T(4,128)S(1)} fusion(f32[3,256,7168]{2,1,0:T(8,128)} %get-tuple-element.145, f32[3,256]{1,0:T(4,128)S(1)} %get-tuple-element.146, pred[256,7168]{1,0:T(8,128)(4,1)S(1)} %bitcast.64), kind=kLoop, calls=%fused_computation.4.clone.1 | loop fusion | flops 22019328 | bytes 23861248 | tf_op jit(solution)/shard_map/while/body/eval_jaxpr/reduce_sum | solution.py:90
  292.1 12.5 %fusion.38 = bf16[256,3,128]{0,2,1:T(8,128)(2,1)S(1)} fusion(bf16[7168,3,128]{0,2,1:T(8,128)(2,1)} %get-tuple-element.179, f32[3,256,7168]{2,1,0:T(8,128)} %get-tuple-element.145, f32[3,256]{1,0:T(4,128)S(1)} %get-tuple-element.146, pred[256,7168]{1,0:T(8,128)(4,1)S(1)} %bitcast.65, f32[256,3]{0,1:T(4,128)S(1)} %bitcast.80), kind=kOutput, calls=%fused_computation.11.clone.1 | convolution fusion | flops 1431502848 | bytes 29562880 | tf_op jit(solution)/shard_map/while/body/eval_jaxpr/htu,uhd->thd/dot_general | solution.py:91
  309.0 11.8 %fusion.36 = (f32[3,256]{1,0:T(4,128)S(1)}, f32[3,256,7168]{2,1,0:T(8,128)}) fusion(pred[256,7168]{1,0:T(8,128)(4,1)S(1)} %bitcast.63, bf16[7168,3,128]{2,0,1:T(8,128)(2,1)} %get-tuple-element.178, bf16[1024,3,128]{0,2,1:T(8,128)(2,1)} %get-tuple-element.177, s32[]{:T(128)S(6)} %select_n.77), kind=kOutput, calls=%fused_computation.3.clone.1 | convolution fusion | flops 1425800448 | bytes 29559812 | tf_op jit(solution)/shard_map/while/body/eval_jaxpr/thd,uhd->htu/dot_general | solution.py:28
  320.8 10.9 %fusion.37 = f32[3,256]{1,0:T(4,128)S(1)} fusion(f32[3,256,7168]{2,1,0:T(8,128)} %get-tuple-element.145, f32[3,256]{1,0:T(4,128)S(1)} %get-tuple-element.146, pred[256,7168]{1,0:T(8,128)(4,1)S(1)} %bitcast.64), kind=kLoop, calls=%fused_computation.4.clone.1 | loop fusion | flops 22019328 | bytes 23861248 | tf_op jit(solution)/shard_map/while/body/eval_jaxpr/reduce_sum | solution.py:90
  331.7 12.5 %fusion.38 = bf16[256,3,128]{0,2,1:T(8,128)(2,1)S(1)} fusion(bf16[7168,3,128]{0,2,1:T(8,128)(2,1)} %get-tuple-element.179, f32[3,256,7168]{2,1,0:T(8,128)} %get-tuple-element.145, f32[3,256]{1,0:T(4,128)S(1)} %get-tuple-element.146, pred[256,7168]{1,0:T(8,128)(4,1)S(1)} %bitcast.65, f32[256,3]{0,1:T(4,128)S(1)} %bitcast.80), kind=kOutput, calls=%fused_computation.11.clone.1 | convolution fusion | flops 1431502848 | bytes 29562880 | tf_op jit(solution)/shard_map/while/body/eval_jaxpr/htu,uhd->thd/dot_general | solution.py:91
  348.6 11.8 %fusion.36 = (f32[3,256]{1,0:T(4,128)S(1)}, f32[3,256,7168]{2,1,0:T(8,128)}) fusion(pred[256,7168]{1,0:T(8,128)(4,1)S(1)} %bitcast.63, bf16[7168,3,128]{2,0,1:T(8,128)(2,1)} %get-tuple-element.178, bf16[1024,3,128]{0,2,1:T(8,128)(2,1)} %get-tuple-element.177, s32[]{:T(128)S(6)} %select_n.77), kind=kOutput, calls=%fused_computation.3.clone.1 | convolution fusion | flops 1425800448 | bytes 29559812 | tf_op jit(solution)/shard_map/while/body/eval_jaxpr/thd,uhd->htu/dot_general | solution.py:28
  360.4 10.9 %fusion.37 = f32[3,256]{1,0:T(4,128)S(1)} fusion(f32[3,256,7168]{2,1,0:T(8,128)} %get-tuple-element.145, f32[3,256]{1,0:T(4,128)S(1)} %get-tuple-element.146, pred[256,7168]{1,0:T(8,128)(4,1)S(1)} %bitcast.64), kind=kLoop, calls=%fused_computation.4.clone.1 | loop fusion | flops 22019328 | bytes 23861248 | tf_op jit(solution)/shard_map/while/body/eval_jaxpr/reduce_sum | solution.py:90
  371.3 12.5 %fusion.38 = bf16[256,3,128]{0,2,1:T(8,128)(2,1)S(1)} fusion(bf16[7168,3,128]{0,2,1:T(8,128)(2,1)} %get-tuple-element.179, f32[3,256,7168]{2,1,0:T(8,128)} %get-tuple-element.145, f32[3,256]{1,0:T(4,128)S(1)} %get-tuple-element.146, pred[256,7168]{1,0:T(8,128)(4,1)S(1)} %bitcast.65, f32[256,3]{0,1:T(4,128)S(1)} %bitcast.80), kind=kOutput, calls=%fused_computation.11.clone.1 | convolution fusion | flops 1431502848 | bytes 29562880 | tf_op jit(solution)/shard_map/while/body/eval_jaxpr/htu,uhd->thd/dot_general | solution.py:91
  388.2 11.8 %fusion.36 = (f32[3,256]{1,0:T(4,128)S(1)}, f32[3,256,7168]{2,1,0:T(8,128)}) fusion(pred[256,7168]{1,0:T(8,128)(4,1)S(1)} %bitcast.63, bf16[7168,3,128]{2,0,1:T(8,128)(2,1)} %get-tuple-element.178, bf16[1024,3,128]{0,2,1:T(8,128)(2,1)} %get-tuple-element.177, s32[]{:T(128)S(6)} %select_n.77), kind=kOutput, calls=%fused_computation.3.clone.1 | convolution fusion | flops 1425800448 | bytes 29559812 | tf_op jit(solution)/shard_map/while/body/eval_jaxpr/thd,uhd->htu/dot_general | solution.py:28
  400.0 10.9 %fusion.37 = f32[3,256]{1,0:T(4,128)S(1)} fusion(f32[3,256,7168]{2,1,0:T(8,128)} %get-tuple-element.145, f32[3,256]{1,0:T(4,128)S(1)} %get-tuple-element.146, pred[256,7168]{1,0:T(8,128)(4,1)S(1)} %bitcast.64), kind=kLoop, calls=%fused_computation.4.clone.1 | loop fusion | flops 22019328 | bytes 23861248 | tf_op jit(solution)/shard_map/while/body/eval_jaxpr/reduce_sum | solution.py:90
  410.9 12.5 %fusion.38 = bf16[256,3,128]{0,2,1:T(8,128)(2,1)S(1)} fusion(bf16[7168,3,128]{0,2,1:T(8,128)(2,1)} %get-tuple-element.179, f32[3,256,7168]{2,1,0:T(8,128)} %get-tuple-element.145, f32[3,256]{1,0:T(4,128)S(1)} %get-tuple-element.146, pred[256,7168]{1,0:T(8,128)(4,1)S(1)} %bitcast.65, f32[256,3]{0,1:T(4,128)S(1)} %bitcast.80), kind=kOutput, calls=%fused_computation.11.clone.1 | convolution fusion | flops 1431502848 | bytes 29562880 | tf_op jit(solution)/shard_map/while/body/eval_jaxpr/htu,uhd->thd/dot_general | solution.py:91
  424.4 13.5 %all_to_all.78 = bf16[8,128,384]{2,1,0:T(8,128)(2,1)S(1)} all-to-all(bf16[8,128,384]{2,1,0:T(8,128)(2,1)} %bitcast.79), channel_id=1, replica_groups=mesh['frame'=32,'head'=8] {'head'}, dimensions={0} | all-to-all | bytes 1572864 | tf_op jit(solution)/shard_map/all_to_all | solution.py:102
  438.2 1.2 copy.76
  (47 shorter events, 12.6 us)
Async XLA Ops:
  0.0 24.1 %copy-start.1 = (s32[256,256]{1,0:T(8,128)S(1)}, s32[256,256]{1,0:T(8,128)}, u32[]{:S(2)}) copy-start(s32[256,256]{1,0:T(8,128)} %param.9) | copy-start | bytes 786436
  2.7 25.0 %copy-start = (bf16[128,3072]{1,0:T(8,128)(2,1)S(1)}, bf16[128,3072]{1,0:T(8,128)(2,1)}, u32[]{:S(2)}) copy-start(bf16[128,3072]{1,0:T(8,128)(2,1)} %param.6) | copy-start | bytes 2359300
  2.7 17.8 %all-to-all-start.2 = ((bf16[128,8,384]{2,0,1:T(8,128)(2,1)}), bf16[128,8,384]{2,0,1:T(8,128)(2,1)S(1)}, u32[]{:S(2)}, u32[]{:S(2)}) async-start(bf16[128,8,384]{2,0,1:T(8,128)(2,1)} %copy.66), calls=%async_computation.2 | async-start | bytes 1572864 | tf_op jit(solution)/shard_map/all_to_all | solution.py:47
  20.5 15.2 %all-to-all-start.1 = ((bf16[128,8,384]{2,0,1:T(8,128)(2,1)}), bf16[128,8,384]{2,0,1:T(8,128)(2,1)S(1)}, u32[]{:S(2)}, u32[]{:S(2)}) async-start(bf16[128,8,384]{2,0,1:T(8,128)(2,1)} %copy.64), calls=%async_computation.1 | async-start | bytes 1572864 | tf_op jit(solution)/shard_map/all_to_all | solution.py:46
  35.7 15.3 %all-to-all-start = ((bf16[128,8,384]{0,2,1:T(8,128)(2,1)}), bf16[128,8,384]{0,2,1:T(8,128)(2,1)}, u32[]{:S(2)}, u32[]{:S(2)}) async-start(bf16[128,8,384]{0,2,1:T(8,128)(2,1)} %bitcast.6), calls=%async_computation | async-start | bytes 1572864 | tf_op jit(solution)/shard_map/all_to_all | solution.py:45
  51.1 182.5 %all-to-all-start.3 = ((bf16[32,128,768]{2,1,0:T(8,128)(2,1)}), bf16[32,128,768]{2,1,0:T(8,128)(2,1)}, u32[]{:S(2)}, u32[]{:S(2)}) async-start(bf16[32,128,768]{2,1,0:T(8,128)(2,1)} %broadcast_select_fusion), calls=%async_computation.3 | async-start | bytes 12582912 | tf_op jit(solution)/shard_map/all_to_all | solution.py:57
  64.0 154.1 %collective-permute-start = (bf16[1024,768]{0,1:T(8,128)(2,1)}, bf16[1024,768]{0,1:T(8,128)(2,1)}, u32[]{:S(2)}, u32[]{:S(2)}) collective-permute-start(bf16[1024,768]{0,1:T(8,128)(2,1)} %pad_maximum_fusion.3), channel_id=1, source_target_pairs={{0,8},{8,16},{16,24},{24,32},{32,40},{40,48},{48,56},{56,64},{64,7... | collective-permute-start | bytes 4718600 | tf_op jit(solution)/shard_map/ppermute | solution.py:20
  66.1 152.1 %collective-permute-start.1 = (bf16[1024,768]{0,1:T(8,128)(2,1)}, bf16[1024,768]{0,1:T(8,128)(2,1)}, u32[]{:S(2)}, u32[]{:S(2)}) collective-permute-start(bf16[1024,768]{0,1:T(8,128)(2,1)} %pad_maximum_fusion.3), channel_id=1, source_target_pairs={{8,0},{16,8},{24,16},{32,24},{40,32},{48,40},{56,48},{64,56},{72,6... | collective-permute-start | bytes 4718600 | tf_op jit(solution)/shard_map/ppermute | solution.py:21
where the time goes:
time: 441 us; the launch traced here: 439 us
  waiting for transfers between devices  157 us (36%)
  matrix products  97.3 us (22%)
  other arithmetic  77.9 us (18%)
  local copies, waits for them, and re-layouts  55.5 us (13%)
  starting transfers between devices  32.5 us (7%)
  blocking collectives  13.5 us (3%)
  loops' own time  5.72 us (1%)
    ppermute x1, waiting for transfers between devices, padded(): before = lax.ppermute(last, axis, up)  141 us
    dot_general x4, matrix products, one_step(): jnp.einsum('htu,uhd->thd', weights.astype(jnp.bfloat16), all_values, pref...  50.2 us
    dot_general x4, matrix products, masked_scores(): jnp.einsum('thd,uhd->htu', query_part, key_part, preferred_element_type=j...  47.2 us
    reduce_sum x4, other arithmetic, one_step(): denominator = jnp.sum(weights, axis=2)  43.6 us
    all_to_all x1, blocking collectives, body(): lax.all_to_all(result, 'head', split_axis=0, concat_axis=1, tiled=True)  13.5 us
    concatenate x1, other arithmetic, padded(): value = jnp.concatenate([before, value, after], axis=dim)  13 us
    all_to_all x1, starting transfers between devices, body(): lax.all_to_all(parcel, 'frame', split_axis=0, concat_axis=0, tiled=True)  11.1 us
    all_to_all x1, waiting for transfers between devices, body(): lax.all_to_all(value_rows, 'head', split_axis=1, concat_axis=0, tiled=True)  9.7 us
  transfers between devices with their start and end apart: 6, of which 4 were waited for; matrix products, arithmetic and copies ran while one was open for 9% of the time, Pallas kernels for 0%

commit v1 on v0

v1 whole, which is shorter than its diff:
```python
import functools
import math

import jax
import jax.numpy as jnp
from jax import lax
from jax.experimental import pallas as pl
from jax.experimental.pallas import tpu as pltpu
from jax.sharding import PartitionSpec as P

HDIM = 128
BLOCK = 128
BF = 8
FT = BF * BLOCK
HEADS_LOCAL = 3
GROUP = 4
NEG = -1e30
SCALE2 = math.log2(math.e) / math.sqrt(HDIM)
NT = (((1,), (1,)), ((), ()))
NN = (((1,), (0,)), ((), ()))


def dot(a, b, dims):
    return lax.dot_general(a, b, dims, preferred_element_type=jnp.float32)


def pack_kernel(q_ref, k_ref, v_ref, out_ref):
    heads = q_ref.shape[1] // HDIM
    for h in range(heads):
        cols = slice(h * HDIM, (h + 1) * HDIM)
        base = 2 * h * HDIM
        out_ref[0, :, base : base + HDIM] = k_ref[:, cols]
        out_ref[0, :, base + HDIM : base + 2 * HDIM] = v_ref[:, cols]
    out_ref[0, :, 2 * heads * HDIM :] = q_ref[...]


def pack(queries, keys, values, peers):
    rows, width = queries.shape
    local = width // peers
    spec = pl.BlockSpec((rows, local), lambda j: (0, j))
    return pl.pallas_call(
        pack_kernel,
        grid=(peers,),
        in_specs=[spec] * 3,
        out_specs=pl.BlockSpec((1, rows, 3 * local), lambda j: (j, 0, 0)),
        out_shape=jax.ShapeDtypeStruct((peers, rows, 3 * local), queries.dtype),
        name="pack",
    )(queries, keys, values)


def unpack_kernel(part_ref, out_ref):
    out_ref[...] = part_ref[0]


def unpack(parts):
    peers, rows, local = parts.shape
    return pl.pallas_call(
        unpack_kernel,
        grid=(peers,),
        in_specs=[pl.BlockSpec((1, rows, local), lambda j: (j, 0, 0))],
        out_specs=pl.BlockSpec((rows, local), lambda j: (0, j)),
        out_shape=jax.ShapeDtypeStruct((rows, peers * local), parts.dtype),
        name="unpack",
    )(parts)


def select_kernel(pick_ref, kv_ref, out_ref):
    base = pl.program_id(0) * out_ref.shape[0]
    for i in range(out_ref.shape[0]):
        out_ref[i] = kv_ref[pick_ref[base + i]]


def select_blocks(picks, blocks, head):
    frames = picks.shape[0]
    step = 8
    count, rows, _ = blocks.shape
    width = 2 * HDIM
    return pl.pallas_call(
        select_kernel,
        grid_spec=pltpu.PrefetchScalarGridSpec(
            num_scalar_prefetch=1,
            grid=(frames // step,),
            in_specs=[pl.BlockSpec((count, rows, width), lambda i, p: (0, 0, head))],
            out_specs=pl.BlockSpec((step, rows, width), lambda i, p: (i, 0, 0)),
        ),
        out_shape=jax.ShapeDtypeStruct((frames, rows, width), blocks.dtype),
        name="select",
    )(picks, blocks)


def near_kernel(on_ref, q_ref, own_ref, before_ref, after_ref, o_ref, ml_ref):
    tile = q_ref.shape[0]
    sub = tile // BLOCK
    first = pl.program_id(0) * sub
    query = q_ref[...]
    parts = [dot(query, own_ref[:, :HDIM], NT)]
    for side, ref in enumerate((before_ref, after_ref)):
        scores = dot(query, ref[:, :HDIM], NT)
        rows = []
        for s in range(sub):
            cols = []
            for b in range(BF):
                bias = jnp.where(on_ref[first + s, side * BF + b] > 0, 0.0, NEG)
                cols.append(
                    scores[s * BLOCK : (s + 1) * BLOCK, b * BLOCK : (b + 1) * BLOCK] + bias
                )
            rows.append(jnp.concatenate(cols, axis=1))
        parts.append(jnp.concatenate(rows, axis=0))
    top = functools.reduce(jnp.maximum, [jnp.max(p, axis=1, keepdims=True) for p in parts])
    total = jnp.zeros((tile, 1), jnp.float32)
    summed = jnp.zeros((tile, HDIM), jnp.float32)
    for part, ref in zip(parts, (own_ref, before_ref, after_ref)):
        weights = jnp.exp2((part - top) * SCALE2)
        total = total + jnp.sum(weights, axis=1, keepdims=True)
        summed = summed + dot(weights.astype(jnp.bfloat16), ref[:, HDIM:], NN)
    o_ref[...] = summed
    half = ml_ref.shape[1] // 2
    ml_ref[:, :half] = jnp.broadcast_to(top, (tile, half))
    ml_ref[:, half:] = jnp.broadcast_to(total, (tile, half))


def near_attention(near_on, mixed, head, before, after):
    tile = 256
    rows, width = mixed.shape
    column = width // HDIM - HEADS_LOCAL + head
    whole = pl.BlockSpec((rows, 2 * HDIM), lambda i, on: (0, head))
    flops = 4 * rows * 3 * rows * HDIM
    return pl.pallas_call(
        near_kernel,
        grid_spec=pltpu.PrefetchScalarGridSpec(
            num_scalar_prefetch=1,
            grid=(rows // tile,),
            in_specs=[pl.BlockSpec((tile, HDIM), lambda i, on: (i, column)), whole, whole, whole],
            out_specs=[pl.BlockSpec((tile, HDIM), lambda i, on: (i, 0))] * 2,
        ),
        out_shape=[jax.ShapeDtypeStruct((rows, HDIM), jnp.float32)] * 2,
        cost_estimate=pl.CostEstimate(
            flops=flops, bytes_accessed=4 * rows * 2 * HDIM * 2, transcendentals=3 * rows * rows
        ),
        name="near",
    )(near_on, mixed, mixed, before, after)


def far_kernel(list_ref, count_ref, q_ref, kv_ref, o_ref, ml_ref, out_ref, m_s, l_s, acc_s):
    half = ml_ref.shape[1] // 2
    m_s[...] = ml_ref[:, :1]
    l_s[...] = ml_ref[:, half : half + 1]
    acc_s[...] = o_ref[...]
    blocks = q_ref.shape[0] // BLOCK
    most = count_ref[0]
    for qb in range(1, blocks):
        most = jnp.maximum(most, count_ref[qb])

    def step(t, carry):
        for qb in range(blocks):
            rows = slice(qb * BLOCK, (qb + 1) * BLOCK)
            query = q_ref[rows, :]
            frames = [list_ref[qb, t * GROUP + i] for i in range(GROUP)]
            scores = []
            for i in range(GROUP):
                bias = jnp.where(t * GROUP + i < count_ref[qb], 0.0, NEG)
                scores.append(dot(query, kv_ref[frames[i], :, :HDIM], NT) + bias)
            old = m_s[rows, :]
            peak = functools.reduce(jnp.maximum, scores)
            top = jnp.maximum(old, jnp.max(peak, axis=1, keepdims=True))
            fade = jnp.exp2((old - top) * SCALE2)
            acc = acc_s[rows, :] * fade
            mass = jnp.zeros((BLOCK, BLOCK), jnp.float32)
            for i in range(GROUP):
                weights = jnp.exp2((scores[i] - top) * SCALE2)
                mass = mass + weights
                acc = acc + dot(weights.astype(jnp.bfloat16), kv_ref[frames[i], :, HDIM:], NN)
            m_s[rows, :] = top
            l_s[rows, :] = l_s[rows, :] * fade + jnp.sum(mass, axis=1, keepdims=True)
            acc_s[rows, :] = acc
        return carry

    lax.fori_loop(0, (most + GROUP - 1) // GROUP, step, 0)
    out_ref[...] = (acc_s[...] / l_s[...]).astype(out_ref.dtype)


def far_attention(order, counts, mixed, head, far, near_o, near_ml):
    rows, width = mixed.shape
    column = width // HDIM - HEADS_LOCAL + head
    frames = far.shape[0]
    full = pl.BlockSpec((rows, HDIM), lambda i, a, b: (0, 0))
    return pl.pallas_call(
        far_kernel,
        grid_spec=pltpu.PrefetchScalarGridSpec(
            num_scalar_prefetch=2,
            grid=(1,),
            in_specs=[
                pl.BlockSpec((rows, HDIM), lambda i, a, b: (0, column)),
                pl.BlockSpec((frames, BLOCK, 2 * HDIM), lambda i, a, b: (0, 0, 0)),
                full,
                full,
            ],
            out_specs=full,
            scratch_shapes=[
                pltpu.VMEM((rows, 1), jnp.float32),
                pltpu.VMEM((rows, 1), jnp.float32),
                pltpu.VMEM((rows, HDIM), jnp.float32),
            ],
        ),
        out_shape=jax.ShapeDtypeStruct((rows, HDIM), mixed.dtype),
        cost_estimate=pl.CostEstimate(
            flops=rows * frames * BLOCK * HDIM,
            bytes_accessed=frames * BLOCK * 2 * HDIM * 2,
            transcendentals=rows * frames * BLOCK // 4,
        ),
        name="far",
    )(order, counts, mixed, far, near_o, near_ml)


def mask_tables(block_mask, frame_id, frame_count):
    block_ids = jnp.arange(BF, dtype=jnp.int32)
    frame_ids = jnp.arange(frame_count, dtype=jnp.int32)
    towards = lax.dynamic_slice_in_dim(block_mask, frame_id * BF, BF, 1)
    towards = jnp.max(towards.reshape(frame_count, BF, BF), axis=1)
    outgoing = jnp.minimum(jnp.sum(towards * block_ids[None, :], axis=1), BF - 1)
    own = lax.dynamic_slice_in_dim(block_mask, frame_id * BF, BF, 0)
    padded = jnp.pad(own, ((0, 0), (BF, BF)))
    beside = lax.dynamic_slice_in_dim(padded, frame_id * BF, 3 * BF, 1)
    near_on = jnp.concatenate([beside[:, :BF], beside[:, 2 * BF :]], axis=1)
    distant = (jnp.abs(frame_ids - frame_id) >= 2).astype(jnp.int32)
    active = jnp.max(own.reshape(BF, frame_count, BF), axis=2) * distant[None, :]
    upto = (frame_ids[:, None] <= frame_ids[None, :]).astype(jnp.int32)
    place = jnp.sum(active[:, :, None] * upto[None, :, :], axis=1)
    counts = jnp.sum(active, axis=1)
    slots = jnp.where(active > 0, place - 1, -1)
    hit = (slots[:, :, None] == frame_ids[None, None, :]).astype(jnp.int32)
    order = jnp.sum(hit * frame_ids[None, :, None], axis=1)
    return outgoing, near_on, order, counts


def body(queries, key_rows, value_rows, block_mask):
    frame_count = lax.axis_size("frame")
    peers = lax.axis_size("head")
    frame_id = lax.axis_index("frame")
    exchange = functools.partial(lax.all_to_all, split_axis=0, concat_axis=0, tiled=True)
    up = [(i, i + 1) for i in range(frame_count - 1)]
    down = [(j, i) for i, j in up]
    heads = range(HEADS_LOCAL)
    outgoing, near_on, order, counts = mask_tables(block_mask, frame_id, frame_count)
    packed = pack(queries, key_rows, value_rows, peers)
    blocks = exchange(packed, "head")
    mixed = blocks.reshape(FT, blocks.shape[2])
    far = []
    for head in heads:
        parcel = select_blocks(outgoing, blocks, head)
        far.append(exchange(parcel, "frame"))
    pairs = mixed[:, : 2 * HDIM * HEADS_LOCAL]
    before = lax.ppermute(pairs, "frame", up)
    after = lax.ppermute(pairs, "frame", down)
    outs = []
    for head in heads:
        near_o, near_ml = near_attention(near_on, mixed, head, before, after)
        outs.append(far_attention(order, counts, mixed, head, far[head], near_o, near_ml))
    result = jnp.concatenate(outs, axis=1).reshape(peers, BLOCK, HEADS_LOCAL * HDIM)
    return unpack(exchange(result, "head"))


def solution(mesh):
    placed = (
        P(("frame", "head"), None),
        P(("frame", "head"), None),
        P(("frame", "head"), None),
        P(),
    )
    return jax.shard_map(
        body, mesh=mesh, in_specs=placed, out_specs=P(("frame", "head"), None), check_vma=False
    )
```

time: 441 us -> 331 us (0.75)
  matrix products: 97.3 us -> 0 us
  Pallas kernels: 0 us -> 90 us
  other arithmetic: 77.9 us -> 4.23 us
  local copies, waits for them, and re-layouts: 55.5 us -> 4.29 us
  waiting for transfers between devices: 157 us -> 183 us
  loops' own time: 5.72 us -> 0 us
    all_to_all x4, waiting for transfers between devices: 16.1 us -> 128 us  [the longest x3 93.9 us: body(): far.append(exchange(parcel, 'frame'))]
    dot_general x8 -> x0, matrix products: 97.3 us -> none  [the longest x4 50.2 us: one_step(): jnp.einsum('htu,uhd->thd', weights.astype(jnp.bfloat16), all_values, pref...]
    pallas_call x0 -> x11, Pallas kernels: none -> 90 us  [the longest x3 41.5 us: far_attention(): pl.pallas_call(far_kernel, grid_spec=pltpu.PrefetchScalarGridSpec(num_sca...]
    ppermute x2, waiting for transfers between devices: 141 us -> 55.3 us  [the longest x1 51.9 us: body(): after = lax.ppermute(pairs, 'frame', down)]
    reduce_sum x7 -> x4, other arithmetic: 45 us -> 1.62 us  [the longest x1 0.71 us: mask_tables(): order = jnp.sum(hit * frame_ids[None, :, None], axis=1)]
    concatenate x6 -> x2, other arithmetic: 24.3 us -> 1.73 us  [the longest x1 1.06 us: body(): jnp.concatenate(outs, axis=1).reshape(peers, BLOCK, HEADS_LOCAL * HDIM)]
    while x5 -> x0, local copies, waits for them, and re-layouts: 11.8 us -> none  [the longest x1 8.29 us: body(): stacked = lax.map(one_step, jnp.arange(BF // step_blocks, dtype=jnp.int32))]
    slice x3 -> x2, local copies, waits for them, and re-layouts: 11.7 us -> 1.42 us  [the longest x1 1.35 us: body(): pairs = mixed[:, :2 * HDIM * HEADS_LOCAL]]
  transfers between devices with their start and end apart: 6 -> 6, of which waited for: 4 -> 5; matrix products, arithmetic and copies ran while one was open for 9% -> 1% of each run, Pallas kernels for 0% -> 19%
where the time goes in v1:
time: 331 us; the launch traced here: 330 us
  waiting for transfers between devices  183 us (55%)
  Pallas kernels  90 us (27%)
  starting transfers between devices  34.9 us (11%)
  blocking collectives  12.8 us (4%)
  local copies, waits for them, and re-layouts  4.29 us (1%)
  other arithmetic  4.23 us (1%)
    all_to_all x3, waiting for transfers between devices, body(): far.append(exchange(parcel, 'frame'))  93.9 us
    ppermute x1, waiting for transfers between devices, body(): after = lax.ppermute(pairs, 'frame', down)  51.9 us
    pallas_call x3, Pallas kernels, far_attention(): pl.pallas_call(far_kernel, grid_spec=pltpu.PrefetchScalarGridSpec(num_sca...  41.5 us
    all_to_all x1, waiting for transfers between devices, body(): blocks = exchange(packed, 'head')  34.2 us
    pallas_call x3, Pallas kernels, near_attention(): pl.pallas_call(near_kernel, grid_spec=pltpu.PrefetchScalarGridSpec(num_sc...  26.7 us
    all_to_all x3, starting transfers between devices, body(): far.append(exchange(parcel, 'frame'))  23 us
    all_to_all x1, blocking collectives, body(): return unpack(exchange(result, 'head'))  12.8 us
    pallas_call x3, Pallas kernels, select_blocks(): pl.pallas_call(select_kernel, grid_spec=pltpu.PrefetchScalarGridSpec(num_...  10.7 us
  transfers between devices with their start and end apart: 6, of which 5 were waited for; matrix products, arithmetic and copies ran while one was open for 1% of the time, Pallas kernels for 19%

profile of v1, /device:TPU:32, one launch (start us, length us, event | category | flops | bytes accessed | tf_op | source)
XLA Modules:
  0.0 329.6 jit_solution(1077136085259120495)
XLA Ops:
  0.0 0.0 copy-start
  0.0 6.1 %pack.1 = bf16[8,128,1152]{2,1,0:T(8,128)(2,1)} custom-call(bf16[128,3072]{1,0:T(8,128)(2,1)} %q_ref.1, bf16[128,3072]{1,0:T(8,128)(2,1)} %k_ref.1, bf16[128,3072]{1,0:T(8,128)(2,1)} %v_ref.1), custom_call_target="tpu_custom_call" | custom-call | tf_op jit(solution)/shard_map/pack/pallas_call | solution.py:41
  6.1 5.3 %all-to-all-start = ((bf16[8,128,1152]{2,1,0:T(8,128)(2,1)}), bf16[8,128,1152]{2,1,0:T(8,128)(2,1)S(1)}, u32[]{:S(2)}, u32[]{:S(2)}) async-start(bf16[8,128,1152]{2,1,0:T(8,128)(2,1)} %pack.1), calls=%async_computation | async-start | bytes 4718592 | tf_op jit(solution)/shard_map/all_to_all | solution.py:246
  11.4 0.0 copy-done
  11.4 0.1 bitcast_reduce_fusion
  11.5 0.1 multiply_reduce_fusion.1
  11.6 0.5 broadcast_minimum_fusion.pick_ref
  12.2 34.2 %all-to-all-done.kv_ref = bf16[8,128,1152]{2,1,0:T(8,128)(2,1)S(1)} async-done(((bf16[8,128,1152]{2,1,0:T(8,128)(2,1)}), bf16[8,128,1152]{2,1,0:T(8,128)(2,1)S(1)}, u32[]{:S(2)}, u32[]{:S(2)}) %all-to-all-start) | async-done | bytes 2359328 | tf_op jit(solution)/shard_map/all_to_all | solution.py:246
  46.3 0.0 copy-start.1
  46.3 1.4 copy-done.1
  47.7 3.6 %select.7 = bf16[32,128,256]{2,1,0:T(8,128)(2,1)} custom-call(s32[32]{0:T(128)} %broadcast_minimum_fusion.pick_ref, bf16[8,128,1152]{2,1,0:T(8,128)(2,1)} %copy-done.1), custom_call_target="tpu_custom_call" | custom-call | tf_op jit(solution)/shard_map/select/pallas_call | solution.py:78
  51.3 11.1 %all-to-all-start.3 = ((bf16[32,128,256]{2,1,0:T(8,128)(2,1)}), bf16[32,128,256]{2,1,0:T(8,128)(2,1)S(1)}, u32[]{:S(2)}, u32[]{:S(2)}) async-start(bf16[32,128,256]{2,1,0:T(8,128)(2,1)} %select.7), calls=%async_computation.3 | async-start | bytes 4194304 | tf_op jit(solution)/shard_map/all_to_all | solution.py:251
  62.4 3.6 %select.6 = bf16[32,128,256]{2,1,0:T(8,128)(2,1)} custom-call(s32[32]{0:T(128)} %broadcast_minimum_fusion.pick_ref, bf16[8,128,1152]{2,1,0:T(8,128)(2,1)} %copy-done.1), custom_call_target="tpu_custom_call" | custom-call | tf_op jit(solution)/shard_map/select/pallas_call | solution.py:78
  65.9 46.9 %all-to-all-done.3.kv_ref = bf16[32,128,256]{2,1,0:T(8,128)(2,1)S(1)} async-done(((bf16[32,128,256]{2,1,0:T(8,128)(2,1)}), bf16[32,128,256]{2,1,0:T(8,128)(2,1)S(1)}, u32[]{:S(2)}, u32[]{:S(2)}) %all-to-all-start.3) | async-done | bytes 2097184 | tf_op jit(solution)/shard_map/all_to_all | solution.py:251
  112.9 0.0 copy-start.5
  112.9 6.0 %all-to-all-start.2 = ((bf16[32,128,256]{2,1,0:T(8,128)(2,1)}), bf16[32,128,256]{2,1,0:T(8,128)(2,1)}, u32[]{:S(2)}, u32[]{:S(2)}) async-start(bf16[32,128,256]{2,1,0:T(8,128)(2,1)} %select.6), calls=%async_computation.2 | async-start | bytes 4194304 | tf_op jit(solution)/shard_map/all_to_all | solution.py:251
  118.9 0.0 copy-done.5
  118.9 3.6 %select.5 = bf16[32,128,256]{2,1,0:T(8,128)(2,1)} custom-call(s32[32]{0:T(128)} %broadcast_minimum_fusion.pick_ref, bf16[8,128,1152]{2,1,0:T(8,128)(2,1)} %copy-done.1), custom_call_target="tpu_custom_call" | custom-call | tf_op jit(solution)/shard_map/select/pallas_call | solution.py:78
  122.5 46.9 %all-to-all-done.2.kv_ref = bf16[32,128,256]{2,1,0:T(8,128)(2,1)} async-done(((bf16[32,128,256]{2,1,0:T(8,128)(2,1)}), bf16[32,128,256]{2,1,0:T(8,128)(2,1)}, u32[]{:S(2)}, u32[]{:S(2)}) %all-to-all-start.2) | async-done | bytes 2097184 | tf_op jit(solution)/shard_map/all_to_all | solution.py:251
  169.4 6.0 %all-to-all-start.1 = ((bf16[32,128,256]{2,1,0:T(8,128)(2,1)}), bf16[32,128,256]{2,1,0:T(8,128)(2,1)}, u32[]{:S(2)}, u32[]{:S(2)}) async-start(bf16[32,128,256]{2,1,0:T(8,128)(2,1)} %select.5), calls=%async_computation.1 | async-start | bytes 4194304 | tf_op jit(solution)/shard_map/all_to_all | solution.py:251
  175.4 0.0 copy-done.2
  175.4 1.3 slice.12
  176.8 4.6 %collective-permute-start.1 = (bf16[1024,768]{1,0:T(8,128)(2,1)}, bf16[1024,768]{1,0:T(8,128)(2,1)S(1)}, u32[]{:S(2)}, u32[]{:S(2)}) collective-permute-start(bf16[1024,768]{1,0:T(8,128)(2,1)} %slice.12), channel_id=1, source_target_pairs={{8,0},{16,8},{24,16},{32,24},{40,32},{48,40},{56,48},{64,56},{72,6... | collective-permute-start | bytes 4718600 | tf_op jit(solution)/shard_map/ppermute | solution.py:254
  181.4 1.9 collective-permute-start
  183.3 0.1 reshape.66
  183.4 0.2 reduce_max.18
  183.6 0.1 pad_dynamic-slice_fusion
  183.7 0.1 fusion.2
  183.8 0.7 pad_add_fusion.on_ref
  184.5 0.7 fusion.1
  185.2 0.1 multiply_reduce_fusion
  185.3 0.7 select_reduce_fusion.list_ref
  186.0 51.9 %collective-permute-done.1.after_ref = bf16[1024,768]{1,0:T(8,128)(2,1)S(1)} collective-permute-done((bf16[1024,768]{1,0:T(8,128)(2,1)}, bf16[1024,768]{1,0:T(8,128)(2,1)S(1)}, u32[]{:S(2)}, u32[]{:S(2)}) %collective-permute-start.1) | collective-permute-done | bytes 1572896 | tf_op jit(solution)/shard_map/ppermute | solution.py:254
  237.9 3.4 %collective-permute-done.before_ref = bf16[1024,768]{1,0:T(8,128)(2,1)S(1)} collective-permute-done((bf16[1024,768]{1,0:T(8,128)(2,1)}, bf16[1024,768]{1,0:T(8,128)(2,1)S(1)}, u32[]{:S(2)}, u32[]{:S(2)}) %collective-permute-start) | collective-permute-done | bytes 1572896 | tf_op jit(solution)/shard_map/ppermute | solution.py:253
  241.3 0.0 copy-done.3
  241.3 1.2 copy-done.4
  242.5 8.9 %near.5 = (f32[1024,128]{1,0:T(8,128)}, f32[1024,128]{1,0:T(8,128)}) custom-call(s32[8,16]{1,0:T(8,128)} %pad_add_fusion.on_ref, bf16[1024,1152]{1,0:T(8,128)(2,1)} %bitcast.4, bf16[1024,1152]{1,0:T(8,128)(2,1)} %bitcast.5, bf16[1024,768]{1,0:T(8,128)(2,1)} %copy-done.4, bf16[1024,768]{1,0:T(8,128)(2,1)} %copy-done.3), custom_call_target="tpu_custom_call" | custom-call | flops 1610612736 | bytes 2097152 | tf_op jit(solution)/shard_map/near/pallas_call | solution.py:128
  251.4 8.9 %near.4 = (f32[1024,128]{1,0:T(8,128)}, f32[1024,128]{1,0:T(8,128)}) custom-call(s32[8,16]{1,0:T(8,128)} %pad_add_fusion.on_ref, bf16[1024,1152]{1,0:T(8,128)(2,1)} %bitcast.6, bf16[1024,1152]{1,0:T(8,128)(2,1)} %bitcast.7, bf16[1024,768]{1,0:T(8,128)(2,1)} %copy-done.4, bf16[1024,768]{1,0:T(8,128)(2,1)} %copy-done.3), custom_call_target="tpu_custom_call" | custom-call | flops 1610612736 | bytes 2097152 | tf_op jit(solution)/shard_map/near/pallas_call | solution.py:128
  260.3 8.9 %near.3 = (f32[1024,128]{1,0:T(8,128)}, f32[1024,128]{1,0:T(8,128)}) custom-call(s32[8,16]{1,0:T(8,128)} %pad_add_fusion.on_ref, bf16[1024,1152]{1,0:T(8,128)(2,1)} %bitcast.8, bf16[1024,1152]{1,0:T(8,128)(2,1)} %bitcast.9, bf16[1024,768]{1,0:T(8,128)(2,1)} %copy-done.4, bf16[1024,768]{1,0:T(8,128)(2,1)} %copy-done.3), custom_call_target="tpu_custom_call" | custom-call | flops 1610612736 | bytes 2097152 | tf_op jit(solution)/shard_map/near/pallas_call | solution.py:128
  269.2 13.7 %far.5 = bf16[1024,128]{1,0:T(8,128)(2,1)} custom-call(s32[8,32]{1,0:T(8,128)} %select_reduce_fusion.list_ref, s32[8]{0:T(128)} %get-tuple-element.17.count_ref, bf16[1024,1152]{1,0:T(8,128)(2,1)} %bitcast.10, bf16[32,128,256]{2,1,0:T(8,128)(2,1)} %copy-done.5, f32[1024,128]{1,0:T(8,128)} %get-tuple-element.15.o_ref, f32[1024,128]{1,0:T(8,128)} %get-tuple-element.16.ml_ref), custom_call_target="tpu_custom_call" | custom-call | flops 536870912 | bytes 2097152 | tf_op jit(solution)/shard_map/far/pallas_call | solution.py:187
  282.9 13.9 %far.4 = bf16[1024,128]{1,0:T(8,128)(2,1)} custom-call(s32[8,32]{1,0:T(8,128)} %select_reduce_fusion.list_ref, s32[8]{0:T(128)} %get-tuple-element.17.count_ref, bf16[1024,1152]{1,0:T(8,128)(2,1)} %bitcast.11, bf16[32,128,256]{2,1,0:T(8,128)(2,1)} %all-to-all-done.2.kv_ref, f32[1024,128]{1,0:T(8,128)} %get-tuple-element.13.o_ref, ...), custom_call_target="tpu_custom_call" | custom-call | flops 536870912 | bytes 2097152 | tf_op jit(solution)/shard_map/far/pallas_call | solution.py:187
  296.8 0.0 all-to-all-done.1.kv_ref
  296.8 13.8 %far.3 = bf16[1024,128]{1,0:T(8,128)(2,1)} custom-call(s32[8,32]{1,0:T(8,128)} %select_reduce_fusion.list_ref, s32[8]{0:T(128)} %get-tuple-element.17.count_ref, bf16[1024,1152]{1,0:T(8,128)(2,1)} %bitcast.12, bf16[32,128,256]{2,1,0:T(8,128)(2,1)} %all-to-all-done.1.kv_ref, f32[1024,128]{1,0:T(8,128)} %get-tuple-element.11.o_ref, ...), custom_call_target="tpu_custom_call" | custom-call | flops 536870912 | bytes 2097152 | tf_op jit(solution)/shard_map/far/pallas_call | solution.py:187
  310.7 0.0 copy-done.6
  310.7 0.0 copy-done.7
  310.7 1.1 pad_maximum_fusion
  311.7 12.8 %all_to_all.25.part_ref = bf16[8,128,384]{2,1,0:T(8,128)(2,1)} all-to-all(bf16[8,128,384]{2,1,0:T(8,128)(2,1)S(1)} %bitcast.14), channel_id=1, replica_groups=mesh['frame'=32,'head'=8] {'head'}, dimensions={0} | all-to-all | bytes 1572864 | tf_op jit(solution)/shard_map/all_to_all | solution.py:260
  324.6 5.0 %unpack.1 = bf16[128,3072]{1,0:T(8,128)(2,1)} custom-call(bf16[8,128,384]{2,1,0:T(8,128)(2,1)} %all_to_all.25.part_ref), custom_call_target="tpu_custom_call" | custom-call | tf_op jit(solution)/shard_map/unpack/pallas_call | solution.py:57
  (9 shorter events, 0.0 us)
Async XLA Ops:
  0.0 11.4 %copy-start = (s32[256,256]{1,0:T(8,128)S(1)}, s32[256,256]{1,0:T(8,128)}, u32[]{:S(2)}) copy-start(s32[256,256]{1,0:T(8,128)} %param.7) | copy-start | bytes 786436
  6.1 40.2 %all-to-all-start = ((bf16[8,128,1152]{2,1,0:T(8,128)(2,1)}), bf16[8,128,1152]{2,1,0:T(8,128)(2,1)S(1)}, u32[]{:S(2)}, u32[]{:S(2)}) async-start(bf16[8,128,1152]{2,1,0:T(8,128)(2,1)} %pack.1), calls=%async_computation | async-start | bytes 4718592 | tf_op jit(solution)/shard_map/all_to_all | solution.py:246
  46.3 1.4 copy-start.1
  51.3 61.6 %all-to-all-start.3 = ((bf16[32,128,256]{2,1,0:T(8,128)(2,1)}), bf16[32,128,256]{2,1,0:T(8,128)(2,1)S(1)}, u32[]{:S(2)}, u32[]{:S(2)}) async-start(bf16[32,128,256]{2,1,0:T(8,128)(2,1)} %select.7), calls=%async_computation.3 | async-start | bytes 4194304 | tf_op jit(solution)/shard_map/all_to_all | solution.py:251
  112.9 6.0 %copy-start.5 = (bf16[32,128,256]{2,1,0:T(8,128)(2,1)}, bf16[32,128,256]{2,1,0:T(8,128)(2,1)S(1)}, u32[]{:S(2)}) copy-start(bf16[32,128,256]{2,1,0:T(8,128)(2,1)S(1)} %all-to-all-done.3.kv_ref) | copy-start | bytes 6291460
  112.9 56.5 %all-to-all-start.2 = ((bf16[32,128,256]{2,1,0:T(8,128)(2,1)}), bf16[32,128,256]{2,1,0:T(8,128)(2,1)}, u32[]{:S(2)}, u32[]{:S(2)}) async-start(bf16[32,128,256]{2,1,0:T(8,128)(2,1)} %select.6), calls=%async_computation.2 | async-start | bytes 4194304 | tf_op jit(solution)/shard_map/all_to_all | solution.py:251
  122.5 52.9 %copy-start.2 = (bf16[8,128,1152]{2,1,0:T(8,128)(2,1)S(1)}, bf16[8,128,1152]{2,1,0:T(8,128)(2,1)}, u32[]{:S(2)}) copy-start(bf16[8,128,1152]{2,1,0:T(8,128)(2,1)} %copy-done.1) | copy-start | bytes 7077892
  169.4 127.4 %all-to-all-start.1 = ((bf16[32,128,256]{2,1,0:T(8,128)(2,1)}), bf16[32,128,256]{2,1,0:T(8,128)(2,1)}, u32[]{:S(2)}, u32[]{:S(2)}) async-start(bf16[32,128,256]{2,1,0:T(8,128)(2,1)} %select.5), calls=%async_computation.1 | async-start | bytes 4194304 | tf_op jit(solution)/shard_map/all_to_all | solution.py:251
  176.8 61.1 %collective-permute-start.1 = (bf16[1024,768]{1,0:T(8,128)(2,1)}, bf16[1024,768]{1,0:T(8,128)(2,1)S(1)}, u32[]{:S(2)}, u32[]{:S(2)}) collective-permute-start(bf16[1024,768]{1,0:T(8,128)(2,1)} %slice.12), channel_id=1, source_target_pairs={{8,0},{16,8},{24,16},{32,24},{40,32},{48,40},{56,48},{64,56},{72,6... | collective-permute-start | bytes 4718600 | tf_op jit(solution)/shard_map/ppermute | solution.py:254
  181.4 59.9 %collective-permute-start = (bf16[1024,768]{1,0:T(8,128)(2,1)}, bf16[1024,768]{1,0:T(8,128)(2,1)S(1)}, u32[]{:S(2)}, u32[]{:S(2)}) collective-permute-start(bf16[1024,768]{1,0:T(8,128)(2,1)} %slice.12), channel_id=1, source_target_pairs={{0,8},{8,16},{16,24},{24,32},{32,40},{40,48},{48,56},{56,64},{64,7... | collective-permute-start | bytes 4718600 | tf_op jit(solution)/shard_map/ppermute | solution.py:253
  237.9 3.4 %copy-start.3 = (bf16[1024,768]{1,0:T(8,128)(2,1)}, bf16[1024,768]{1,0:T(8,128)(2,1)S(1)}, u32[]{:S(2)}) copy-start(bf16[1024,768]{1,0:T(8,128)(2,1)S(1)} %collective-permute-done.1.after_ref) | copy-start | bytes 4718596
  241.3 1.2 copy-start.4
  296.8 13.8 %copy-start.6 = (bf16[1024,128]{1,0:T(8,128)(2,1)S(1)}, bf16[1024,128]{1,0:T(8,128)(2,1)}, u32[]{:S(2)}) copy-start(bf16[1024,128]{1,0:T(8,128)(2,1)} %far.5) | copy-start | bytes 786436
  296.8 13.8 %copy-start.7 = (bf16[1024,128]{1,0:T(8,128)(2,1)S(1)}, bf16[1024,128]{1,0:T(8,128)(2,1)}, u32[]{:S(2)}) copy-start(bf16[1024,128]{1,0:T(8,128)(2,1)} %far.4) | copy-start | bytes 786436

commit v2 on v1

--- a/solution.py
+++ b/solution.py
@@ -13,53 +13,68 @@
 BF = 8
 FT = BF * BLOCK
 HEADS_LOCAL = 3
-GROUP = 4
+GROUP = 2
+PACK_STEPS = 4
+SELECT_STEPS = 2
+PARAMS = pltpu.CompilerParams(vmem_limit_bytes=24 << 20)
 NEG = -1e30
 SCALE2 = math.log2(math.e) / math.sqrt(HDIM)
 NT = (((1,), (1,)), ((), ()))
 NN = (((1,), (0,)), ((), ()))
 
 
+def in_hbm(*arrays):
+    return [pltpu.with_memory_space_constraint(a, pltpu.HBM) for a in arrays]
+
+
 def dot(a, b, dims):
     return lax.dot_general(a, b, dims, preferred_element_type=jnp.float32)
 
 
 def pack_kernel(q_ref, k_ref, v_ref, out_ref):
-    heads = q_ref.shape[1] // HDIM
-    for h in range(heads):
-        cols = slice(h * HDIM, (h + 1) * HDIM)
-        base = 2 * h * HDIM
-        out_ref[0, :, base : base + HDIM] = k_ref[:, cols]
-        out_ref[0, :, base + HDIM : base + 2 * HDIM] = v_ref[:, cols]
-    out_ref[0, :, 2 * heads * HDIM :] = q_ref[...]
+    peers = out_ref.shape[0]
+    local = q_ref.shape[1] // peers
+    for j in range(peers):
+        for h in range(local // HDIM):
+            cols = slice(j * local + h * HDIM, j * local + (h + 1) * HDIM)
+            base = 2 * h * HDIM
+            out_ref[j, :, base : base + HDIM] = k_ref[:, cols]
+            out_ref[j, :, base + HDIM : base + 2 * HDIM] = v_ref[:, cols]
+        out_ref[j, :, 2 * local :] = q_ref[:, j * local : (j + 1) * local]
 
 
 def pack(queries, keys, values, peers):
     rows, width = queries.shape
     local = width // peers
-    spec = pl.BlockSpec((rows, local), lambda j: (0, j))
+    tile = rows // PACK_STEPS
+    spec = pl.BlockSpec((tile, width), lambda i: (i, 0))
     return pl.pallas_call(
         pack_kernel,
-        grid=(peers,),
+        grid=(PACK_STEPS,),
         in_specs=[spec] * 3,
-        out_specs=pl.BlockSpec((1, rows, 3 * local), lambda j: (j, 0, 0)),
-        out_shape=jax.ShapeDtypeStruct((peers, rows, 3 * local), queries.dtype),
+        out_specs=pl.BlockSpec((peers, tile, 3 * local), lambda i: (0, i, 0)),
+        out_shape=pltpu.HBM((peers, rows, 3 * local), queries.dtype),
+        compiler_params=PARAMS,
         name="pack",
-    )(queries, keys, values)
+    )(*in_hbm(queries, keys, values))
 
 
 def unpack_kernel(part_ref, out_ref):
-    out_ref[...] = part_ref[0]
+    peers, _, local = part_ref.shape
+    for j in range(peers):
+        out_ref[:, j * local : (j + 1) * local] = part_ref[j]
 
 
 def unpack(parts):
     peers, rows, local = parts.shape
+    tile = rows // PACK_STEPS
     return pl.pallas_call(
         unpack_kernel,
-        grid=(peers,),
-        in_specs=[pl.BlockSpec((1, rows, local), lambda j: (j, 0, 0))],
-        out_specs=pl.BlockSpec((rows, local), lambda j: (0, j)),
+        grid=(PACK_STEPS,),
+        in_specs=[pl.BlockSpec((peers, tile, local), lambda i: (0, i, 0))],
+        out_specs=pl.BlockSpec((tile, peers * local), lambda i: (i, 0)),
         out_shape=jax.ShapeDtypeStruct((rows, peers * local), parts.dtype),
+        compiler_params=PARAMS,
         name="unpack",
     )(parts)
 
@@ -72,7 +87,7 @@
 
 def select_blocks(picks, blocks, head):
     frames = picks.shape[0]
-    step = 8
+    step = frames // SELECT_STEPS
     count, rows, _ = blocks.shape
     width = 2 * HDIM
     return pl.pallas_call(
@@ -83,12 +98,13 @@
             in_specs=[pl.BlockSpec((count, rows, width), lambda i, p: (0, 0, head))],
             out_specs=pl.BlockSpec((step, rows, width), lambda i, p: (i, 0, 0)),
         ),
-        out_shape=jax.ShapeDtypeStruct((frames, rows, width), blocks.dtype),
+        out_shape=pltpu.HBM((frames, rows, width), blocks.dtype),
+        compiler_params=PARAMS,
         name="select",
     )(picks, blocks)
 
 
-def near_kernel(on_ref, q_ref, own_ref, before_ref, after_ref, o_ref, ml_ref):
+def near_kernel(on_ref, q_ref, own_ref, before_ref, after_ref, o_ref, m_ref, l_ref):
     tile = q_ref.shape[0]
     sub = tile // BLOCK
     first = pl.program_id(0) * sub
@@ -107,16 +123,16 @@
             rows.append(jnp.concatenate(cols, axis=1))
         parts.append(jnp.concatenate(rows, axis=0))
     top = functools.reduce(jnp.maximum, [jnp.max(p, axis=1, keepdims=True) for p in parts])
-    total = jnp.zeros((tile, 1), jnp.float32)
+    mass = jnp.zeros((tile, HDIM), jnp.float32)
     summed = jnp.zeros((tile, HDIM), jnp.float32)
     for part, ref in zip(parts, (own_ref, before_ref, after_ref)):
         weights = jnp.exp2((part - top) * SCALE2)
-        total = total + jnp.sum(weights, axis=1, keepdims=True)
+        for b in range(BF):
+            mass = mass + weights[:, b * BLOCK : (b + 1) * BLOCK]
         summed = summed + dot(weights.astype(jnp.bfloat16), ref[:, HDIM:], NN)
     o_ref[...] = summed
-    half = ml_ref.shape[1] // 2
-    ml_ref[:, :half] = jnp.broadcast_to(top, (tile, half))
-    ml_ref[:, half:] = jnp.broadcast_to(total, (tile, half))
+    m_ref[...] = jnp.broadcast_to(top, (tile, HDIM))
+    l_ref[...] = mass
 
 
 def near_attention(near_on, mixed, head, before, after):
@@ -131,20 +147,20 @@
             num_scalar_prefetch=1,
             grid=(rows // tile,),
             in_specs=[pl.BlockSpec((tile, HDIM), lambda i, on: (i, column)), whole, whole, whole],
-            out_specs=[pl.BlockSpec((tile, HDIM), lambda i, on: (i, 0))] * 2,
-        ),
-        out_shape=[jax.ShapeDtypeStruct((rows, HDIM), jnp.float32)] * 2,
+            out_specs=[pl.BlockSpec((tile, HDIM), lambda i, on: (i, 0))] * 3,
+        ),
+        out_shape=[pltpu.HBM((rows, HDIM), jnp.float32)] * 3,
         cost_estimate=pl.CostEstimate(
             flops=flops, bytes_accessed=4 * rows * 2 * HDIM * 2, transcendentals=3 * rows * rows
         ),
+        compiler_params=PARAMS,
         name="near",
     )(near_on, mixed, mixed, before, after)
 
 
-def far_kernel(list_ref, count_ref, q_ref, kv_ref, o_ref, ml_ref, out_ref, m_s, l_s, acc_s):
-    half = ml_ref.shape[1] // 2
-    m_s[...] = ml_ref[:, :1]
-    l_s[...] = ml_ref[:, half : half + 1]
+def far_kernel(list_ref, count_ref, q_ref, kv_ref, o_ref, m_ref, l_ref, out_ref, m_s, l_s, acc_s):
+    m_s[...] = m_ref[...]
+    l_s[...] = l_ref[...]
     acc_s[...] = o_ref[...]
     blocks = q_ref.shape[0] // BLOCK
     most = count_ref[0]
@@ -156,30 +172,30 @@
             rows = slice(qb * BLOCK, (qb + 1) * BLOCK)
             query = q_ref[rows, :]
             frames = [list_ref[qb, t * GROUP + i] for i in range(GROUP)]
+            keys = jnp.concatenate([kv_ref[f, :, :HDIM] for f in frames], axis=0)
+            values = jnp.concatenate([kv_ref[f, :, HDIM:] for f in frames], axis=0)
+            raw = dot(query, keys, NT)
             scores = []
             for i in range(GROUP):
                 bias = jnp.where(t * GROUP + i < count_ref[qb], 0.0, NEG)
-                scores.append(dot(query, kv_ref[frames[i], :, :HDIM], NT) + bias)
+                scores.append(raw[:, i * BLOCK : (i + 1) * BLOCK] + bias)
             old = m_s[rows, :]
             peak = functools.reduce(jnp.maximum, scores)
             top = jnp.maximum(old, jnp.max(peak, axis=1, keepdims=True))
             fade = jnp.exp2((old - top) * SCALE2)
-            acc = acc_s[rows, :] * fade
-            mass = jnp.zeros((BLOCK, BLOCK), jnp.float32)
-            for i in range(GROUP):
-                weights = jnp.exp2((scores[i] - top) * SCALE2)
-                mass = mass + weights
-                acc = acc + dot(weights.astype(jnp.bfloat16), kv_ref[frames[i], :, HDIM:], NN)
+            weights = [jnp.exp2((s - top) * SCALE2) for s in scores]
+            rounded = jnp.concatenate([w.astype(jnp.bfloat16) for w in weights], axis=1)
             m_s[rows, :] = top
-            l_s[rows, :] = l_s[rows, :] * fade + jnp.sum(mass, axis=1, keepdims=True)
-            acc_s[rows, :] = acc
+            l_s[rows, :] = l_s[rows, :] * fade + functools.reduce(jnp.add, weights)
+            acc_s[rows, :] = acc_s[rows, :] * fade + dot(rounded, values, NN)
         return carry
 
     lax.fori_loop(0, (most + GROUP - 1) // GROUP, step, 0)
-    out_ref[...] = (acc_s[...] / l_s[...]).astype(out_ref.dtype)
-
-
-def far_attention(order, counts, mixed, head, far, near_o, near_ml):
+    total = jnp.sum(l_s[...], axis=1, keepdims=True)
+    out_ref[...] = (acc_s[...] / total).astype(out_ref.dtype)
+
+
+def far_attention(order, counts, mixed, head, far, near):
     rows, width = mixed.shape
     column = width // HDIM - HEADS_LOCAL + head
     frames = far.shape[0]
@@ -194,11 +210,12 @@
                 pl.BlockSpec((frames, BLOCK, 2 * HDIM), lambda i, a, b: (0, 0, 0)),
                 full,
                 full,
+                full,
             ],
             out_specs=full,
             scratch_shapes=[
-                pltpu.VMEM((rows, 1), jnp.float32),
-                pltpu.VMEM((rows, 1), jnp.float32),
+                pltpu.VMEM((rows, HDIM), jnp.float32),
+                pltpu.VMEM((rows, HDIM), jnp.float32),
                 pltpu.VMEM((rows, HDIM), jnp.float32),
             ],
         ),
@@ -208,8 +225,9 @@
             bytes_accessed=frames * BLOCK * 2 * HDIM * 2,
             transcendentals=rows * frames * BLOCK // 4,
         ),
+        compiler_params=PARAMS,
         name="far",
-    )(order, counts, mixed, far, near_o, near_ml)
+    )(order, counts, mixed, far, *in_hbm(*near))
 
 
 def mask_tables(block_mask, frame_id, frame_count):
@@ -254,8 +272,8 @@
     after = lax.ppermute(pairs, "frame", down)
     outs = []
     for head in heads:
-        near_o, near_ml = near_attention(near_on, mixed, head, before, after)
-        outs.append(far_attention(order, counts, mixed, head, far[head], near_o, near_ml))
+        near = near_attention(near_on, mixed, head, before, after)
+        outs.append(far_attention(order, counts, mixed, head, far[head], near))
     result = jnp.concatenate(outs, axis=1).reshape(peers, BLOCK, HEADS_LOCAL * HDIM)
     return unpack(exchange(result, "head"))
 

time: 331 us -> 299 us (0.903)
  Pallas kernels: 90 us -> 57.1 us
  waiting for transfers between devices: 183 us -> 188 us
    ppermute x1, waiting for transfers between devices: 3.4 us -> 55.7 us  [body(): before = lax.ppermute(pairs, 'frame', up)]
    ppermute x1, waiting for transfers between devices: 51.9 us -> 0.01 us  [body(): after = lax.ppermute(pairs, 'frame', down)]
    pallas_call x3, Pallas kernels: 41.5 us -> 21.8 us  [far_attention(): pl.pallas_call(far_kernel, grid_spec=pltpu.PrefetchScalarGridSpec(num_sca...]
    pallas_call x2, Pallas kernels: 11.1 us -> 5.62 us  [the longest x1 4.08 us: pack(): pl.pallas_call(pack_kernel, grid=(PACK_STEPS,), in_specs=[spec] * 3, out_...]
    pallas_call x3, Pallas kernels: 10.7 us -> 6.02 us  [select_blocks(): pl.pallas_call(select_kernel, grid_spec=pltpu.PrefetchScalarGridSpec(num_...]
  transfers between devices with their start and end apart: 6 -> 6, of which waited for: 5 -> 4; matrix products, arithmetic and copies ran while one was open for 1% -> 1% of each run, Pallas kernels for 19% -> 14%
where the time goes in v2:
time: 299 us; the launch traced here: 296 us
  waiting for transfers between devices  188 us (63%)
  Pallas kernels  57.1 us (19%)
  starting transfers between devices  36.4 us (12%)
  blocking collectives  12.2 us (4%)
    all_to_all x3, waiting for transfers between devices, body(): far.append(exchange(parcel, 'frame'))  97.1 us
    ppermute x1, waiting for transfers between devices, body(): before = lax.ppermute(pairs, 'frame', up)  55.7 us
    all_to_all x1, waiting for transfers between devices, body(): blocks = exchange(packed, 'head')  34.7 us
    pallas_call x3, Pallas kernels, near_attention(): pl.pallas_call(near_kernel, grid_spec=pltpu.PrefetchScalarGridSpec(num_sc...  23.7 us
    all_to_all x3, starting transfers between devices, body(): far.append(exchange(parcel, 'frame'))  23.1 us
    pallas_call x3, Pallas kernels, far_attention(): pl.pallas_call(far_kernel, grid_spec=pltpu.PrefetchScalarGridSpec(num_sca...  21.8 us
    all_to_all x1, blocking collectives, body(): return unpack(exchange(result, 'head'))  12.2 us
    pallas_call x3, Pallas kernels, select_blocks(): pl.pallas_call(select_kernel, grid_spec=pltpu.PrefetchScalarGridSpec(num_...  6.02 us
  transfers between devices with their start and end apart: 6, of which 4 were waited for; matrix products, arithmetic and copies ran while one was open for 1% of the time, Pallas kernels for 14%

profile of v2, /device:TPU:32, one launch (start us, length us, event | category | flops | bytes accessed | tf_op | source)
XLA Modules:
  0.0 295.9 jit_solution(10093149610677411807)
XLA Ops:
  0.0 0.0 copy-start
  0.0 4.1 %pack.1 = bf16[8,128,1152]{2,1,0:T(8,128)(2,1)} custom-call(bf16[128,3072]{1,0:T(8,128)(2,1)} %q_ref.1, bf16[128,3072]{1,0:T(8,128)(2,1)} %k_ref.1, bf16[128,3072]{1,0:T(8,128)(2,1)} %v_ref.1), custom_call_target="tpu_custom_call" | custom-call | tf_op jit(solution)/shard_map/pack/pallas_call | solution.py:51
  4.1 5.3 %all-to-all-start = ((bf16[8,128,1152]{2,1,0:T(8,128)(2,1)}), bf16[8,128,1152]{2,1,0:T(8,128)(2,1)S(1)}, u32[]{:S(2)}, u32[]{:S(2)}) async-start(bf16[8,128,1152]{2,1,0:T(8,128)(2,1)} %pack.1), calls=%async_computation | async-start | bytes 4718592 | tf_op jit(solution)/shard_map/all_to_all | solution.py:264
  9.4 0.0 copy-done
  9.4 0.1 bitcast_reduce_fusion
  9.5 0.1 multiply_reduce_fusion.1
  9.7 34.7 %all-to-all-done.kv_ref = bf16[8,128,1152]{2,1,0:T(8,128)(2,1)S(1)} async-done(((bf16[8,128,1152]{2,1,0:T(8,128)(2,1)}), bf16[8,128,1152]{2,1,0:T(8,128)(2,1)S(1)}, u32[]{:S(2)}, u32[]{:S(2)}) %all-to-all-start) | async-done | bytes 2359328 | tf_op jit(solution)/shard_map/all_to_all | solution.py:264
  44.3 2.0 select.7
  46.4 11.1 %all-to-all-start.3 = ((bf16[32,128,256]{2,1,0:T(8,128)(2,1)}), bf16[32,128,256]{2,1,0:T(8,128)(2,1)}, u32[]{:S(2)}, u32[]{:S(2)}) async-start(bf16[32,128,256]{2,1,0:T(8,128)(2,1)} %select.7), calls=%async_computation.3 | async-start | bytes 4194304 | tf_op jit(solution)/shard_map/all_to_all | solution.py:269
  57.5 2.0 select.6
  59.5 48.6 %all-to-all-done.3.kv_ref = bf16[32,128,256]{2,1,0:T(8,128)(2,1)} async-done(((bf16[32,128,256]{2,1,0:T(8,128)(2,1)}), bf16[32,128,256]{2,1,0:T(8,128)(2,1)}, u32[]{:S(2)}, u32[]{:S(2)}) %all-to-all-start.3) | async-done | bytes 2097184 | tf_op jit(solution)/shard_map/all_to_all | solution.py:269
  108.0 6.0 %all-to-all-start.2 = ((bf16[32,128,256]{2,1,0:T(8,128)(2,1)}), bf16[32,128,256]{2,1,0:T(8,128)(2,1)}, u32[]{:S(2)}, u32[]{:S(2)}) async-start(bf16[32,128,256]{2,1,0:T(8,128)(2,1)} %select.6), calls=%async_computation.2 | async-start | bytes 4194304 | tf_op jit(solution)/shard_map/all_to_all | solution.py:269
  114.0 2.0 select.5
  116.1 48.5 %all-to-all-done.2.kv_ref = bf16[32,128,256]{2,1,0:T(8,128)(2,1)} async-done(((bf16[32,128,256]{2,1,0:T(8,128)(2,1)}), bf16[32,128,256]{2,1,0:T(8,128)(2,1)}, u32[]{:S(2)}, u32[]{:S(2)}) %all-to-all-start.2) | async-done | bytes 2097184 | tf_op jit(solution)/shard_map/all_to_all | solution.py:269
  164.6 6.0 %all-to-all-start.1 = ((bf16[32,128,256]{2,1,0:T(8,128)(2,1)}), bf16[32,128,256]{2,1,0:T(8,128)(2,1)}, u32[]{:S(2)}, u32[]{:S(2)}) async-start(bf16[32,128,256]{2,1,0:T(8,128)(2,1)} %select.5), calls=%async_computation.1 | async-start | bytes 4194304 | tf_op jit(solution)/shard_map/all_to_all | solution.py:269
  170.6 1.3 slice.12
  171.9 2.0 collective-permute-start
  173.9 5.9 %collective-permute-start.1 = (bf16[1024,768]{1,0:T(8,128)(2,1)}, bf16[1024,768]{1,0:T(8,128)(2,1)}, u32[]{:S(2)}, u32[]{:S(2)}) collective-permute-start(bf16[1024,768]{1,0:T(8,128)(2,1)} %slice.12), channel_id=1, source_target_pairs={{8,0},{16,8},{24,16},{32,24},{40,32},{48,40},{56,48},{64,56},{72,6... | collective-permute-start | bytes 4718600 | tf_op jit(solution)/shard_map/ppermute | solution.py:272
  179.8 0.1 reshape.66
  179.9 0.2 reduce_max.18
  180.2 0.1 pad_dynamic-slice_fusion
  180.3 0.1 fusion.2
  180.3 0.1 pad_add_fusion.on_ref
  180.4 0.1 fusion.1
  180.5 0.1 multiply_reduce_fusion
  180.7 0.1 select_reduce_fusion.list_ref
  180.8 55.7 %collective-permute-done.before_ref = bf16[1024,768]{1,0:T(8,128)(2,1)} collective-permute-done((bf16[1024,768]{1,0:T(8,128)(2,1)}, bf16[1024,768]{1,0:T(8,128)(2,1)}, u32[]{:S(2)}, u32[]{:S(2)}) %collective-permute-start) | collective-permute-done | bytes 1572896 | tf_op jit(solution)/shard_map/ppermute | solution.py:271
  236.5 0.0 collective-permute-done.1.after_ref
  236.5 7.9 %near.5 = (f32[1024,128]{1,0:T(8,128)}, f32[1024,128]{1,0:T(8,128)}, f32[1024,128]{1,0:T(8,128)}) custom-call(s32[8,16]{1,0:T(8,128)S(1)} %pad_add_fusion.on_ref, bf16[1024,1152]{1,0:T(8,128)(2,1)S(1)} %bitcast.5, bf16[1024,1152]{1,0:T(8,128)(2,1)S(1)} %bitcast.6, bf16[1024,768]{1,0:T(8,128)(2,1)} %collective-permute-done.before_ref, ...), custom_call_target="tpu_custom_call" | custom-call | flops 1610612736 | bytes 2097152 | tf_op jit(solution)/shard_map/near/pallas_call | solution.py:144
  244.4 7.9 %near.4 = (f32[1024,128]{1,0:T(8,128)}, f32[1024,128]{1,0:T(8,128)}, f32[1024,128]{1,0:T(8,128)}) custom-call(s32[8,16]{1,0:T(8,128)S(1)} %pad_add_fusion.on_ref, bf16[1024,1152]{1,0:T(8,128)(2,1)S(1)} %bitcast.7, bf16[1024,1152]{1,0:T(8,128)(2,1)S(1)} %bitcast.8, bf16[1024,768]{1,0:T(8,128)(2,1)} %collective-permute-done.before_ref, ...), custom_call_target="tpu_custom_call" | custom-call | flops 1610612736 | bytes 2097152 | tf_op jit(solution)/shard_map/near/pallas_call | solution.py:144
  252.4 7.9 %near.3 = (f32[1024,128]{1,0:T(8,128)}, f32[1024,128]{1,0:T(8,128)}, f32[1024,128]{1,0:T(8,128)}) custom-call(s32[8,16]{1,0:T(8,128)S(1)} %pad_add_fusion.on_ref, bf16[1024,1152]{1,0:T(8,128)(2,1)S(1)} %bitcast.9, bf16[1024,1152]{1,0:T(8,128)(2,1)S(1)} %bitcast.10, bf16[1024,768]{1,0:T(8,128)(2,1)} %collective-permute-done.before_ref, ...), custom_call_target="tpu_custom_call" | custom-call | flops 1610612736 | bytes 2097152 | tf_op jit(solution)/shard_map/near/pallas_call | solution.py:144
  260.2 7.3 %far.5 = bf16[1024,128]{1,0:T(8,128)(2,1)S(1)} custom-call(s32[8,32]{1,0:T(8,128)S(1)} %select_reduce_fusion.list_ref, s32[8]{0:T(128)S(1)} %get-tuple-element.23.count_ref, bf16[1024,1152]{1,0:T(8,128)(2,1)S(1)} %bitcast.11, bf16[32,128,256]{2,1,0:T(8,128)(2,1)} %all-to-all-done.3.kv_ref, f32[1024,128]{1,0:T(8,128)} %get-tuple-element.20.o_ref, ...), custom_call_target="tpu_custom_call" | custom-call | flops 536870912 | bytes 2097152 | tf_op jit(solution)/shard_map/far/pallas_call | solution.py:203
  267.5 7.3 %far.4 = bf16[1024,128]{1,0:T(8,128)(2,1)S(1)} custom-call(s32[8,32]{1,0:T(8,128)S(1)} %select_reduce_fusion.list_ref, s32[8]{0:T(128)S(1)} %get-tuple-element.23.count_ref, bf16[1024,1152]{1,0:T(8,128)(2,1)S(1)} %bitcast.12, bf16[32,128,256]{2,1,0:T(8,128)(2,1)} %all-to-all-done.2.kv_ref, f32[1024,128]{1,0:T(8,128)} %get-tuple-element.17.o_ref, ...), custom_call_target="tpu_custom_call" | custom-call | flops 536870912 | bytes 2097152 | tf_op jit(solution)/shard_map/far/pallas_call | solution.py:203
  274.8 0.0 all-to-all-done.1.kv_ref
  274.8 7.3 %far.3 = bf16[1024,128]{1,0:T(8,128)(2,1)S(1)} custom-call(s32[8,32]{1,0:T(8,128)S(1)} %select_reduce_fusion.list_ref, s32[8]{0:T(128)S(1)} %get-tuple-element.23.count_ref, bf16[1024,1152]{1,0:T(8,128)(2,1)S(1)} %bitcast.13, bf16[32,128,256]{2,1,0:T(8,128)(2,1)} %all-to-all-done.1.kv_ref, f32[1024,128]{1,0:T(8,128)} %get-tuple-element.14.o_ref, ...), custom_call_target="tpu_custom_call" | custom-call | flops 536870912 | bytes 2097152 | tf_op jit(solution)/shard_map/far/pallas_call | solution.py:203
  282.1 0.1 pad_maximum_fusion
  282.2 12.2 %all_to_all.25.part_ref = bf16[8,128,384]{2,1,0:T(8,128)(2,1)S(1)} all-to-all(bf16[8,128,384]{2,1,0:T(8,128)(2,1)S(1)} %bitcast.14), channel_id=1, replica_groups=mesh['frame'=32,'head'=8] {'head'}, dimensions={0} | all-to-all | bytes 1572864 | tf_op jit(solution)/shard_map/all_to_all | solution.py:278
  294.3 1.5 unpack.1
  (5 shorter events, 0.0 us)
Async XLA Ops:
  0.0 9.4 %copy-start = (s32[256,256]{1,0:T(8,128)S(1)}, s32[256,256]{1,0:T(8,128)}, u32[]{:S(2)}) copy-start(s32[256,256]{1,0:T(8,128)} %param.7) | copy-start | bytes 786436
  4.1 40.2 %all-to-all-start = ((bf16[8,128,1152]{2,1,0:T(8,128)(2,1)}), bf16[8,128,1152]{2,1,0:T(8,128)(2,1)S(1)}, u32[]{:S(2)}, u32[]{:S(2)}) async-start(bf16[8,128,1152]{2,1,0:T(8,128)(2,1)} %pack.1), calls=%async_computation | async-start | bytes 4718592 | tf_op jit(solution)/shard_map/all_to_all | solution.py:264
  46.4 61.7 %all-to-all-start.3 = ((bf16[32,128,256]{2,1,0:T(8,128)(2,1)}), bf16[32,128,256]{2,1,0:T(8,128)(2,1)}, u32[]{:S(2)}, u32[]{:S(2)}) async-start(bf16[32,128,256]{2,1,0:T(8,128)(2,1)} %select.7), calls=%async_computation.3 | async-start | bytes 4194304 | tf_op jit(solution)/shard_map/all_to_all | solution.py:269
  108.0 56.5 %all-to-all-start.2 = ((bf16[32,128,256]{2,1,0:T(8,128)(2,1)}), bf16[32,128,256]{2,1,0:T(8,128)(2,1)}, u32[]{:S(2)}, u32[]{:S(2)}) async-start(bf16[32,128,256]{2,1,0:T(8,128)(2,1)} %select.6), calls=%async_computation.2 | async-start | bytes 4194304 | tf_op jit(solution)/shard_map/all_to_all | solution.py:269
  164.6 110.2 %all-to-all-start.1 = ((bf16[32,128,256]{2,1,0:T(8,128)(2,1)}), bf16[32,128,256]{2,1,0:T(8,128)(2,1)}, u32[]{:S(2)}, u32[]{:S(2)}) async-start(bf16[32,128,256]{2,1,0:T(8,128)(2,1)} %select.5), calls=%async_computation.1 | async-start | bytes 4194304 | tf_op jit(solution)/shard_map/all_to_all | solution.py:269
  171.9 64.7 %collective-permute-start = (bf16[1024,768]{1,0:T(8,128)(2,1)}, bf16[1024,768]{1,0:T(8,128)(2,1)}, u32[]{:S(2)}, u32[]{:S(2)}) collective-permute-start(bf16[1024,768]{1,0:T(8,128)(2,1)} %slice.12), channel_id=1, source_target_pairs={{0,8},{8,16},{16,24},{24,32},{32,40},{40,48},{48,56},{56,64},{64,7... | collective-permute-start | bytes 4718600 | tf_op jit(solution)/shard_map/ppermute | solution.py:271
  173.9 62.7 %collective-permute-start.1 = (bf16[1024,768]{1,0:T(8,128)(2,1)}, bf16[1024,768]{1,0:T(8,128)(2,1)}, u32[]{:S(2)}, u32[]{:S(2)}) collective-permute-start(bf16[1024,768]{1,0:T(8,128)(2,1)} %slice.12), channel_id=1, source_target_pairs={{8,0},{16,8},{24,16},{32,24},{40,32},{48,40},{56,48},{64,56},{72,6... | collective-permute-start | bytes 4718600 | tf_op jit(solution)/shard_map/ppermute | solution.py:272

commit v3 on v2

--- a/solution.py
+++ b/solution.py
@@ -31,32 +31,103 @@
     return lax.dot_general(a, b, dims, preferred_element_type=jnp.float32)
 
 
-def pack_kernel(q_ref, k_ref, v_ref, out_ref):
+def lead_kernel(k_ref, v_ref, out_ref):
     peers = out_ref.shape[0]
+    local = k_ref.shape[1] // peers
+    for j in range(peers):
+        out_ref[j, :, :HDIM] = k_ref[:, j * local : j * local + HDIM]
+        out_ref[j, :, HDIM:] = v_ref[:, j * local : j * local + HDIM]
+
+
+def pack_lead(keys, values, peers):
+    rows, width = keys.shape
+    tile = rows // PACK_STEPS
+    spec = pl.BlockSpec((tile, width), lambda i: (i, 0))
+    return pl.pallas_call(
+        lead_kernel,
+        grid=(PACK_STEPS,),
+        in_specs=[spec] * 2,
+        out_specs=pl.BlockSpec((peers, tile, 2 * HDIM), lambda i: (0, i, 0)),
+        out_shape=pltpu.HBM((peers, rows, 2 * HDIM), keys.dtype),
+        compiler_params=PARAMS,
+        name="lead",
+    )(*in_hbm(keys, values))
+
+
+def rest_kernel(me_ref, q_ref, k_ref, v_ref, *out_refs):
+    peers = len(out_refs)
     local = q_ref.shape[1] // peers
-    for j in range(peers):
-        for h in range(local // HDIM):
-            cols = slice(j * local + h * HDIM, j * local + (h + 1) * HDIM)
-            base = 2 * h * HDIM
-            out_ref[j, :, base : base + HDIM] = k_ref[:, cols]
-            out_ref[j, :, base + HDIM : base + 2 * HDIM] = v_ref[:, cols]
-        out_ref[j, :, 2 * local :] = q_ref[:, j * local : (j + 1) * local]
-
-
-def pack(queries, keys, values, peers):
+    heads = local // HDIM
+    for d, out_ref in enumerate(out_refs):
+        base = lax.rem(me_ref[0] + d, peers) * local
+        for h in range(1, heads):
+            cols = pl.ds(pl.multiple_of(base + h * HDIM, HDIM), HDIM)
+            left = 2 * (h - 1) * HDIM
+            out_ref[:, left : left + HDIM] = k_ref[:, cols]
+            out_ref[:, left + HDIM : left + 2 * HDIM] = v_ref[:, cols]
+        left = 2 * (heads - 1) * HDIM
+        for h in range(heads):
+            cols = pl.ds(pl.multiple_of(base + h * HDIM, HDIM), HDIM)
+            out_ref[:, left + h * HDIM : left + (h + 1) * HDIM] = q_ref[:, cols]
+
+
+def pack_rest(me, queries, keys, values, peers):
     rows, width = queries.shape
     local = width // peers
+    size = 3 * local - 2 * HDIM
     tile = rows // PACK_STEPS
-    spec = pl.BlockSpec((tile, width), lambda i: (i, 0))
-    return pl.pallas_call(
-        pack_kernel,
-        grid=(PACK_STEPS,),
-        in_specs=[spec] * 3,
-        out_specs=pl.BlockSpec((peers, tile, 3 * local), lambda i: (0, i, 0)),
-        out_shape=pltpu.HBM((peers, rows, 3 * local), queries.dtype),
-        compiler_params=PARAMS,
-        name="pack",
-    )(*in_hbm(queries, keys, values))
+    spec = pl.BlockSpec((tile, width), lambda i, m: (i, 0))
+    return pl.pallas_call(
+        rest_kernel,
+        grid_spec=pltpu.PrefetchScalarGridSpec(
+            num_scalar_prefetch=1,
+            grid=(PACK_STEPS,),
+            in_specs=[spec] * 3,
+            out_specs=[pl.BlockSpec((tile, size), lambda i, m: (i, 0))] * peers,
+        ),
+        out_shape=[pltpu.HBM((rows, size), queries.dtype)] * peers,
+        compiler_params=PARAMS,
+        name="rest",
+    )(me, *in_hbm(queries, keys, values))
+
+
+def gather_kernel(me_ref, lead_ref, *refs):
+    parts, (mixed_ref, pairs_ref) = refs[:-2], refs[-2:]
+    peers = len(parts)
+    split = pairs_ref.shape[2] - 2 * HDIM
+    mixed_ref[:, :, : 2 * HDIM] = lead_ref[...]
+    pairs_ref[:, :, : 2 * HDIM] = lead_ref[...]
+    for d, ref in enumerate(parts):
+        block = lax.rem(me_ref[0] - d + peers, peers)
+        part = ref[...]
+        mixed_ref[block, :, 2 * HDIM :] = part
+        pairs_ref[block, :, 2 * HDIM :] = part[:, :split]
+
+
+def assemble(me, lead, parts):
+    peers, rows, _ = lead.shape
+    size = parts[0].shape[1]
+    local = (size + 2 * HDIM) // 3
+    tile = rows // PACK_STEPS
+    return pl.pallas_call(
+        gather_kernel,
+        grid_spec=pltpu.PrefetchScalarGridSpec(
+            num_scalar_prefetch=1,
+            grid=(PACK_STEPS,),
+            in_specs=[pl.BlockSpec((peers, tile, 2 * HDIM), lambda i, m: (0, i, 0))]
+            + [pl.BlockSpec((tile, size), lambda i, m: (i, 0))] * peers,
+            out_specs=[
+                pl.BlockSpec((peers, tile, 3 * local), lambda i, m: (0, i, 0)),
+                pl.BlockSpec((peers, tile, 2 * local), lambda i, m: (0, i, 0)),
+            ],
+        ),
+        out_shape=[
+            pltpu.HBM((peers, rows, 3 * local), lead.dtype),
+            pltpu.HBM((peers, rows, 2 * local), lead.dtype),
+        ],
+        compiler_params=PARAMS,
+        name="assemble",
+    )(me, lead, *parts)
 
 
 def unpack_kernel(part_ref, out_ref):
@@ -79,35 +150,39 @@
     )(parts)
 
 
-def select_kernel(pick_ref, kv_ref, out_ref):
+def select_kernel(pick_ref, *refs):
+    out_ref = refs[-1]
     base = pl.program_id(0) * out_ref.shape[0]
     for i in range(out_ref.shape[0]):
-        out_ref[i] = kv_ref[pick_ref[base + i]]
-
-
-def select_blocks(picks, blocks, head):
+        for g, kv_ref in enumerate(refs[:-1]):
+            out_ref[i, :, 2 * g * HDIM : 2 * (g + 1) * HDIM] = kv_ref[pick_ref[base + i]]
+
+
+def select_blocks(picks, blocks, heads):
     frames = picks.shape[0]
     step = frames // SELECT_STEPS
     count, rows, _ = blocks.shape
-    width = 2 * HDIM
+    width = 2 * HDIM * len(heads)
     return pl.pallas_call(
         select_kernel,
         grid_spec=pltpu.PrefetchScalarGridSpec(
             num_scalar_prefetch=1,
-            grid=(frames // step,),
-            in_specs=[pl.BlockSpec((count, rows, width), lambda i, p: (0, 0, head))],
+            grid=(SELECT_STEPS,),
+            in_specs=[
+                pl.BlockSpec((count, rows, 2 * HDIM), lambda i, p, h=h: (0, 0, h)) for h in heads
+            ],
             out_specs=pl.BlockSpec((step, rows, width), lambda i, p: (i, 0, 0)),
         ),
         out_shape=pltpu.HBM((frames, rows, width), blocks.dtype),
         compiler_params=PARAMS,
         name="select",
-    )(picks, blocks)
+    )(picks, *([blocks] * len(heads)))
 
 
 def near_kernel(on_ref, q_ref, own_ref, before_ref, after_ref, o_ref, m_ref, l_ref):
     tile = q_ref.shape[0]
     sub = tile // BLOCK
-    first = pl.program_id(0) * sub
+    first = pl.program_id(1) * sub
     query = q_ref[...]
     parts = [dot(query, own_ref[:, :HDIM], NT)]
     for side, ref in enumerate((before_ref, after_ref)):
@@ -135,30 +210,38 @@
     l_ref[...] = mass
 
 
-def near_attention(near_on, mixed, head, before, after):
+def near_attention(near_on, mixed, before, after):
     tile = 256
     rows, width = mixed.shape
-    column = width // HDIM - HEADS_LOCAL + head
-    whole = pl.BlockSpec((rows, 2 * HDIM), lambda i, on: (0, head))
-    flops = 4 * rows * 3 * rows * HDIM
+    heads = HEADS_LOCAL
+    first = width // HDIM - heads
+    whole = pl.BlockSpec((rows, 2 * HDIM), lambda h, i, on: (0, h))
     return pl.pallas_call(
         near_kernel,
         grid_spec=pltpu.PrefetchScalarGridSpec(
             num_scalar_prefetch=1,
-            grid=(rows // tile,),
-            in_specs=[pl.BlockSpec((tile, HDIM), lambda i, on: (i, column)), whole, whole, whole],
-            out_specs=[pl.BlockSpec((tile, HDIM), lambda i, on: (i, 0))] * 3,
-        ),
-        out_shape=[pltpu.HBM((rows, HDIM), jnp.float32)] * 3,
+            grid=(heads, rows // tile),
+            in_specs=[
+                pl.BlockSpec((tile, HDIM), lambda h, i, on: (i, first + h)),
+                whole,
+                whole,
+                whole,
+            ],
+            out_specs=[pl.BlockSpec((tile, HDIM), lambda h, i, on: (i, h))] * 3,
+        ),
+        out_shape=[pltpu.HBM((rows, heads * HDIM), jnp.float32)] * 3,
         cost_estimate=pl.CostEstimate(
-            flops=flops, bytes_accessed=4 * rows * 2 * HDIM * 2, transcendentals=3 * rows * rows
+            flops=12 * heads * rows * rows * HDIM,
+            bytes_accessed=8 * heads * rows * 2 * HDIM,
+            transcendentals=3 * heads * rows * rows,
         ),
         compiler_params=PARAMS,
         name="near",
     )(near_on, mixed, mixed, before, after)
 
 
-def far_kernel(list_ref, count_ref, q_ref, kv_ref, o_ref, m_ref, l_ref, out_ref, m_s, l_s, acc_s):
+def far_kernel(list_ref, count_ref, q_ref, kv_ref, o_ref, m_ref, l_ref, *refs):
+    out_ref, m_s, l_s, acc_s = refs[-4:]
     m_s[...] = m_ref[...]
     l_s[...] = l_ref[...]
     acc_s[...] = o_ref[...]
@@ -195,23 +278,26 @@
     out_ref[...] = (acc_s[...] / total).astype(out_ref.dtype)
 
 
-def far_attention(order, counts, mixed, head, far, near):
+def far_attention(order, counts, mixed, heads, far, near, result):
     rows, width = mixed.shape
-    column = width // HDIM - HEADS_LOCAL + head
+    column = width // HDIM - HEADS_LOCAL + heads[0]
+    first = heads[0]
     frames = far.shape[0]
-    full = pl.BlockSpec((rows, HDIM), lambda i, a, b: (0, 0))
+    full = pl.BlockSpec((rows, HDIM), lambda g, a, b: (0, first + g))
+    operands = [order, counts, mixed, far, *in_hbm(*near)] + ([] if result is None else [result])
     return pl.pallas_call(
         far_kernel,
         grid_spec=pltpu.PrefetchScalarGridSpec(
             num_scalar_prefetch=2,
-            grid=(1,),
+            grid=(len(heads),),
             in_specs=[
-                pl.BlockSpec((rows, HDIM), lambda i, a, b: (0, column)),
-                pl.BlockSpec((frames, BLOCK, 2 * HDIM), lambda i, a, b: (0, 0, 0)),
+                pl.BlockSpec((rows, HDIM), lambda g, a, b: (0, column + g)),
+                pl.BlockSpec((frames, BLOCK, 2 * HDIM), lambda g, a, b: (0, 0, g)),
                 full,
                 full,
                 full,
-            ],
+            ]
+            + ([] if result is None else [pl.BlockSpec(memory_space=pl.ANY)]),
             out_specs=full,
             scratch_shapes=[
                 pltpu.VMEM((rows, HDIM), jnp.float32),
@@ -219,15 +305,16 @@
                 pltpu.VMEM((rows, HDIM), jnp.float32),
             ],
         ),
-        out_shape=jax.ShapeDtypeStruct((rows, HDIM), mixed.dtype),
+        out_shape=pltpu.HBM((rows, HEADS_LOCAL * HDIM), mixed.dtype),
+        input_output_aliases={} if result is None else {7: 0},
         cost_estimate=pl.CostEstimate(
-            flops=rows * frames * BLOCK * HDIM,
-            bytes_accessed=frames * BLOCK * 2 * HDIM * 2,
-            transcendentals=rows * frames * BLOCK // 4,
+            flops=len(heads) * rows * frames * BLOCK * HDIM,
+            bytes_accessed=len(heads) * frames * BLOCK * 2 * HDIM * 2,
+            transcendentals=len(heads) * rows * frames * BLOCK // 4,
         ),
         compiler_params=PARAMS,
         name="far",
-    )(order, counts, mixed, far, *in_hbm(*near))
+    )(*operands)
 
 
 def mask_tables(block_mask, frame_id, frame_count):
@@ -255,26 +342,31 @@
     frame_count = lax.axis_size("frame")
     peers = lax.axis_size("head")
     frame_id = lax.axis_index("frame")
+    me = lax.axis_index("head").astype(jnp.int32).reshape(1)
     exchange = functools.partial(lax.all_to_all, split_axis=0, concat_axis=0, tiled=True)
     up = [(i, i + 1) for i in range(frame_count - 1)]
     down = [(j, i) for i, j in up]
-    heads = range(HEADS_LOCAL)
+    early, late = [0], list(range(1, HEADS_LOCAL))
     outgoing, near_on, order, counts = mask_tables(block_mask, frame_id, frame_count)
-    packed = pack(queries, key_rows, value_rows, peers)
-    blocks = exchange(packed, "head")
+    lead = exchange(pack_lead(key_rows, value_rows, peers), "head")
+    parts = pack_rest(me, queries, key_rows, value_rows, peers)
+    parcel = select_blocks(outgoing, lead, early)
+    far_early = exchange(parcel, "frame")
+    moved = [parts[0]]
+    for d in range(1, peers):
+        turn = [(i, (i + d) % peers) for i in range(peers)]
+        moved.append(lax.ppermute(parts[d], "head", turn))
+    blocks, pairs = assemble(me, lead, moved)
     mixed = blocks.reshape(FT, blocks.shape[2])
-    far = []
-    for head in heads:
-        parcel = select_blocks(outgoing, blocks, head)
-        far.append(exchange(parcel, "frame"))
-    pairs = mixed[:, : 2 * HDIM * HEADS_LOCAL]
+    pairs = pairs.reshape(FT, pairs.shape[2])
+    parcel = select_blocks(outgoing, blocks, late)
+    far_late = exchange(parcel, "frame")
     before = lax.ppermute(pairs, "frame", up)
     after = lax.ppermute(pairs, "frame", down)
-    outs = []
-    for head in heads:
-        near = near_attention(near_on, mixed, head, before, after)
-        outs.append(far_attention(order, counts, mixed, head, far[head], near))
-    result = jnp.concatenate(outs, axis=1).reshape(peers, BLOCK, HEADS_LOCAL * HDIM)
+    near = near_attention(near_on, mixed, before, after)
+    result = far_attention(order, counts, mixed, early, far_early, near, None)
+    result = far_attention(order, counts, mixed, late, far_late, near, result)
+    result = result.reshape(peers, BLOCK, HEADS_LOCAL * HDIM)
     return unpack(exchange(result, "head"))
 
 

time: 299 us -> 267 us (0.89)
  waiting for transfers between devices: 188 us -> 133 us
  starting transfers between devices: 36.4 us -> 56.7 us
    all_to_all x4 -> x3, waiting for transfers between devices: 132 us -> 9.22 us  [the longest x1 9.21 us: body(): lead = exchange(pack_lead(key_rows, value_rows, peers), 'head')]
    ppermute x1, waiting for transfers between devices: 55.7 us -> 102 us  [body(): before = lax.ppermute(pairs, 'frame', up)]
    ppermute x0 -> x7, waiting for transfers between devices: none -> 22 us  [body(): moved.append(lax.ppermute(parts[d], 'head', turn))]
    ppermute x0 -> x7, starting transfers between devices: none -> 19.3 us  [body(): moved.append(lax.ppermute(parts[d], 'head', turn))]
    pallas_call x1 -> x3, Pallas kernels: 4.08 us -> 9.97 us  [the longest x1 3.99 us: pack_rest(): pl.pallas_call(rest_kernel, grid_spec=pltpu.PrefetchScalarGridSpec(num_sc...]
    pallas_call x3 -> x1, Pallas kernels: 23.7 us -> 19 us  [near_attention(): pl.pallas_call(near_kernel, grid_spec=pltpu.PrefetchScalarGridSpec(num_sc...]
    pallas_call x3 -> x2, Pallas kernels: 6.02 us -> 4.67 us  [select_blocks(): pl.pallas_call(select_kernel, grid_spec=pltpu.PrefetchScalarGridSpec(num_...]
    pallas_call x3 -> x2, Pallas kernels: 21.8 us -> 20.7 us  [far_attention(): pl.pallas_call(far_kernel, grid_spec=pltpu.PrefetchScalarGridSpec(num_sca...]
  transfers between devices with their start and end apart: 6 -> 12, of which waited for: 4 -> 5; matrix products, arithmetic and copies ran while one was open for 1% -> 0% of each run, Pallas kernels for 14% -> 14%
where the time goes in v3:
time: 267 us; the launch traced here: 265 us
  waiting for transfers between devices  133 us (50%)
  starting transfers between devices  56.7 us (21%)
  Pallas kernels  55.9 us (21%)
  blocking collectives  14.9 us (6%)
  local copies, waits for them, and re-layouts  2.88 us (1%)
    ppermute x1, waiting for transfers between devices, body(): before = lax.ppermute(pairs, 'frame', up)  102 us
    ppermute x7, waiting for transfers between devices, body(): moved.append(lax.ppermute(parts[d], 'head', turn))  22 us
    pallas_call x2, Pallas kernels, far_attention(): pl.pallas_call(far_kernel, grid_spec=pltpu.PrefetchScalarGridSpec(num_sca...  20.7 us
    ppermute x7, starting transfers between devices, body(): moved.append(lax.ppermute(parts[d], 'head', turn))  19.3 us
    pallas_call x1, Pallas kernels, near_attention(): pl.pallas_call(near_kernel, grid_spec=pltpu.PrefetchScalarGridSpec(num_sc...  19 us
    all_to_all x1, blocking collectives, body(): return unpack(exchange(result, 'head'))  14.9 us
    all_to_all x1, starting transfers between devices, body(): far_late = exchange(parcel, 'frame')  13 us
    all_to_all x1, starting transfers between devices, body(): far_early = exchange(parcel, 'frame')  11.1 us
  transfers between devices with their start and end apart: 12, of which 5 were waited for; matrix products, arithmetic and copies ran while one was open for 0% of the time, Pallas kernels for 14%

profile of v3, /device:TPU:32, one launch (start us, length us, event | category | flops | bytes accessed | tf_op | source)
XLA Modules:
  0.0 264.6 jit_solution(16469099401004743417)
XLA Ops:
  0.0 0.0 copy-start
  0.0 3.5 %lead.1 = bf16[8,128,256]{2,1,0:T(8,128)(2,1)} custom-call(bf16[128,3072]{1,0:T(8,128)(2,1)} %k_ref.3, bf16[128,3072]{1,0:T(8,128)(2,1)} %v_ref.3), custom_call_target="tpu_custom_call" | custom-call | tf_op jit(solution)/shard_map/lead/pallas_call | solution.py:46
  3.5 5.3 %all-to-all-start = ((bf16[8,128,256]{2,1,0:T(8,128)(2,1)}), bf16[8,128,256]{2,1,0:T(8,128)(2,1)S(1)}, u32[]{:S(2)}, u32[]{:S(2)}) async-start(bf16[8,128,256]{2,1,0:T(8,128)(2,1)} %lead.1), calls=%async_computation | async-start | bytes 1048576 | tf_op jit(solution)/shard_map/all_to_all | solution.py:351
  8.8 0.0 copy-done
  8.8 0.1 bitcast_reduce_fusion
  8.9 0.1 multiply_reduce_fusion.1
  9.1 9.2 %all-to-all-done.lead_ref.refs_0_ = bf16[8,128,256]{2,1,0:T(8,128)(2,1)S(1)} async-done(((bf16[8,128,256]{2,1,0:T(8,128)(2,1)}), bf16[8,128,256]{2,1,0:T(8,128)(2,1)S(1)}, u32[]{:S(2)}, u32[]{:S(2)}) %all-to-all-start) | async-done | bytes 524320 | tf_op jit(solution)/shard_map/all_to_all | solution.py:351
  18.3 1.9 select.5
  20.2 11.1 %all-to-all-start.2 = ((bf16[32,128,256]{2,1,0:T(8,128)(2,1)}), bf16[32,128,256]{2,1,0:T(8,128)(2,1)}, u32[]{:S(2)}, u32[]{:S(2)}) async-start(bf16[32,128,256]{2,1,0:T(8,128)(2,1)} %select.5), calls=%async_computation.2 | async-start | bytes 4194304 | tf_op jit(solution)/shard_map/all_to_all | solution.py:354
  31.4 4.0 %rest.1 = (bf16[128,896]{1,0:T(8,128)(2,1)}, bf16[128,896]{1,0:T(8,128)(2,1)}, bf16[128,896]{1,0:T(8,128)(2,1)}, bf16[128,896]{1,0:T(8,128)(2,1)}, bf16[128,896]...) custom-call(s32[1]{0:T(128)} %bitcast.me_ref, ...), custom_call_target="tpu_custom_call" | custom-call | tf_op jit(solution)/shard_map/rest/pallas_call | solution.py:80
  35.3 0.9 collective-permute-start
  36.3 0.6 collective-permute-start.1
  36.8 2.1 collective-permute-start.2
  38.9 2.8 %collective-permute-start.3 = (bf16[128,896]{1,0:T(8,128)(2,1)}, bf16[128,896]{1,0:T(8,128)(2,1)S(1)}, u32[]{:S(2)}, u32[]{:S(2)}) collective-permute-start(bf16[128,896]{1,0:T(8,128)(2,1)} %get-tuple-element.22), channel_id=1, source_target_pairs={{0,4},{1,5},{2,6},{3,7},{4,0},{5,1},{6,2},{7,3},{8,12},{9,13},{10,... | collective-permute-start | bytes 688136 | tf_op jit(solution)/shard_map/ppermute | solution.py:358
  41.7 1.7 collective-permute-start.4
  43.3 11.6 %collective-permute-done.refs_1_ = bf16[128,896]{1,0:T(8,128)(2,1)S(1)} collective-permute-done((bf16[128,896]{1,0:T(8,128)(2,1)}, bf16[128,896]{1,0:T(8,128)(2,1)S(1)}, u32[]{:S(2)}, u32[]{:S(2)}) %collective-permute-start) | collective-permute-done | bytes 229408 | tf_op jit(solution)/shard_map/ppermute | solution.py:358
  55.0 8.5 %collective-permute-start.5 = (bf16[128,896]{1,0:T(8,128)(2,1)}, bf16[128,896]{1,0:T(8,128)(2,1)S(1)}, u32[]{:S(2)}, u32[]{:S(2)}) collective-permute-start(bf16[128,896]{1,0:T(8,128)(2,1)} %get-tuple-element.24), channel_id=1, source_target_pairs={{0,6},{1,7},{2,0},{3,1},{4,2},{5,3},{6,4},{7,5},{8,14},{9,15},{10,... | collective-permute-start | bytes 688136 | tf_op jit(solution)/shard_map/ppermute | solution.py:358
  63.4 0.0 collective-permute-done.1.refs_2_
  63.4 2.9 %collective-permute-start.6 = (bf16[128,896]{1,0:T(8,128)(2,1)}, bf16[128,896]{1,0:T(8,128)(2,1)S(1)}, u32[]{:S(2)}, u32[]{:S(2)}) collective-permute-start(bf16[128,896]{1,0:T(8,128)(2,1)} %get-tuple-element.25), channel_id=1, source_target_pairs={{0,7},{1,0},{2,1},{3,2},{4,3},{5,4},{6,5},{7,6},{8,15},{9,8},{10,9... | collective-permute-start | bytes 688136 | tf_op jit(solution)/shard_map/ppermute | solution.py:358
  66.3 0.0 collective-permute-done.2.refs_3_
  66.3 0.0 collective-permute-done.3.refs_4_
  66.3 0.0 collective-permute-done.4.refs_5_
  66.3 3.4 %collective-permute-done.5.refs_6_ = bf16[128,896]{1,0:T(8,128)(2,1)S(1)} collective-permute-done((bf16[128,896]{1,0:T(8,128)(2,1)}, bf16[128,896]{1,0:T(8,128)(2,1)S(1)}, u32[]{:S(2)}, u32[]{:S(2)}) %collective-permute-start.5) | collective-permute-done | bytes 229408 | tf_op jit(solution)/shard_map/ppermute | solution.py:358
  69.7 6.9 %collective-permute-done.6.refs_7_ = bf16[128,896]{1,0:T(8,128)(2,1)S(1)} collective-permute-done((bf16[128,896]{1,0:T(8,128)(2,1)}, bf16[128,896]{1,0:T(8,128)(2,1)S(1)}, u32[]{:S(2)}, u32[]{:S(2)}) %collective-permute-start.6) | collective-permute-done | bytes 229408 | tf_op jit(solution)/shard_map/ppermute | solution.py:358
  76.7 0.9 copy-done.3
  77.6 2.5 assemble.1
  80.1 1.7 copy-done.1
  81.8 2.7 %select.4 = bf16[32,128,512]{2,1,0:T(8,128)(2,1)} custom-call(s32[32]{0:T(128)S(1)} %broadcast_minimum_fusion.pick_ref, bf16[8,128,1152]{2,1,0:T(8,128)(2,1)S(1)} %copy-done.1, bf16[8,128,1152]{2,1,0:T(8,128)(2,1)S(1)} %copy-done.1), custom_call_target="tpu_custom_call" | custom-call | tf_op jit(solution)/shard_map/select/pallas_call | solution.py:166
  84.5 0.0 all-to-all-done.2.kv_ref
  84.5 13.0 %all-to-all-start.1 = ((bf16[32,128,512]{2,1,0:T(8,128)(2,1)}), bf16[32,128,512]{2,1,0:T(8,128)(2,1)}, u32[]{:S(2)}, u32[]{:S(2)}) async-start(bf16[32,128,512]{2,1,0:T(8,128)(2,1)} %select.4), calls=%async_computation.1 | async-start | bytes 8388608 | tf_op jit(solution)/shard_map/all_to_all | solution.py:363
  97.5 2.0 collective-permute-start.7
  99.6 5.9 %collective-permute-start.8 = (bf16[1024,768]{1,0:T(8,128)(2,1)}, bf16[1024,768]{1,0:T(8,128)(2,1)}, u32[]{:S(2)}, u32[]{:S(2)}) collective-permute-start(bf16[1024,768]{1,0:T(8,128)(2,1)} %bitcast.12), channel_id=1, source_target_pairs={{8,0},{16,8},{24,16},{32,24},{40,32},{48,40},{56,48},{64,56},{72,6... | collective-permute-start | bytes 4718600 | tf_op jit(solution)/shard_map/ppermute | solution.py:365
  105.5 0.1 reshape.72
  105.6 0.2 reduce_max.18
  105.9 0.1 pad_dynamic-slice_fusion
  105.9 0.1 fusion.2
  106.0 0.1 pad_add_fusion.on_ref
  106.1 0.1 fusion.1
  106.2 0.1 multiply_reduce_fusion
  106.3 0.1 select_reduce_fusion.list_ref
  106.5 102.1 %collective-permute-done.7.before_ref = bf16[1024,768]{1,0:T(8,128)(2,1)} collective-permute-done((bf16[1024,768]{1,0:T(8,128)(2,1)}, bf16[1024,768]{1,0:T(8,128)(2,1)}, u32[]{:S(2)}, u32[]{:S(2)}) %collective-permute-start.7) | collective-permute-done | bytes 1572896 | tf_op jit(solution)/shard_map/ppermute | solution.py:364
  208.5 0.0 collective-permute-done.8.after_ref
  208.5 19.0 %near.1 = (f32[1024,384]{1,0:T(8,128)}, f32[1024,384]{1,0:T(8,128)}, f32[1024,384]{1,0:T(8,128)}) custom-call(s32[8,16]{1,0:T(8,128)S(1)} %pad_add_fusion.on_ref, bf16[1024,1152]{1,0:T(8,128)(2,1)S(1)} %bitcast.6, bf16[1024,1152]{1,0:T(8,128)(2,1)S(1)} %bitcast.7, bf16[1024,768]{1,0:T(8,128)(2,1)} %collective-permute-done.7.before_ref, ...), custom_call_target="tpu_custom_call" | custom-call | flops 4831838208 | bytes 6291456 | tf_op jit(solution)/shard_map/near/pallas_call | solution.py:219
  227.5 8.0 %far.2.refs_0_ = bf16[1024,384]{1,0:T(8,128)(2,1)} custom-call(s32[8,32]{1,0:T(8,128)S(1)} %select_reduce_fusion.list_ref, s32[8]{0:T(128)S(1)} %get-tuple-element.31.count_ref, bf16[1024,1152]{1,0:T(8,128)(2,1)S(1)} %bitcast.8, bf16[32,128,256]{2,1,0:T(8,128)(2,1)} %all-to-all-done.2.kv_ref, f32[1024,384]{1,0:T(8,128)} %get-tuple-element.28.o_ref, ...), custom_call_target="tpu_custom_call" | custom-call | flops 536870912 | bytes 2097152 | tf_op jit(solution)/shard_map/far/pallas_call | solution.py:288
  235.5 0.0 all-to-all-done.1.kv_ref
  235.5 12.7 %far.3 = bf16[1024,384]{1,0:T(8,128)(2,1)} custom-call(s32[8,32]{1,0:T(8,128)S(1)} %select_reduce_fusion.list_ref, s32[8]{0:T(128)S(1)} %get-tuple-element.31.count_ref, bf16[1024,1152]{1,0:T(8,128)(2,1)S(1)} %bitcast.9, bf16[32,128,512]{2,1,0:T(8,128)(2,1)} %all-to-all-done.1.kv_ref, ...), custom_call_target="tpu_custom_call", output_to_operand_aliasing={{}: (7, {})} | custom-call | flops 1073741824 | bytes 4194304 | tf_op jit(solution)/shard_map/far/pallas_call | solution.py:288
  248.2 14.9 %all_to_all.20.part_ref = bf16[8,128,384]{2,1,0:T(8,128)(2,1)S(1)} all-to-all(bf16[8,128,384]{2,1,0:T(8,128)(2,1)} %bitcast.10), channel_id=1, replica_groups=mesh['frame'=32,'head'=8] {'head'}, dimensions={0} | all-to-all | bytes 1572864 | tf_op jit(solution)/shard_map/all_to_all | solution.py:370
  263.1 1.5 unpack.1
  (9 shorter events, 0.0 us)
Async XLA Ops:
  0.0 8.8 %copy-start = (s32[256,256]{1,0:T(8,128)S(1)}, s32[256,256]{1,0:T(8,128)}, u32[]{:S(2)}) copy-start(s32[256,256]{1,0:T(8,128)} %param.7) | copy-start | bytes 786436
  3.5 14.8 %all-to-all-start = ((bf16[8,128,256]{2,1,0:T(8,128)(2,1)}), bf16[8,128,256]{2,1,0:T(8,128)(2,1)S(1)}, u32[]{:S(2)}, u32[]{:S(2)}) async-start(bf16[8,128,256]{2,1,0:T(8,128)(2,1)} %lead.1), calls=%async_computation | async-start | bytes 1048576 | tf_op jit(solution)/shard_map/all_to_all | solution.py:351
  20.2 64.3 %all-to-all-start.2 = ((bf16[32,128,256]{2,1,0:T(8,128)(2,1)}), bf16[32,128,256]{2,1,0:T(8,128)(2,1)}, u32[]{:S(2)}, u32[]{:S(2)}) async-start(bf16[32,128,256]{2,1,0:T(8,128)(2,1)} %select.5), calls=%async_computation.2 | async-start | bytes 4194304 | tf_op jit(solution)/shard_map/all_to_all | solution.py:354
  35.3 19.6 %collective-permute-start = (bf16[128,896]{1,0:T(8,128)(2,1)}, bf16[128,896]{1,0:T(8,128)(2,1)S(1)}, u32[]{:S(2)}, u32[]{:S(2)}) collective-permute-start(bf16[128,896]{1,0:T(8,128)(2,1)} %get-tuple-element.19), channel_id=1, source_target_pairs={{0,1},{1,2},{2,3},{3,4},{4,5},{5,6},{6,7},{7,0},{8,9},{9,10},{10,1... | collective-permute-start | bytes 688136 | tf_op jit(solution)/shard_map/ppermute | solution.py:358
  36.3 27.2 %collective-permute-start.1 = (bf16[128,896]{1,0:T(8,128)(2,1)}, bf16[128,896]{1,0:T(8,128)(2,1)S(1)}, u32[]{:S(2)}, u32[]{:S(2)}) collective-permute-start(bf16[128,896]{1,0:T(8,128)(2,1)} %get-tuple-element.20), channel_id=1, source_target_pairs={{0,2},{1,3},{2,4},{3,5},{4,6},{5,7},{6,0},{7,1},{8,10},{9,11},{10,... | collective-permute-start | bytes 688136 | tf_op jit(solution)/shard_map/ppermute | solution.py:358
  36.8 29.5 %collective-permute-start.2 = (bf16[128,896]{1,0:T(8,128)(2,1)}, bf16[128,896]{1,0:T(8,128)(2,1)S(1)}, u32[]{:S(2)}, u32[]{:S(2)}) collective-permute-start(bf16[128,896]{1,0:T(8,128)(2,1)} %get-tuple-element.21), channel_id=1, source_target_pairs={{0,3},{1,4},{2,5},{3,6},{4,7},{5,0},{6,1},{7,2},{8,11},{9,12},{10,... | collective-permute-start | bytes 688136 | tf_op jit(solution)/shard_map/ppermute | solution.py:358
  38.9 27.4 %collective-permute-start.3 = (bf16[128,896]{1,0:T(8,128)(2,1)}, bf16[128,896]{1,0:T(8,128)(2,1)S(1)}, u32[]{:S(2)}, u32[]{:S(2)}) collective-permute-start(bf16[128,896]{1,0:T(8,128)(2,1)} %get-tuple-element.22), channel_id=1, source_target_pairs={{0,4},{1,5},{2,6},{3,7},{4,0},{5,1},{6,2},{7,3},{8,12},{9,13},{10,... | collective-permute-start | bytes 688136 | tf_op jit(solution)/shard_map/ppermute | solution.py:358
  41.7 24.7 %collective-permute-start.4 = (bf16[128,896]{1,0:T(8,128)(2,1)}, bf16[128,896]{1,0:T(8,128)(2,1)S(1)}, u32[]{:S(2)}, u32[]{:S(2)}) collective-permute-start(bf16[128,896]{1,0:T(8,128)(2,1)} %get-tuple-element.23), channel_id=1, source_target_pairs={{0,5},{1,6},{2,7},{3,0},{4,1},{5,2},{6,3},{7,4},{8,13},{9,14},{10,... | collective-permute-start | bytes 688136 | tf_op jit(solution)/shard_map/ppermute | solution.py:358
  55.0 14.8 %collective-permute-start.5 = (bf16[128,896]{1,0:T(8,128)(2,1)}, bf16[128,896]{1,0:T(8,128)(2,1)S(1)}, u32[]{:S(2)}, u32[]{:S(2)}) collective-permute-start(bf16[128,896]{1,0:T(8,128)(2,1)} %get-tuple-element.24), channel_id=1, source_target_pairs={{0,6},{1,7},{2,0},{3,1},{4,2},{5,3},{6,4},{7,5},{8,14},{9,15},{10,... | collective-permute-start | bytes 688136 | tf_op jit(solution)/shard_map/ppermute | solution.py:358
  63.4 13.2 %collective-permute-start.6 = (bf16[128,896]{1,0:T(8,128)(2,1)}, bf16[128,896]{1,0:T(8,128)(2,1)S(1)}, u32[]{:S(2)}, u32[]{:S(2)}) collective-permute-start(bf16[128,896]{1,0:T(8,128)(2,1)} %get-tuple-element.25), channel_id=1, source_target_pairs={{0,7},{1,0},{2,1},{3,2},{4,3},{5,4},{6,5},{7,6},{8,15},{9,8},{10,9... | collective-permute-start | bytes 688136 | tf_op jit(solution)/shard_map/ppermute | solution.py:358
  76.7 0.9 copy-start.3
  80.1 1.7 copy-start.1
  84.5 124.0 %copy-start.2 = (bf16[8,128,1152]{2,1,0:T(8,128)(2,1)S(1)}, bf16[8,128,1152]{2,1,0:T(8,128)(2,1)}, u32[]{:S(2)}) copy-start(bf16[8,128,1152]{2,1,0:T(8,128)(2,1)} %get-tuple-element.26.refs_0_.refs_1_) | copy-start | bytes 7077892
  84.5 151.0 %all-to-all-start.1 = ((bf16[32,128,512]{2,1,0:T(8,128)(2,1)}), bf16[32,128,512]{2,1,0:T(8,128)(2,1)}, u32[]{:S(2)}, u32[]{:S(2)}) async-start(bf16[32,128,512]{2,1,0:T(8,128)(2,1)} %select.4), calls=%async_computation.1 | async-start | bytes 8388608 | tf_op jit(solution)/shard_map/all_to_all | solution.py:363
  97.5 111.0 %collective-permute-start.7 = (bf16[1024,768]{1,0:T(8,128)(2,1)}, bf16[1024,768]{1,0:T(8,128)(2,1)}, u32[]{:S(2)}, u32[]{:S(2)}) collective-permute-start(bf16[1024,768]{1,0:T(8,128)(2,1)} %bitcast.11), channel_id=1, source_target_pairs={{0,8},{8,16},{16,24},{24,32},{32,40},{40,48},{48,56},{56,64},{64,7... | collective-permute-start | bytes 4718600 | tf_op jit(solution)/shard_map/ppermute | solution.py:364
  99.6 109.0 %collective-permute-start.8 = (bf16[1024,768]{1,0:T(8,128)(2,1)}, bf16[1024,768]{1,0:T(8,128)(2,1)}, u32[]{:S(2)}, u32[]{:S(2)}) collective-permute-start(bf16[1024,768]{1,0:T(8,128)(2,1)} %bitcast.12), channel_id=1, source_target_pairs={{8,0},{16,8},{24,16},{32,24},{40,32},{48,40},{56,48},{64,56},{72,6... | collective-permute-start | bytes 4718600 | tf_op jit(solution)/shard_map/ppermute | solution.py:365

commit v4 on v3

--- a/solution.py
+++ b/solution.py
@@ -13,7 +13,8 @@
 BF = 8
 FT = BF * BLOCK
 HEADS_LOCAL = 3
-GROUP = 2
+GROUP = 4
+TEAM = 4
 PACK_STEPS = 4
 SELECT_STEPS = 2
 PARAMS = pltpu.CompilerParams(vmem_limit_bytes=24 << 20)
@@ -94,14 +95,13 @@
 def gather_kernel(me_ref, lead_ref, *refs):
     parts, (mixed_ref, pairs_ref) = refs[:-2], refs[-2:]
     peers = len(parts)
-    split = pairs_ref.shape[2] - 2 * HDIM
+    split = pairs_ref.shape[2]
     mixed_ref[:, :, : 2 * HDIM] = lead_ref[...]
-    pairs_ref[:, :, : 2 * HDIM] = lead_ref[...]
     for d, ref in enumerate(parts):
         block = lax.rem(me_ref[0] - d + peers, peers)
         part = ref[...]
         mixed_ref[block, :, 2 * HDIM :] = part
-        pairs_ref[block, :, 2 * HDIM :] = part[:, :split]
+        pairs_ref[block] = part[:, :split]
 
 
 def assemble(me, lead, parts):
@@ -118,12 +118,12 @@
             + [pl.BlockSpec((tile, size), lambda i, m: (i, 0))] * peers,
             out_specs=[
                 pl.BlockSpec((peers, tile, 3 * local), lambda i, m: (0, i, 0)),
-                pl.BlockSpec((peers, tile, 2 * local), lambda i, m: (0, i, 0)),
+                pl.BlockSpec((peers, tile, 2 * local - 2 * HDIM), lambda i, m: (0, i, 0)),
             ],
         ),
         out_shape=[
             pltpu.HBM((peers, rows, 3 * local), lead.dtype),
-            pltpu.HBM((peers, rows, 2 * local), lead.dtype),
+            pltpu.HBM((peers, rows, 2 * local - 2 * HDIM), lead.dtype),
         ],
         compiler_params=PARAMS,
         name="assemble",
@@ -210,11 +210,12 @@
     l_ref[...] = mass
 
 
-def near_attention(near_on, mixed, before, after):
+def near_attention(near_on, mixed, group, before, after):
     tile = 256
     rows, width = mixed.shape
-    heads = HEADS_LOCAL
-    first = width // HDIM - heads
+    heads = len(group)
+    start = group[0]
+    first = width // HDIM - HEADS_LOCAL + start
     whole = pl.BlockSpec((rows, 2 * HDIM), lambda h, i, on: (0, h))
     return pl.pallas_call(
         near_kernel,
@@ -223,7 +224,7 @@
             grid=(heads, rows // tile),
             in_specs=[
                 pl.BlockSpec((tile, HDIM), lambda h, i, on: (i, first + h)),
-                whole,
+                pl.BlockSpec((rows, 2 * HDIM), lambda h, i, on: (0, start + h)),
                 whole,
                 whole,
             ],
@@ -240,65 +241,73 @@
     )(near_on, mixed, mixed, before, after)
 
 
-def far_kernel(list_ref, count_ref, q_ref, kv_ref, o_ref, m_ref, l_ref, *refs):
+def far_kernel(list_ref, rank_ref, count_ref, q_ref, kv_ref, o_ref, m_ref, l_ref, *refs):
     out_ref, m_s, l_s, acc_s = refs[-4:]
     m_s[...] = m_ref[...]
     l_s[...] = l_ref[...]
     acc_s[...] = o_ref[...]
     blocks = q_ref.shape[0] // BLOCK
-    most = count_ref[0]
-    for qb in range(1, blocks):
-        most = jnp.maximum(most, count_ref[qb])
-
-    def step(t, carry):
-        for qb in range(blocks):
-            rows = slice(qb * BLOCK, (qb + 1) * BLOCK)
-            query = q_ref[rows, :]
+
+    def step(lead, t, carry):
+        units = []
+        for s in range(lead, lead + TEAM):
+            qb = rank_ref[s]
+            rows = pl.ds(pl.multiple_of(qb * BLOCK, BLOCK), BLOCK)
             frames = [list_ref[qb, t * GROUP + i] for i in range(GROUP)]
             keys = jnp.concatenate([kv_ref[f, :, :HDIM] for f in frames], axis=0)
-            values = jnp.concatenate([kv_ref[f, :, HDIM:] for f in frames], axis=0)
-            raw = dot(query, keys, NT)
+            raw = dot(q_ref[rows, :], keys, NT)
+            units.append((qb, rows, frames, raw, m_s[rows, :], l_s[rows, :], acc_s[rows, :]))
+        soft = []
+        for qb, rows, frames, raw, old, mass, acc in units:
             scores = []
             for i in range(GROUP):
                 bias = jnp.where(t * GROUP + i < count_ref[qb], 0.0, NEG)
                 scores.append(raw[:, i * BLOCK : (i + 1) * BLOCK] + bias)
-            old = m_s[rows, :]
             peak = functools.reduce(jnp.maximum, scores)
             top = jnp.maximum(old, jnp.max(peak, axis=1, keepdims=True))
             fade = jnp.exp2((old - top) * SCALE2)
             weights = [jnp.exp2((s - top) * SCALE2) for s in scores]
             rounded = jnp.concatenate([w.astype(jnp.bfloat16) for w in weights], axis=1)
+            mass = mass * fade + functools.reduce(jnp.add, weights)
+            soft.append((rows, frames, top, mass, acc * fade, rounded))
+        done = []
+        for rows, frames, top, mass, acc, rounded in soft:
+            values = jnp.concatenate([kv_ref[f, :, HDIM:] for f in frames], axis=0)
+            done.append((rows, top, mass, acc + dot(rounded, values, NN)))
+        for rows, top, mass, acc in done:
             m_s[rows, :] = top
-            l_s[rows, :] = l_s[rows, :] * fade + functools.reduce(jnp.add, weights)
-            acc_s[rows, :] = acc_s[rows, :] * fade + dot(rounded, values, NN)
+            l_s[rows, :] = mass
+            acc_s[rows, :] = acc
         return carry
 
-    lax.fori_loop(0, (most + GROUP - 1) // GROUP, step, 0)
+    for lead in range(0, blocks, TEAM):
+        trips = (count_ref[rank_ref[lead]] + GROUP - 1) // GROUP
+        lax.fori_loop(0, trips, functools.partial(step, lead), 0)
     total = jnp.sum(l_s[...], axis=1, keepdims=True)
     out_ref[...] = (acc_s[...] / total).astype(out_ref.dtype)
 
 
-def far_attention(order, counts, mixed, heads, far, near, result):
+def far_attention(tables, mixed, heads, far, near, result):
     rows, width = mixed.shape
     column = width // HDIM - HEADS_LOCAL + heads[0]
     first = heads[0]
     frames = far.shape[0]
-    full = pl.BlockSpec((rows, HDIM), lambda g, a, b: (0, first + g))
-    operands = [order, counts, mixed, far, *in_hbm(*near)] + ([] if result is None else [result])
+    full = pl.BlockSpec((rows, HDIM), lambda g, a, b, c: (0, g))
+    operands = [*tables, mixed, far, *in_hbm(*near)] + ([] if result is None else [result])
     return pl.pallas_call(
         far_kernel,
         grid_spec=pltpu.PrefetchScalarGridSpec(
-            num_scalar_prefetch=2,
+            num_scalar_prefetch=3,
             grid=(len(heads),),
             in_specs=[
-                pl.BlockSpec((rows, HDIM), lambda g, a, b: (0, column + g)),
-                pl.BlockSpec((frames, BLOCK, 2 * HDIM), lambda g, a, b: (0, 0, g)),
+                pl.BlockSpec((rows, HDIM), lambda g, a, b, c: (0, column + g)),
+                pl.BlockSpec((frames, BLOCK, 2 * HDIM), lambda g, a, b, c: (0, 0, g)),
                 full,
                 full,
                 full,
             ]
             + ([] if result is None else [pl.BlockSpec(memory_space=pl.ANY)]),
-            out_specs=full,
+            out_specs=pl.BlockSpec((rows, HDIM), lambda g, a, b, c: (0, first + g)),
             scratch_shapes=[
                 pltpu.VMEM((rows, HDIM), jnp.float32),
                 pltpu.VMEM((rows, HDIM), jnp.float32),
@@ -306,7 +315,7 @@
             ],
         ),
         out_shape=pltpu.HBM((rows, HEADS_LOCAL * HDIM), mixed.dtype),
-        input_output_aliases={} if result is None else {7: 0},
+        input_output_aliases={} if result is None else {8: 0},
         cost_estimate=pl.CostEstimate(
             flops=len(heads) * rows * frames * BLOCK * HDIM,
             bytes_accessed=len(heads) * frames * BLOCK * 2 * HDIM * 2,
@@ -335,7 +344,13 @@
     slots = jnp.where(active > 0, place - 1, -1)
     hit = (slots[:, :, None] == frame_ids[None, None, :]).astype(jnp.int32)
     order = jnp.sum(hit * frame_ids[None, :, None], axis=1)
-    return outgoing, near_on, order, counts
+    ids = block_ids
+    ahead = (counts[None, :] > counts[:, None]) | (
+        (counts[None, :] == counts[:, None]) & (ids[None, :] < ids[:, None])
+    )
+    seat = jnp.sum(ahead.astype(jnp.int32), axis=1)
+    rank = jnp.sum((seat[:, None] == ids[None, :]).astype(jnp.int32) * ids[:, None], axis=0)
+    return outgoing, near_on, (order, rank, counts)
 
 
 def body(queries, key_rows, value_rows, block_mask):
@@ -347,9 +362,12 @@
     up = [(i, i + 1) for i in range(frame_count - 1)]
     down = [(j, i) for i, j in up]
     early, late = [0], list(range(1, HEADS_LOCAL))
-    outgoing, near_on, order, counts = mask_tables(block_mask, frame_id, frame_count)
+    outgoing, near_on, tables = mask_tables(block_mask, frame_id, frame_count)
     lead = exchange(pack_lead(key_rows, value_rows, peers), "head")
     parts = pack_rest(me, queries, key_rows, value_rows, peers)
+    flat = lead.reshape(FT, lead.shape[2])
+    before_early = lax.ppermute(flat, "frame", up)
+    after_early = lax.ppermute(flat, "frame", down)
     parcel = select_blocks(outgoing, lead, early)
     far_early = exchange(parcel, "frame")
     moved = [parts[0]]
@@ -361,11 +379,12 @@
     pairs = pairs.reshape(FT, pairs.shape[2])
     parcel = select_blocks(outgoing, blocks, late)
     far_late = exchange(parcel, "frame")
-    before = lax.ppermute(pairs, "frame", up)
-    after = lax.ppermute(pairs, "frame", down)
-    near = near_attention(near_on, mixed, before, after)
-    result = far_attention(order, counts, mixed, early, far_early, near, None)
-    result = far_attention(order, counts, mixed, late, far_late, near, result)
+    before_late = lax.ppermute(pairs, "frame", up)
+    after_late = lax.ppermute(pairs, "frame", down)
+    near_early = near_attention(near_on, mixed, early, before_early, after_early)
+    near_late = near_attention(near_on, mixed, late, before_late, after_late)
+    result = far_attention(tables, mixed, early, far_early, near_early, None)
+    result = far_attention(tables, mixed, late, far_late, near_late, result)
     result = result.reshape(peers, BLOCK, HEADS_LOCAL * HDIM)
     return unpack(exchange(result, "head"))
 

time: 267 us -> 263 us (0.985)
  starting transfers between devices: 56.7 us -> 64.7 us
  waiting for transfers between devices: 133 us -> 125 us
  Pallas kernels: 55.9 us -> 52.4 us
    ppermute x2 -> x4, waiting for transfers between devices: 102 us -> 93.7 us  [the longest x1 93.7 us: body(): before_early = lax.ppermute(flat, 'frame', up)]
    ppermute x2 -> x4, starting transfers between devices: 7.97 us -> 15.9 us  [the longest x1 6.05 us: body(): after_early = lax.ppermute(flat, 'frame', down)]
    pallas_call x2, Pallas kernels: 20.7 us -> 17.1 us  [far_attention(): pl.pallas_call(far_kernel, grid_spec=pltpu.PrefetchScalarGridSpec(num_sca...]
    pallas_call x1 -> x2, Pallas kernels: 19 us -> 19.3 us  [near_attention(): pl.pallas_call(near_kernel, grid_spec=pltpu.PrefetchScalarGridSpec(num_sc...]
  transfers between devices with their start and end apart: 12 -> 14, of which waited for: 5 -> 5; matrix products, arithmetic and copies ran while one was open for 0% -> 1% of each run, Pallas kernels for 14% -> 13%
where the time goes in v4:
time: 263 us; the launch traced here: 261 us
  waiting for transfers between devices  125 us (48%)
  starting transfers between devices  64.7 us (25%)
  Pallas kernels  52.4 us (20%)
  blocking collectives  14.8 us (6%)
  local copies, waits for them, and re-layouts  2.88 us (1%)
    ppermute x1, waiting for transfers between devices, body(): before_early = lax.ppermute(flat, 'frame', up)  93.7 us
    ppermute x7, waiting for transfers between devices, body(): moved.append(lax.ppermute(parts[d], 'head', turn))  22 us
    ppermute x7, starting transfers between devices, body(): moved.append(lax.ppermute(parts[d], 'head', turn))  19.3 us
    pallas_call x2, Pallas kernels, near_attention(): pl.pallas_call(near_kernel, grid_spec=pltpu.PrefetchScalarGridSpec(num_sc...  19.3 us
    pallas_call x2, Pallas kernels, far_attention(): pl.pallas_call(far_kernel, grid_spec=pltpu.PrefetchScalarGridSpec(num_sca...  17.1 us
    all_to_all x1, blocking collectives, body(): return unpack(exchange(result, 'head'))  14.8 us
    all_to_all x1, starting transfers between devices, body(): far_late = exchange(parcel, 'frame')  13 us
    all_to_all x1, starting transfers between devices, body(): far_early = exchange(parcel, 'frame')  11.1 us
  transfers between devices with their start and end apart: 14, of which 5 were waited for; matrix products, arithmetic and copies ran while one was open for 1% of the time, Pallas kernels for 13%

profile of v4, /device:TPU:32, one launch (start us, length us, event | category | flops | bytes accessed | tf_op | source)
XLA Modules:
  0.0 261.0 jit_solution(14729675282042828941)
XLA Ops:
  0.0 3.5 %lead.1 = bf16[8,128,256]{2,1,0:T(8,128)(2,1)} custom-call(bf16[128,3072]{1,0:T(8,128)(2,1)} %k_ref.3, bf16[128,3072]{1,0:T(8,128)(2,1)} %v_ref.3), custom_call_target="tpu_custom_call" | custom-call | tf_op jit(solution)/shard_map/lead/pallas_call | solution.py:47
  3.5 5.3 %all-to-all-start = ((bf16[8,128,256]{2,1,0:T(8,128)(2,1)}), bf16[8,128,256]{2,1,0:T(8,128)(2,1)S(1)}, u32[]{:S(2)}, u32[]{:S(2)}) async-start(bf16[8,128,256]{2,1,0:T(8,128)(2,1)} %lead.1), calls=%async_computation | async-start | bytes 1048576 | tf_op jit(solution)/shard_map/all_to_all | solution.py:366
  8.8 0.1 bitcast_reduce_fusion
  8.9 0.1 multiply_reduce_fusion.1
  9.1 9.2 %all-to-all-done.lead_ref.refs_0_ = bf16[8,128,256]{2,1,0:T(8,128)(2,1)S(1)} async-done(((bf16[8,128,256]{2,1,0:T(8,128)(2,1)}), bf16[8,128,256]{2,1,0:T(8,128)(2,1)S(1)}, u32[]{:S(2)}, u32[]{:S(2)}) %all-to-all-start) | async-done | bytes 524320 | tf_op jit(solution)/shard_map/all_to_all | solution.py:366
  18.3 1.9 select.6
  20.2 11.1 %all-to-all-start.2 = ((bf16[32,128,256]{2,1,0:T(8,128)(2,1)}), bf16[32,128,256]{2,1,0:T(8,128)(2,1)}, u32[]{:S(2)}, u32[]{:S(2)}) async-start(bf16[32,128,256]{2,1,0:T(8,128)(2,1)} %select.6), calls=%async_computation.2 | async-start | bytes 4194304 | tf_op jit(solution)/shard_map/all_to_all | solution.py:372
  31.3 4.0 %rest.1 = (bf16[128,896]{1,0:T(8,128)(2,1)}, bf16[128,896]{1,0:T(8,128)(2,1)}, bf16[128,896]{1,0:T(8,128)(2,1)}, bf16[128,896]{1,0:T(8,128)(2,1)}, bf16[128,896]...) custom-call(s32[1]{0:T(128)} %bitcast.me_ref, ...), custom_call_target="tpu_custom_call" | custom-call | tf_op jit(solution)/shard_map/rest/pallas_call | solution.py:81
  35.3 0.9 collective-permute-start
  36.2 0.6 collective-permute-start.1
  36.8 2.1 collective-permute-start.2
  38.9 2.8 %collective-permute-start.3 = (bf16[128,896]{1,0:T(8,128)(2,1)}, bf16[128,896]{1,0:T(8,128)(2,1)S(1)}, u32[]{:S(2)}, u32[]{:S(2)}) collective-permute-start(bf16[128,896]{1,0:T(8,128)(2,1)} %get-tuple-element.25), channel_id=1, source_target_pairs={{0,4},{1,5},{2,6},{3,7},{4,0},{5,1},{6,2},{7,3},{8,12},{9,13},{10,... | collective-permute-start | bytes 688136 | tf_op jit(solution)/shard_map/ppermute | solution.py:376
  41.6 1.7 collective-permute-start.4
  43.3 11.7 %collective-permute-done.refs_1_ = bf16[128,896]{1,0:T(8,128)(2,1)S(1)} collective-permute-done((bf16[128,896]{1,0:T(8,128)(2,1)}, bf16[128,896]{1,0:T(8,128)(2,1)S(1)}, u32[]{:S(2)}, u32[]{:S(2)}) %collective-permute-start) | collective-permute-done | bytes 229408 | tf_op jit(solution)/shard_map/ppermute | solution.py:376
  55.0 8.4 %collective-permute-start.5 = (bf16[128,896]{1,0:T(8,128)(2,1)}, bf16[128,896]{1,0:T(8,128)(2,1)S(1)}, u32[]{:S(2)}, u32[]{:S(2)}) collective-permute-start(bf16[128,896]{1,0:T(8,128)(2,1)} %get-tuple-element.27), channel_id=1, source_target_pairs={{0,6},{1,7},{2,0},{3,1},{4,2},{5,3},{6,4},{7,5},{8,14},{9,15},{10,... | collective-permute-start | bytes 688136 | tf_op jit(solution)/shard_map/ppermute | solution.py:376
  63.4 0.0 collective-permute-done.1.refs_2_
  63.4 2.9 %collective-permute-start.6 = (bf16[128,896]{1,0:T(8,128)(2,1)}, bf16[128,896]{1,0:T(8,128)(2,1)S(1)}, u32[]{:S(2)}, u32[]{:S(2)}) collective-permute-start(bf16[128,896]{1,0:T(8,128)(2,1)} %get-tuple-element.28), channel_id=1, source_target_pairs={{0,7},{1,0},{2,1},{3,2},{4,3},{5,4},{6,5},{7,6},{8,15},{9,8},{10,9... | collective-permute-start | bytes 688136 | tf_op jit(solution)/shard_map/ppermute | solution.py:376
  66.3 0.0 collective-permute-done.2.refs_3_
  66.3 3.4 %collective-permute-done.5.refs_6_ = bf16[128,896]{1,0:T(8,128)(2,1)S(1)} collective-permute-done((bf16[128,896]{1,0:T(8,128)(2,1)}, bf16[128,896]{1,0:T(8,128)(2,1)S(1)}, u32[]{:S(2)}, u32[]{:S(2)}) %collective-permute-start.5) | collective-permute-done | bytes 229408 | tf_op jit(solution)/shard_map/ppermute | solution.py:376
  69.7 7.0 %collective-permute-done.6.refs_7_ = bf16[128,896]{1,0:T(8,128)(2,1)S(1)} collective-permute-done((bf16[128,896]{1,0:T(8,128)(2,1)}, bf16[128,896]{1,0:T(8,128)(2,1)S(1)}, u32[]{:S(2)}, u32[]{:S(2)}) %collective-permute-start.6) | collective-permute-done | bytes 229408 | tf_op jit(solution)/shard_map/ppermute | solution.py:376
  76.7 0.9 copy-done.3
  77.6 2.3 assemble.1
  80.0 1.7 copy-done.1
  81.6 2.7 %select.5 = bf16[32,128,512]{2,1,0:T(8,128)(2,1)} custom-call(s32[32]{0:T(128)S(1)} %broadcast_minimum_fusion.pick_ref, bf16[8,128,1152]{2,1,0:T(8,128)(2,1)S(1)} %copy-done.1, bf16[8,128,1152]{2,1,0:T(8,128)(2,1)S(1)} %copy-done.1), custom_call_target="tpu_custom_call" | custom-call | tf_op jit(solution)/shard_map/select/pallas_call | solution.py:166
  84.3 0.0 all-to-all-done.2.kv_ref
  84.3 13.0 %all-to-all-start.1 = ((bf16[32,128,512]{2,1,0:T(8,128)(2,1)}), bf16[32,128,512]{2,1,0:T(8,128)(2,1)}, u32[]{:S(2)}, u32[]{:S(2)}) async-start(bf16[32,128,512]{2,1,0:T(8,128)(2,1)} %select.5), calls=%async_computation.1 | async-start | bytes 8388608 | tf_op jit(solution)/shard_map/all_to_all | solution.py:381
  97.4 0.1 reshape.78
  97.5 0.2 reduce_max.18
  97.7 0.1 fusion.3
  97.8 0.2 convert_reduce_fusion
  98.0 0.1 select_reduce_fusion.1.rank_ref
  98.1 2.0 collective-permute-start.7
  100.1 5.9 %collective-permute-start.8 = (bf16[1024,512]{1,0:T(8,128)(2,1)}, bf16[1024,512]{1,0:T(8,128)(2,1)S(1)}, u32[]{:S(2)}, u32[]{:S(2)}) collective-permute-start(bf16[1024,512]{1,0:T(8,128)(2,1)} %bitcast.17), channel_id=1, source_target_pairs={{8,0},{16,8},{24,16},{32,24},{40,32},{48,40},{56,48},{64,56},{72,6... | collective-permute-start | bytes 3145736 | tf_op jit(solution)/shard_map/ppermute | solution.py:383
  106.1 0.1 pad_dynamic-slice_fusion
  106.1 0.1 fusion.4
  106.2 1.9 collective-permute-start.9
  108.1 6.0 %collective-permute-start.10 = (bf16[1024,256]{1,0:T(8,128)(2,1)S(1)}, bf16[1024,256]{1,0:T(8,128)(2,1)S(1)}, u32[]{:S(2)}, u32[]{:S(2)}) collective-permute-start(bf16[1024,256]{1,0:T(8,128)(2,1)S(1)} %bitcast.14), channel_id=1, source_target_pairs={{8,0},{16,8},{24,16},{32,24},{40,32},{48,40},{56,48},{64,56},{72,6... | collective-permute-start | bytes 1572872 | tf_op jit(solution)/shard_map/ppermute | solution.py:370
  114.2 0.1 pad_add_fusion.on_ref
  114.3 0.1 multiply_reduce_fusion
  114.4 0.1 select_reduce_fusion.list_ref
  114.5 93.7 %collective-permute-done.9.before_ref = bf16[1024,256]{1,0:T(8,128)(2,1)S(1)} collective-permute-done((bf16[1024,256]{1,0:T(8,128)(2,1)S(1)}, bf16[1024,256]{1,0:T(8,128)(2,1)S(1)}, u32[]{:S(2)}, u32[]{:S(2)}) %collective-permute-start.9) | collective-permute-done | bytes 524320 | tf_op jit(solution)/shard_map/ppermute | solution.py:369
  208.2 0.0 collective-permute-done.10.after_ref
  208.2 6.7 %near.3 = (f32[1024,128]{1,0:T(8,128)}, f32[1024,128]{1,0:T(8,128)}, f32[1024,128]{1,0:T(8,128)}) custom-call(s32[8,16]{1,0:T(8,128)S(1)} %pad_add_fusion.on_ref, bf16[1024,1152]{1,0:T(8,128)(2,1)S(1)} %bitcast.7, bf16[1024,1152]{1,0:T(8,128)(2,1)S(1)} %bitcast.8, bf16[1024,256]{1,0:T(8,128)(2,1)S(1)} %collective-permute-done.9.before_ref, ...), custom_call_target="tpu_custom_call" | custom-call | flops 1610612736 | bytes 2097152 | tf_op jit(solution)/shard_map/near/pallas_call | solution.py:220
  215.0 12.5 %near.2 = (f32[1024,256]{1,0:T(8,128)}, f32[1024,256]{1,0:T(8,128)}, f32[1024,256]{1,0:T(8,128)}) custom-call(s32[8,16]{1,0:T(8,128)S(1)} %pad_add_fusion.on_ref, bf16[1024,1152]{1,0:T(8,128)(2,1)S(1)} %bitcast.9, bf16[1024,1152]{1,0:T(8,128)(2,1)S(1)} %bitcast.10, bf16[1024,512]{1,0:T(8,128)(2,1)S(1)} %collective-permute-done.7.before_ref, ...), custom_call_target="tpu_custom_call" | custom-call | flops 3221225472 | bytes 4194304 | tf_op jit(solution)/shard_map/near/pallas_call | solution.py:220
  227.5 6.9 %far.2.refs_0_ = bf16[1024,384]{1,0:T(8,128)(2,1)} custom-call(s32[8,32]{1,0:T(8,128)S(1)} %select_reduce_fusion.list_ref, s32[8]{0:T(128)S(1)} %select_reduce_fusion.1.rank_ref, s32[8]{0:T(128)S(1)} %get-tuple-element.37.count_ref, bf16[1024,1152]{1,0:T(8,128)(2,1)S(1)} %bitcast.11, bf16[32,128,256]{2,1,0:T(8,128)(2,1)} %all-to-all-done.2.kv_ref, ...), custom_call_target="tpu_custom_call" | custom-call | flops 536870912 | bytes 2097152 | tf_op jit(solution)/shard_map/far/pallas_call | solution.py:297
  234.4 10.2 %far.3 = bf16[1024,384]{1,0:T(8,128)(2,1)} custom-call(s32[8,32]{1,0:T(8,128)S(1)} %select_reduce_fusion.list_ref, s32[8]{0:T(128)S(1)} %select_reduce_fusion.1.rank_ref, s32[8]{0:T(128)S(1)} %get-tuple-element.37.count_ref, bf16[1024,1152]{1,0:T(8,128)(2,1)S(1)} %bitcast.12, ...), custom_call_target="tpu_custom_call", output_to_operand_aliasing={{}: (8, {})} | custom-call | flops 1073741824 | bytes 4194304 | tf_op jit(solution)/shard_map/far/pallas_call | solution.py:297
  244.6 14.8 %all_to_all.20.part_ref = bf16[8,128,384]{2,1,0:T(8,128)(2,1)S(1)} all-to-all(bf16[8,128,384]{2,1,0:T(8,128)(2,1)} %bitcast.15), channel_id=1, replica_groups=mesh['frame'=32,'head'=8] {'head'}, dimensions={0} | all-to-all | bytes 1572864 | tf_op jit(solution)/shard_map/all_to_all | solution.py:389
  259.5 1.5 unpack.1
  (16 shorter events, 0.1 us)
Async XLA Ops:
  0.0 8.8 %copy-start = (s32[256,256]{1,0:T(8,128)S(1)}, s32[256,256]{1,0:T(8,128)}, u32[]{:S(2)}) copy-start(s32[256,256]{1,0:T(8,128)} %param.7) | copy-start | bytes 786436
  3.5 14.8 %all-to-all-start = ((bf16[8,128,256]{2,1,0:T(8,128)(2,1)}), bf16[8,128,256]{2,1,0:T(8,128)(2,1)S(1)}, u32[]{:S(2)}, u32[]{:S(2)}) async-start(bf16[8,128,256]{2,1,0:T(8,128)(2,1)} %lead.1), calls=%async_computation | async-start | bytes 1048576 | tf_op jit(solution)/shard_map/all_to_all | solution.py:366
  20.2 64.1 %all-to-all-start.2 = ((bf16[32,128,256]{2,1,0:T(8,128)(2,1)}), bf16[32,128,256]{2,1,0:T(8,128)(2,1)}, u32[]{:S(2)}, u32[]{:S(2)}) async-start(bf16[32,128,256]{2,1,0:T(8,128)(2,1)} %select.6), calls=%async_computation.2 | async-start | bytes 4194304 | tf_op jit(solution)/shard_map/all_to_all | solution.py:372
  35.3 19.6 %collective-permute-start = (bf16[128,896]{1,0:T(8,128)(2,1)}, bf16[128,896]{1,0:T(8,128)(2,1)S(1)}, u32[]{:S(2)}, u32[]{:S(2)}) collective-permute-start(bf16[128,896]{1,0:T(8,128)(2,1)} %get-tuple-element.22), channel_id=1, source_target_pairs={{0,1},{1,2},{2,3},{3,4},{4,5},{5,6},{6,7},{7,0},{8,9},{9,10},{10,1... | collective-permute-start | bytes 688136 | tf_op jit(solution)/shard_map/ppermute | solution.py:376
  36.2 27.2 %collective-permute-start.1 = (bf16[128,896]{1,0:T(8,128)(2,1)}, bf16[128,896]{1,0:T(8,128)(2,1)S(1)}, u32[]{:S(2)}, u32[]{:S(2)}) collective-permute-start(bf16[128,896]{1,0:T(8,128)(2,1)} %get-tuple-element.23), channel_id=1, source_target_pairs={{0,2},{1,3},{2,4},{3,5},{4,6},{5,7},{6,0},{7,1},{8,10},{9,11},{10,... | collective-permute-start | bytes 688136 | tf_op jit(solution)/shard_map/ppermute | solution.py:376
  36.8 29.5 %collective-permute-start.2 = (bf16[128,896]{1,0:T(8,128)(2,1)}, bf16[128,896]{1,0:T(8,128)(2,1)S(1)}, u32[]{:S(2)}, u32[]{:S(2)}) collective-permute-start(bf16[128,896]{1,0:T(8,128)(2,1)} %get-tuple-element.24), channel_id=1, source_target_pairs={{0,3},{1,4},{2,5},{3,6},{4,7},{5,0},{6,1},{7,2},{8,11},{9,12},{10,... | collective-permute-start | bytes 688136 | tf_op jit(solution)/shard_map/ppermute | solution.py:376
  38.9 27.4 %collective-permute-start.3 = (bf16[128,896]{1,0:T(8,128)(2,1)}, bf16[128,896]{1,0:T(8,128)(2,1)S(1)}, u32[]{:S(2)}, u32[]{:S(2)}) collective-permute-start(bf16[128,896]{1,0:T(8,128)(2,1)} %get-tuple-element.25), channel_id=1, source_target_pairs={{0,4},{1,5},{2,6},{3,7},{4,0},{5,1},{6,2},{7,3},{8,12},{9,13},{10,... | collective-permute-start | bytes 688136 | tf_op jit(solution)/shard_map/ppermute | solution.py:376
  41.6 24.7 %collective-permute-start.4 = (bf16[128,896]{1,0:T(8,128)(2,1)}, bf16[128,896]{1,0:T(8,128)(2,1)S(1)}, u32[]{:S(2)}, u32[]{:S(2)}) collective-permute-start(bf16[128,896]{1,0:T(8,128)(2,1)} %get-tuple-element.26), channel_id=1, source_target_pairs={{0,5},{1,6},{2,7},{3,0},{4,1},{5,2},{6,3},{7,4},{8,13},{9,14},{10,... | collective-permute-start | bytes 688136 | tf_op jit(solution)/shard_map/ppermute | solution.py:376
  55.0 14.8 %collective-permute-start.5 = (bf16[128,896]{1,0:T(8,128)(2,1)}, bf16[128,896]{1,0:T(8,128)(2,1)S(1)}, u32[]{:S(2)}, u32[]{:S(2)}) collective-permute-start(bf16[128,896]{1,0:T(8,128)(2,1)} %get-tuple-element.27), channel_id=1, source_target_pairs={{0,6},{1,7},{2,0},{3,1},{4,2},{5,3},{6,4},{7,5},{8,14},{9,15},{10,... | collective-permute-start | bytes 688136 | tf_op jit(solution)/shard_map/ppermute | solution.py:376
  63.4 13.3 %collective-permute-start.6 = (bf16[128,896]{1,0:T(8,128)(2,1)}, bf16[128,896]{1,0:T(8,128)(2,1)S(1)}, u32[]{:S(2)}, u32[]{:S(2)}) collective-permute-start(bf16[128,896]{1,0:T(8,128)(2,1)} %get-tuple-element.28), channel_id=1, source_target_pairs={{0,7},{1,0},{2,1},{3,2},{4,3},{5,4},{6,5},{7,6},{8,15},{9,8},{10,9... | collective-permute-start | bytes 688136 | tf_op jit(solution)/shard_map/ppermute | solution.py:376
  76.7 0.9 copy-start.3
  80.0 1.7 copy-start.1
  84.3 123.9 %copy-start.2 = (bf16[8,128,1152]{2,1,0:T(8,128)(2,1)S(1)}, bf16[8,128,1152]{2,1,0:T(8,128)(2,1)}, u32[]{:S(2)}) copy-start(bf16[8,128,1152]{2,1,0:T(8,128)(2,1)} %get-tuple-element.29.refs_0_.refs_1_) | copy-start | bytes 7077892
  84.3 150.1 %all-to-all-start.1 = ((bf16[32,128,512]{2,1,0:T(8,128)(2,1)}), bf16[32,128,512]{2,1,0:T(8,128)(2,1)}, u32[]{:S(2)}, u32[]{:S(2)}) async-start(bf16[32,128,512]{2,1,0:T(8,128)(2,1)} %select.5), calls=%async_computation.1 | async-start | bytes 8388608 | tf_op jit(solution)/shard_map/all_to_all | solution.py:381
  98.1 116.9 %collective-permute-start.7 = (bf16[1024,512]{1,0:T(8,128)(2,1)}, bf16[1024,512]{1,0:T(8,128)(2,1)S(1)}, u32[]{:S(2)}, u32[]{:S(2)}) collective-permute-start(bf16[1024,512]{1,0:T(8,128)(2,1)} %bitcast.16), channel_id=1, source_target_pairs={{0,8},{8,16},{16,24},{24,32},{32,40},{40,48},{48,56},{56,64},{64,7... | collective-permute-start | bytes 3145736 | tf_op jit(solution)/shard_map/ppermute | solution.py:382
  100.1 114.8 %collective-permute-start.8 = (bf16[1024,512]{1,0:T(8,128)(2,1)}, bf16[1024,512]{1,0:T(8,128)(2,1)S(1)}, u32[]{:S(2)}, u32[]{:S(2)}) collective-permute-start(bf16[1024,512]{1,0:T(8,128)(2,1)} %bitcast.17), channel_id=1, source_target_pairs={{8,0},{16,8},{24,16},{32,24},{40,32},{48,40},{56,48},{64,56},{72,6... | collective-permute-start | bytes 3145736 | tf_op jit(solution)/shard_map/ppermute | solution.py:383
  106.2 102.0 %collective-permute-start.9 = (bf16[1024,256]{1,0:T(8,128)(2,1)S(1)}, bf16[1024,256]{1,0:T(8,128)(2,1)S(1)}, u32[]{:S(2)}, u32[]{:S(2)}) collective-permute-start(bf16[1024,256]{1,0:T(8,128)(2,1)S(1)} %bitcast.13), channel_id=1, source_target_pairs={{0,8},{8,16},{16,24},{24,32},{32,40},{40,48},{48,56},{56,64},{64,7... | collective-permute-start | bytes 1572872 | tf_op jit(solution)/shard_map/ppermute | solution.py:369
  108.1 100.1 %collective-permute-start.10 = (bf16[1024,256]{1,0:T(8,128)(2,1)S(1)}, bf16[1024,256]{1,0:T(8,128)(2,1)S(1)}, u32[]{:S(2)}, u32[]{:S(2)}) collective-permute-start(bf16[1024,256]{1,0:T(8,128)(2,1)S(1)} %bitcast.14), channel_id=1, source_target_pairs={{8,0},{16,8},{24,16},{32,24},{40,32},{48,40},{56,48},{64,56},{72,6... | collective-permute-start | bytes 1572872 | tf_op jit(solution)/shard_map/ppermute | solution.py:370

commit v5 on v4

--- a/solution.py
+++ b/solution.py
@@ -16,6 +16,8 @@
 GROUP = 4
 TEAM = 4
 PACK_STEPS = 4
+LEAD_STEPS = 2
+JOIN_STEPS = 2
 SELECT_STEPS = 2
 PARAMS = pltpu.CompilerParams(vmem_limit_bytes=24 << 20)
 NEG = -1e30
@@ -32,102 +34,92 @@
     return lax.dot_general(a, b, dims, preferred_element_type=jnp.float32)
 
 
-def lead_kernel(k_ref, v_ref, out_ref):
-    peers = out_ref.shape[0]
-    local = k_ref.shape[1] // peers
-    for j in range(peers):
-        out_ref[j, :, :HDIM] = k_ref[:, j * local : j * local + HDIM]
-        out_ref[j, :, HDIM:] = v_ref[:, j * local : j * local + HDIM]
+def lead_kernel(*refs):
+    out_ref = refs[-1]
+    group = out_ref.shape[0]
+    for j in range(group):
+        out_ref[j, :, :HDIM] = refs[j][...]
+        out_ref[j, :, HDIM:] = refs[group + j][...]
 
 
 def pack_lead(keys, values, peers):
     rows, width = keys.shape
-    tile = rows // PACK_STEPS
-    spec = pl.BlockSpec((tile, width), lambda i: (i, 0))
+    stride = width // peers // HDIM
+    group = peers // LEAD_STEPS
+    specs = [
+        pl.BlockSpec((rows, HDIM), lambda i, j=j: (0, (i * group + j) * stride)) for j in range(group)
+    ]
+    keys, values = in_hbm(keys, values)
     return pl.pallas_call(
         lead_kernel,
-        grid=(PACK_STEPS,),
-        in_specs=[spec] * 2,
-        out_specs=pl.BlockSpec((peers, tile, 2 * HDIM), lambda i: (0, i, 0)),
+        grid=(LEAD_STEPS,),
+        in_specs=specs * 2,
+        out_specs=pl.BlockSpec((group, rows, 2 * HDIM), lambda i: (i, 0, 0)),
         out_shape=pltpu.HBM((peers, rows, 2 * HDIM), keys.dtype),
         compiler_params=PARAMS,
         name="lead",
-    )(*in_hbm(keys, values))
+    )(*([keys] * group), *([values] * group))
 
 
 def rest_kernel(me_ref, q_ref, k_ref, v_ref, *out_refs):
-    peers = len(out_refs)
+    peers = len(out_refs) // 2
     local = q_ref.shape[1] // peers
     heads = local // HDIM
-    for d, out_ref in enumerate(out_refs):
+    for d in range(peers):
+        pair_ref, query_ref = out_refs[d], out_refs[peers + d]
         base = lax.rem(me_ref[0] + d, peers) * local
         for h in range(1, heads):
             cols = pl.ds(pl.multiple_of(base + h * HDIM, HDIM), HDIM)
             left = 2 * (h - 1) * HDIM
-            out_ref[:, left : left + HDIM] = k_ref[:, cols]
-            out_ref[:, left + HDIM : left + 2 * HDIM] = v_ref[:, cols]
-        left = 2 * (heads - 1) * HDIM
-        for h in range(heads):
-            cols = pl.ds(pl.multiple_of(base + h * HDIM, HDIM), HDIM)
-            out_ref[:, left + h * HDIM : left + (h + 1) * HDIM] = q_ref[:, cols]
+            pair_ref[:, left : left + HDIM] = k_ref[:, cols]
+            pair_ref[:, left + HDIM : left + 2 * HDIM] = v_ref[:, cols]
+        query_ref[...] = q_ref[:, pl.ds(pl.multiple_of(base, HDIM), local)]
 
 
 def pack_rest(me, queries, keys, values, peers):
     rows, width = queries.shape
     local = width // peers
-    size = 3 * local - 2 * HDIM
     tile = rows // PACK_STEPS
     spec = pl.BlockSpec((tile, width), lambda i, m: (i, 0))
-    return pl.pallas_call(
+    sizes = [2 * local - 2 * HDIM] * peers + [local] * peers
+    outs = pl.pallas_call(
         rest_kernel,
         grid_spec=pltpu.PrefetchScalarGridSpec(
             num_scalar_prefetch=1,
             grid=(PACK_STEPS,),
             in_specs=[spec] * 3,
-            out_specs=[pl.BlockSpec((tile, size), lambda i, m: (i, 0))] * peers,
-        ),
-        out_shape=[pltpu.HBM((rows, size), queries.dtype)] * peers,
+            out_specs=[pl.BlockSpec((tile, size), lambda i, m: (i, 0)) for size in sizes],
+        ),
+        out_shape=[pltpu.HBM((rows, size), queries.dtype) for size in sizes],
         compiler_params=PARAMS,
         name="rest",
     )(me, *in_hbm(queries, keys, values))
-
-
-def gather_kernel(me_ref, lead_ref, *refs):
-    parts, (mixed_ref, pairs_ref) = refs[:-2], refs[-2:]
+    return outs[:peers], outs[peers:]
+
+
+def gather_kernel(me_ref, *refs):
+    out_ref = refs[-1]
+    peers = len(refs) - 1
+    for d, ref in enumerate(refs[:-1]):
+        out_ref[lax.rem(me_ref[0] - d + peers, peers)] = ref[...]
+
+
+def assemble(me, parts):
     peers = len(parts)
-    split = pairs_ref.shape[2]
-    mixed_ref[:, :, : 2 * HDIM] = lead_ref[...]
-    for d, ref in enumerate(parts):
-        block = lax.rem(me_ref[0] - d + peers, peers)
-        part = ref[...]
-        mixed_ref[block, :, 2 * HDIM :] = part
-        pairs_ref[block] = part[:, :split]
-
-
-def assemble(me, lead, parts):
-    peers, rows, _ = lead.shape
-    size = parts[0].shape[1]
-    local = (size + 2 * HDIM) // 3
-    tile = rows // PACK_STEPS
+    rows, size = parts[0].shape
+    tile = rows // JOIN_STEPS
     return pl.pallas_call(
         gather_kernel,
         grid_spec=pltpu.PrefetchScalarGridSpec(
             num_scalar_prefetch=1,
-            grid=(PACK_STEPS,),
-            in_specs=[pl.BlockSpec((peers, tile, 2 * HDIM), lambda i, m: (0, i, 0))]
-            + [pl.BlockSpec((tile, size), lambda i, m: (i, 0))] * peers,
-            out_specs=[
-                pl.BlockSpec((peers, tile, 3 * local), lambda i, m: (0, i, 0)),
-                pl.BlockSpec((peers, tile, 2 * local - 2 * HDIM), lambda i, m: (0, i, 0)),
-            ],
-        ),
-        out_shape=[
-            pltpu.HBM((peers, rows, 3 * local), lead.dtype),
-            pltpu.HBM((peers, rows, 2 * local - 2 * HDIM), lead.dtype),
-        ],
+            grid=(JOIN_STEPS,),
+            in_specs=[pl.BlockSpec((tile, size), lambda i, m: (i, 0))] * peers,
+            out_specs=pl.BlockSpec((peers, tile, size), lambda i, m: (0, i, 0)),
+        ),
+        out_shape=pltpu.HBM((peers, rows, size), parts[0].dtype),
         compiler_params=PARAMS,
         name="assemble",
-    )(me, lead, *parts)
+    )(me, *parts)
 
 
 def unpack_kernel(part_ref, out_ref):
@@ -158,11 +150,11 @@
             out_ref[i, :, 2 * g * HDIM : 2 * (g + 1) * HDIM] = kv_ref[pick_ref[base + i]]
 
 
-def select_blocks(picks, blocks, heads):
+def select_blocks(picks, blocks):
     frames = picks.shape[0]
     step = frames // SELECT_STEPS
-    count, rows, _ = blocks.shape
-    width = 2 * HDIM * len(heads)
+    count, rows, width = blocks.shape
+    heads = range(width // (2 * HDIM))
     return pl.pallas_call(
         select_kernel,
         grid_spec=pltpu.PrefetchScalarGridSpec(
@@ -210,12 +202,11 @@
     l_ref[...] = mass
 
 
-def near_attention(near_on, mixed, group, before, after):
+def near_attention(near_on, query, group, own, before, after):
     tile = 256
-    rows, width = mixed.shape
+    rows = query.shape[0]
     heads = len(group)
-    start = group[0]
-    first = width // HDIM - HEADS_LOCAL + start
+    first = group[0]
     whole = pl.BlockSpec((rows, 2 * HDIM), lambda h, i, on: (0, h))
     return pl.pallas_call(
         near_kernel,
@@ -224,7 +215,7 @@
             grid=(heads, rows // tile),
             in_specs=[
                 pl.BlockSpec((tile, HDIM), lambda h, i, on: (i, first + h)),
-                pl.BlockSpec((rows, 2 * HDIM), lambda h, i, on: (0, start + h)),
+                whole,
                 whole,
                 whole,
             ],
@@ -238,7 +229,7 @@
         ),
         compiler_params=PARAMS,
         name="near",
-    )(near_on, mixed, mixed, before, after)
+    )(near_on, query, own, before, after)
 
 
 def far_kernel(list_ref, rank_ref, count_ref, q_ref, kv_ref, o_ref, m_ref, l_ref, *refs):
@@ -287,20 +278,19 @@
     out_ref[...] = (acc_s[...] / total).astype(out_ref.dtype)
 
 
-def far_attention(tables, mixed, heads, far, near, result):
-    rows, width = mixed.shape
-    column = width // HDIM - HEADS_LOCAL + heads[0]
+def far_attention(tables, query, heads, far, near, result):
+    rows = query.shape[0]
     first = heads[0]
     frames = far.shape[0]
     full = pl.BlockSpec((rows, HDIM), lambda g, a, b, c: (0, g))
-    operands = [*tables, mixed, far, *in_hbm(*near)] + ([] if result is None else [result])
+    operands = [*tables, query, far, *in_hbm(*near)] + ([] if result is None else [result])
     return pl.pallas_call(
         far_kernel,
         grid_spec=pltpu.PrefetchScalarGridSpec(
             num_scalar_prefetch=3,
             grid=(len(heads),),
             in_specs=[
-                pl.BlockSpec((rows, HDIM), lambda g, a, b, c: (0, column + g)),
+                pl.BlockSpec((rows, HDIM), lambda g, a, b, c: (0, first + g)),
                 pl.BlockSpec((frames, BLOCK, 2 * HDIM), lambda g, a, b, c: (0, 0, g)),
                 full,
                 full,
@@ -314,7 +304,7 @@
                 pltpu.VMEM((rows, HDIM), jnp.float32),
             ],
         ),
-        out_shape=pltpu.HBM((rows, HEADS_LOCAL * HDIM), mixed.dtype),
+        out_shape=pltpu.HBM((rows, HEADS_LOCAL * HDIM), query.dtype),
         input_output_aliases={} if result is None else {8: 0},
         cost_estimate=pl.CostEstimate(
             flops=len(heads) * rows * frames * BLOCK * HDIM,
@@ -361,30 +351,35 @@
     exchange = functools.partial(lax.all_to_all, split_axis=0, concat_axis=0, tiled=True)
     up = [(i, i + 1) for i in range(frame_count - 1)]
     down = [(j, i) for i, j in up]
+
+    def turned(parts):
+        moved = [parts[0]]
+        for d in range(1, peers):
+            turn = [(i, (i + d) % peers) for i in range(peers)]
+            moved.append(lax.ppermute(parts[d], "head", turn))
+        return moved
+
     early, late = [0], list(range(1, HEADS_LOCAL))
     outgoing, near_on, tables = mask_tables(block_mask, frame_id, frame_count)
     lead = exchange(pack_lead(key_rows, value_rows, peers), "head")
-    parts = pack_rest(me, queries, key_rows, value_rows, peers)
+    pair_parts, query_parts = pack_rest(me, queries, key_rows, value_rows, peers)
+    parcel = select_blocks(outgoing, lead)
+    far_early = exchange(parcel, "frame")
     flat = lead.reshape(FT, lead.shape[2])
+    pairs = assemble(me, turned(pair_parts))
+    parcel = select_blocks(outgoing, pairs)
+    far_late = exchange(parcel, "frame")
+    pairs = pairs.reshape(FT, pairs.shape[2])
     before_early = lax.ppermute(flat, "frame", up)
     after_early = lax.ppermute(flat, "frame", down)
-    parcel = select_blocks(outgoing, lead, early)
-    far_early = exchange(parcel, "frame")
-    moved = [parts[0]]
-    for d in range(1, peers):
-        turn = [(i, (i + d) % peers) for i in range(peers)]
-        moved.append(lax.ppermute(parts[d], "head", turn))
-    blocks, pairs = assemble(me, lead, moved)
-    mixed = blocks.reshape(FT, blocks.shape[2])
-    pairs = pairs.reshape(FT, pairs.shape[2])
-    parcel = select_blocks(outgoing, blocks, late)
-    far_late = exchange(parcel, "frame")
     before_late = lax.ppermute(pairs, "frame", up)
     after_late = lax.ppermute(pairs, "frame", down)
-    near_early = near_attention(near_on, mixed, early, before_early, after_early)
-    near_late = near_attention(near_on, mixed, late, before_late, after_late)
-    result = far_attention(tables, mixed, early, far_early, near_early, None)
-    result = far_attention(tables, mixed, late, far_late, near_late, result)
+    query = assemble(me, turned(query_parts))
+    query = query.reshape(FT, query.shape[2])
+    near_early = near_attention(near_on, query, early, flat, before_early, after_early)
+    near_late = near_attention(near_on, query, late, pairs, before_late, after_late)
+    result = far_attention(tables, query, early, far_early, near_early, None)
+    result = far_attention(tables, query, late, far_late, near_late, result)
     result = result.reshape(peers, BLOCK, HEADS_LOCAL * HDIM)
     return unpack(exchange(result, "head"))
 

time: 263 us -> 253 us (0.962)
  waiting for transfers between devices: 125 us -> 106 us
  starting transfers between devices: 64.7 us -> 73.2 us
    ppermute x1, waiting for transfers between devices: 93.7 us -> 3.49 us  [body(): before_early = lax.ppermute(flat, 'frame', up)]
    ppermute x1, waiting for transfers between devices: 0.01 us -> 53.8 us  [body(): after_early = lax.ppermute(flat, 'frame', down)]
    ppermute x7 -> x14, starting transfers between devices: 19.3 us -> 36.9 us  [turned(): moved.append(lax.ppermute(parts[d], 'head', turn))]
    all_to_all x1, waiting for transfers between devices: 0.01 us -> 11.8 us  [body(): far_early = exchange(parcel, 'frame')]
    ppermute x7 -> x14, waiting for transfers between devices: 22 us -> 27.4 us  [turned(): moved.append(lax.ppermute(parts[d], 'head', turn))]
    ppermute x1, starting transfers between devices: 6.05 us -> 1.91 us  [body(): after_early = lax.ppermute(flat, 'frame', down)]
    all_to_all x1, starting transfers between devices: 13 us -> 9.5 us  [body(): far_late = exchange(parcel, 'frame')]
  transfers between devices with their start and end apart: 14 -> 21, of which waited for: 5 -> 12; matrix products, arithmetic and copies ran while one was open for 1% -> 1% of each run, Pallas kernels for 13% -> 14%
where the time goes in v5:
time: 253 us; the launch traced here: 252 us
  waiting for transfers between devices  106 us (42%)
  starting transfers between devices  73.2 us (29%)
  Pallas kernels  50.4 us (20%)
  blocking collectives  14.9 us (6%)
  local copies, waits for them, and re-layouts  5.23 us (2%)
    ppermute x1, waiting for transfers between devices, body(): after_early = lax.ppermute(flat, 'frame', down)  53.8 us
    ppermute x14, starting transfers between devices, turned(): moved.append(lax.ppermute(parts[d], 'head', turn))  36.9 us
    ppermute x14, waiting for transfers between devices, turned(): moved.append(lax.ppermute(parts[d], 'head', turn))  27.4 us
    pallas_call x2, Pallas kernels, near_attention(): pl.pallas_call(near_kernel, grid_spec=pltpu.PrefetchScalarGridSpec(num_sc...  19.1 us
    pallas_call x2, Pallas kernels, far_attention(): pl.pallas_call(far_kernel, grid_spec=pltpu.PrefetchScalarGridSpec(num_sca...  16.4 us
    all_to_all x1, blocking collectives, body(): return unpack(exchange(result, 'head'))  14.9 us
    all_to_all x1, waiting for transfers between devices, body(): far_early = exchange(parcel, 'frame')  11.8 us
    all_to_all x1, starting transfers between devices, body(): far_early = exchange(parcel, 'frame')  11.1 us
  transfers between devices with their start and end apart: 21, of which 12 were waited for; matrix products, arithmetic and copies ran while one was open for 1% of the time, Pallas kernels for 14%

profile of v5, /device:TPU:32, one launch (start us, length us, event | category | flops | bytes accessed | tf_op | source)
XLA Modules:
  0.0 251.7 jit_solution(11854184523678102895)
XLA Ops:
  0.0 1.8 lead.1
  1.8 5.3 %all-to-all-start.1 = ((bf16[8,128,256]{2,1,0:T(8,128)(2,1)}), bf16[8,128,256]{2,1,0:T(8,128)(2,1)S(1)}, u32[]{:S(2)}, u32[]{:S(2)}) async-start(bf16[8,128,256]{2,1,0:T(8,128)(2,1)} %lead.1), calls=%async_computation.1 | async-start | bytes 1048576 | tf_op jit(solution)/shard_map/all_to_all | solution.py:364
  7.4 9.2 %all-to-all-done.1.refs_0_ = bf16[8,128,256]{2,1,0:T(8,128)(2,1)S(1)} async-done(((bf16[8,128,256]{2,1,0:T(8,128)(2,1)}), bf16[8,128,256]{2,1,0:T(8,128)(2,1)S(1)}, u32[]{:S(2)}, u32[]{:S(2)}) %all-to-all-start.1) | async-done | bytes 524320 | tf_op jit(solution)/shard_map/all_to_all | solution.py:364
  16.6 2.0 select.6
  18.6 11.1 %all-to-all-start.2 = ((bf16[32,128,256]{2,1,0:T(8,128)(2,1)}), bf16[32,128,256]{2,1,0:T(8,128)(2,1)S(1)}, u32[]{:S(2)}, u32[]{:S(2)}) async-start(bf16[32,128,256]{2,1,0:T(8,128)(2,1)} %select.6), calls=%async_computation.2 | async-start | bytes 4194304 | tf_op jit(solution)/shard_map/all_to_all | solution.py:367
  29.7 3.9 %rest.1 = (bf16[128,512]{1,0:T(8,128)(2,1)}, bf16[128,512]{1,0:T(8,128)(2,1)}, bf16[128,512]{1,0:T(8,128)(2,1)}, bf16[128,512]{1,0:T(8,128)(2,1)}, bf16[128,512]...) custom-call(s32[1]{0:T(128)} %bitcast.me_ref, ...), custom_call_target="tpu_custom_call" | custom-call | tf_op jit(solution)/shard_map/rest/pallas_call | solution.py:85
  33.6 0.9 collective-permute-start.7
  35.1 2.1 collective-permute-start.9
  37.2 2.8 %collective-permute-start.10 = (bf16[128,512]{1,0:T(8,128)(2,1)}, bf16[128,512]{1,0:T(8,128)(2,1)S(1)}, u32[]{:S(2)}, u32[]{:S(2)}) collective-permute-start(bf16[128,512]{1,0:T(8,128)(2,1)} %get-tuple-element.39), channel_id=1, source_target_pairs={{0,4},{1,5},{2,6},{3,7},{4,0},{5,1},{6,2},{7,3},{8,12},{9,13},{10,... | collective-permute-start | bytes 393224 | tf_op jit(solution)/shard_map/ppermute | solution.py:359
  39.9 1.7 collective-permute-start.11
  41.6 3.1 %collective-permute-done.7.refs_1_ = bf16[128,512]{1,0:T(8,128)(2,1)S(1)} collective-permute-done((bf16[128,512]{1,0:T(8,128)(2,1)}, bf16[128,512]{1,0:T(8,128)(2,1)S(1)}, u32[]{:S(2)}, u32[]{:S(2)}) %collective-permute-start.7) | collective-permute-done | bytes 131104 | tf_op jit(solution)/shard_map/ppermute | solution.py:359
  44.7 8.0 %collective-permute-start.12 = (bf16[128,512]{1,0:T(8,128)(2,1)}, bf16[128,512]{1,0:T(8,128)(2,1)S(1)}, u32[]{:S(2)}, u32[]{:S(2)}) collective-permute-start(bf16[128,512]{1,0:T(8,128)(2,1)} %get-tuple-element.41), channel_id=1, source_target_pairs={{0,6},{1,7},{2,0},{3,1},{4,2},{5,3},{6,4},{7,5},{8,14},{9,15},{10,... | collective-permute-start | bytes 393224 | tf_op jit(solution)/shard_map/ppermute | solution.py:359
  52.7 3.2 %collective-permute-start.13 = (bf16[128,512]{1,0:T(8,128)(2,1)}, bf16[128,512]{1,0:T(8,128)(2,1)S(1)}, u32[]{:S(2)}, u32[]{:S(2)}) collective-permute-start(bf16[128,512]{1,0:T(8,128)(2,1)} %get-tuple-element.42), channel_id=1, source_target_pairs={{0,7},{1,0},{2,1},{3,2},{4,3},{5,4},{6,5},{7,6},{8,15},{9,8},{10,9... | collective-permute-start | bytes 393224 | tf_op jit(solution)/shard_map/ppermute | solution.py:359
  56.4 3.0 %collective-permute-done.13.refs_7_ = bf16[128,512]{1,0:T(8,128)(2,1)S(1)} collective-permute-done((bf16[128,512]{1,0:T(8,128)(2,1)}, bf16[128,512]{1,0:T(8,128)(2,1)S(1)}, u32[]{:S(2)}, u32[]{:S(2)}) %collective-permute-start.13) | collective-permute-done | bytes 131104 | tf_op jit(solution)/shard_map/ppermute | solution.py:359
  59.4 0.9 copy-done.7
  60.3 1.1 assemble.3.refs_0_.refs_1_
  61.4 1.2 copy-done.1
  62.7 2.7 %select.5 = bf16[32,128,512]{2,1,0:T(8,128)(2,1)} custom-call(s32[32]{0:T(128)S(1)} %broadcast_minimum_fusion.pick_ref, bf16[8,128,512]{2,1,0:T(8,128)(2,1)S(1)} %copy-done.1, bf16[8,128,512]{2,1,0:T(8,128)(2,1)S(1)} %copy-done.1), custom_call_target="tpu_custom_call" | custom-call | tf_op jit(solution)/shard_map/select/pallas_call | solution.py:158
  65.4 11.8 %all-to-all-done.2.kv_ref = bf16[32,128,256]{2,1,0:T(8,128)(2,1)S(1)} async-done(((bf16[32,128,256]{2,1,0:T(8,128)(2,1)}), bf16[32,128,256]{2,1,0:T(8,128)(2,1)S(1)}, u32[]{:S(2)}, u32[]{:S(2)}) %all-to-all-start.2) | async-done | bytes 2097184 | tf_op jit(solution)/shard_map/all_to_all | solution.py:367
  77.2 9.5 %all-to-all-start = ((bf16[32,128,512]{2,1,0:T(8,128)(2,1)}), bf16[32,128,512]{2,1,0:T(8,128)(2,1)}, u32[]{:S(2)}, u32[]{:S(2)}) async-start(bf16[32,128,512]{2,1,0:T(8,128)(2,1)} %select.5), calls=%async_computation | async-start | bytes 8388608 | tf_op jit(solution)/shard_map/all_to_all | solution.py:371
  86.7 3.6 %collective-permute-start = (bf16[128,384]{1,0:T(8,128)(2,1)}, bf16[128,384]{1,0:T(8,128)(2,1)}, u32[]{:S(2)}, u32[]{:S(2)}) collective-permute-start(bf16[128,384]{1,0:T(8,128)(2,1)} %get-tuple-element.28), channel_id=1, source_target_pairs={{0,1},{1,2},{2,3},{3,4},{4,5},{5,6},{6,7},{7,0},{8,9},{9,10},{10,1... | collective-permute-start | bytes 294920 | tf_op jit(solution)/shard_map/ppermute | solution.py:359
  90.3 0.8 collective-permute-start.1
  91.6 0.8 reshape.78
  92.4 1.1 reduce_max.18
  93.8 4.2 %collective-permute-start.15 = (bf16[1024,512]{1,0:T(8,128)(2,1)S(1)}, bf16[1024,512]{1,0:T(8,128)(2,1)S(1)}, u32[]{:S(2)}, u32[]{:S(2)}) collective-permute-start(bf16[1024,512]{1,0:T(8,128)(2,1)S(1)} %bitcast.7), channel_id=1, source_target_pairs={{8,0},{16,8},{24,16},{32,24},{40,32},{48,40},{56,48},{64,56},{72,6... | collective-permute-start | bytes 3145736 | tf_op jit(solution)/shard_map/ppermute | solution.py:376
  98.0 1.9 collective-permute-start.14
  100.1 5.5 %collective-permute-done.refs_1_ = bf16[128,384]{1,0:T(8,128)(2,1)} collective-permute-done((bf16[128,384]{1,0:T(8,128)(2,1)}, bf16[128,384]{1,0:T(8,128)(2,1)}, u32[]{:S(2)}, u32[]{:S(2)}) %collective-permute-start) | collective-permute-done | bytes 98336 | tf_op jit(solution)/shard_map/ppermute | solution.py:359
  105.6 1.9 collective-permute-start.17
  107.5 2.4 collective-permute-start.16
  109.9 1.6 collective-permute-start.3
  111.7 5.5 %collective-permute-done.3.refs_4_ = bf16[128,384]{1,0:T(8,128)(2,1)S(1)} collective-permute-done((bf16[128,384]{1,0:T(8,128)(2,1)}, bf16[128,384]{1,0:T(8,128)(2,1)S(1)}, u32[]{:S(2)}, u32[]{:S(2)}) %collective-permute-start.3) | collective-permute-done | bytes 98336 | tf_op jit(solution)/shard_map/ppermute | solution.py:359
  117.2 3.6 %collective-permute-start.4 = (bf16[128,384]{1,0:T(8,128)(2,1)}, bf16[128,384]{1,0:T(8,128)(2,1)S(1)}, u32[]{:S(2)}, u32[]{:S(2)}) collective-permute-start(bf16[128,384]{1,0:T(8,128)(2,1)} %get-tuple-element.32), channel_id=1, source_target_pairs={{0,5},{1,6},{2,7},{3,0},{4,1},{5,2},{6,3},{7,4},{8,13},{9,14},{10,... | collective-permute-start | bytes 294920 | tf_op jit(solution)/shard_map/ppermute | solution.py:359
  121.0 4.7 %collective-permute-done.4.refs_5_ = bf16[128,384]{1,0:T(8,128)(2,1)S(1)} collective-permute-done((bf16[128,384]{1,0:T(8,128)(2,1)}, bf16[128,384]{1,0:T(8,128)(2,1)S(1)}, u32[]{:S(2)}, u32[]{:S(2)}) %collective-permute-start.4) | collective-permute-done | bytes 98336 | tf_op jit(solution)/shard_map/ppermute | solution.py:359
  125.7 2.1 collective-permute-start.5
  127.8 2.7 %collective-permute-done.5.refs_6_ = bf16[128,384]{1,0:T(8,128)(2,1)S(1)} collective-permute-done((bf16[128,384]{1,0:T(8,128)(2,1)}, bf16[128,384]{1,0:T(8,128)(2,1)S(1)}, u32[]{:S(2)}, u32[]{:S(2)}) %collective-permute-start.5) | collective-permute-done | bytes 98336 | tf_op jit(solution)/shard_map/ppermute | solution.py:359
  130.5 5.4 %collective-permute-start.6 = (bf16[128,384]{1,0:T(8,128)(2,1)}, bf16[128,384]{1,0:T(8,128)(2,1)S(1)}, u32[]{:S(2)}, u32[]{:S(2)}) collective-permute-start(bf16[128,384]{1,0:T(8,128)(2,1)} %get-tuple-element.34), channel_id=1, source_target_pairs={{0,7},{1,0},{2,1},{3,2},{4,3},{5,4},{6,5},{7,6},{8,15},{9,8},{10,9... | collective-permute-start | bytes 294920 | tf_op jit(solution)/shard_map/ppermute | solution.py:359
  136.0 2.5 collective-permute-done.6.refs_7_
  138.5 1.8 assemble.2
  140.2 53.8 %collective-permute-done.17.after_ref = bf16[1024,256]{1,0:T(8,128)(2,1)S(1)} collective-permute-done((bf16[1024,256]{1,0:T(8,128)(2,1)}, bf16[1024,256]{1,0:T(8,128)(2,1)S(1)}, u32[]{:S(2)}, u32[]{:S(2)}) %collective-permute-start.17) | collective-permute-done | bytes 524320 | tf_op jit(solution)/shard_map/ppermute | solution.py:374
  194.1 3.5 %collective-permute-done.16.before_ref = bf16[1024,256]{1,0:T(8,128)(2,1)S(1)} collective-permute-done((bf16[1024,256]{1,0:T(8,128)(2,1)}, bf16[1024,256]{1,0:T(8,128)(2,1)S(1)}, u32[]{:S(2)}, u32[]{:S(2)}) %collective-permute-start.16) | collective-permute-done | bytes 524320 | tf_op jit(solution)/shard_map/ppermute | solution.py:373
  197.6 1.1 copy-done.3
  198.7 1.0 copy-done.6
  199.8 6.7 %near.3 = (f32[1024,128]{1,0:T(8,128)}, f32[1024,128]{1,0:T(8,128)}, f32[1024,128]{1,0:T(8,128)}) custom-call(s32[8,16]{1,0:T(8,128)S(1)} %pad_add_fusion.on_ref, bf16[1024,384]{1,0:T(8,128)(2,1)S(1)} %bitcast.10, bf16[1024,256]{1,0:T(8,128)(2,1)S(1)} %bitcast.16, bf16[1024,256]{1,0:T(8,128)(2,1)S(1)} %collective-permute-done.16.before_ref, ...), custom_call_target="tpu_custom_call" | custom-call | flops 1610612736 | bytes 2097152 | tf_op jit(solution)/shard_map/near/pallas_call | solution.py:211
  206.5 12.4 %near.2 = (f32[1024,256]{1,0:T(8,128)}, f32[1024,256]{1,0:T(8,128)}, f32[1024,256]{1,0:T(8,128)}) custom-call(s32[8,16]{1,0:T(8,128)S(1)} %pad_add_fusion.on_ref, bf16[1024,384]{1,0:T(8,128)(2,1)S(1)} %bitcast.11, bf16[1024,512]{1,0:T(8,128)(2,1)S(1)} %bitcast.9, bf16[1024,512]{1,0:T(8,128)(2,1)S(1)} %collective-permute-done.14.before_ref, ...), custom_call_target="tpu_custom_call" | custom-call | flops 3221225472 | bytes 4194304 | tf_op jit(solution)/shard_map/near/pallas_call | solution.py:211
  218.9 6.1 %far.2.refs_0_ = bf16[1024,384]{1,0:T(8,128)(2,1)} custom-call(s32[8,32]{1,0:T(8,128)S(1)} %select_reduce_fusion.list_ref, s32[8]{0:T(128)S(1)} %select_reduce_fusion.1.rank_ref, s32[8]{0:T(128)S(1)} %get-tuple-element.49.count_ref, bf16[1024,384]{1,0:T(8,128)(2,1)S(1)} %bitcast.12, bf16[32,128,256]{2,1,0:T(8,128)(2,1)S(1)} %all-to-all-done.2.kv_ref, ...), custom_call_target="tpu_custom_call" | custom-call | flops 536870912 | bytes 2097152 | tf_op jit(solution)/shard_map/far/pallas_call | solution.py:287
  225.0 10.3 %far.3 = bf16[1024,384]{1,0:T(8,128)(2,1)} custom-call(s32[8,32]{1,0:T(8,128)S(1)} %select_reduce_fusion.list_ref, s32[8]{0:T(128)S(1)} %select_reduce_fusion.1.rank_ref, s32[8]{0:T(128)S(1)} %get-tuple-element.49.count_ref, bf16[1024,384]{1,0:T(8,128)(2,1)S(1)} %bitcast.13, ...), custom_call_target="tpu_custom_call", output_to_operand_aliasing={{}: (8, {})} | custom-call | flops 1073741824 | bytes 4194304 | tf_op jit(solution)/shard_map/far/pallas_call | solution.py:287
  235.3 14.9 %all_to_all.20.part_ref = bf16[8,128,384]{2,1,0:T(8,128)(2,1)S(1)} all-to-all(bf16[8,128,384]{2,1,0:T(8,128)(2,1)} %bitcast.17), channel_id=1, replica_groups=mesh['frame'=32,'head'=8] {'head'}, dimensions={0} | all-to-all | bytes 1572864 | tf_op jit(solution)/shard_map/all_to_all | solution.py:384
  250.2 1.5 unpack.1
  (41 shorter events, 2.6 us)
Async XLA Ops:
  0.0 7.1 %copy-start = (s32[256,256]{1,0:T(8,128)S(1)}, s32[256,256]{1,0:T(8,128)}, u32[]{:S(2)}) copy-start(s32[256,256]{1,0:T(8,128)} %param.7) | copy-start | bytes 786436
  1.8 14.8 %all-to-all-start.1 = ((bf16[8,128,256]{2,1,0:T(8,128)(2,1)}), bf16[8,128,256]{2,1,0:T(8,128)(2,1)S(1)}, u32[]{:S(2)}, u32[]{:S(2)}) async-start(bf16[8,128,256]{2,1,0:T(8,128)(2,1)} %lead.1), calls=%async_computation.1 | async-start | bytes 1048576 | tf_op jit(solution)/shard_map/all_to_all | solution.py:364
  16.6 2.0 copy-start.5
  18.6 58.6 %all-to-all-start.2 = ((bf16[32,128,256]{2,1,0:T(8,128)(2,1)}), bf16[32,128,256]{2,1,0:T(8,128)(2,1)S(1)}, u32[]{:S(2)}, u32[]{:S(2)}) async-start(bf16[32,128,256]{2,1,0:T(8,128)(2,1)} %select.6), calls=%async_computation.2 | async-start | bytes 4194304 | tf_op jit(solution)/shard_map/all_to_all | solution.py:367
  33.6 11.1 %collective-permute-start.7 = (bf16[128,512]{1,0:T(8,128)(2,1)}, bf16[128,512]{1,0:T(8,128)(2,1)S(1)}, u32[]{:S(2)}, u32[]{:S(2)}) collective-permute-start(bf16[128,512]{1,0:T(8,128)(2,1)} %get-tuple-element.36), channel_id=1, source_target_pairs={{0,1},{1,2},{2,3},{3,4},{4,5},{5,6},{6,7},{7,0},{8,9},{9,10},{10,1... | collective-permute-start | bytes 393224 | tf_op jit(solution)/shard_map/ppermute | solution.py:359
  34.5 18.1 %collective-permute-start.8 = (bf16[128,512]{1,0:T(8,128)(2,1)}, bf16[128,512]{1,0:T(8,128)(2,1)S(1)}, u32[]{:S(2)}, u32[]{:S(2)}) collective-permute-start(bf16[128,512]{1,0:T(8,128)(2,1)} %get-tuple-element.37), channel_id=1, source_target_pairs={{0,2},{1,3},{2,4},{3,5},{4,6},{5,7},{6,0},{7,1},{8,10},{9,11},{10,... | collective-permute-start | bytes 393224 | tf_op jit(solution)/shard_map/ppermute | solution.py:359
  35.1 20.8 %collective-permute-start.9 = (bf16[128,512]{1,0:T(8,128)(2,1)}, bf16[128,512]{1,0:T(8,128)(2,1)S(1)}, u32[]{:S(2)}, u32[]{:S(2)}) collective-permute-start(bf16[128,512]{1,0:T(8,128)(2,1)} %get-tuple-element.38), channel_id=1, source_target_pairs={{0,3},{1,4},{2,5},{3,6},{4,7},{5,0},{6,1},{7,2},{8,11},{9,12},{10,... | collective-permute-start | bytes 393224 | tf_op jit(solution)/shard_map/ppermute | solution.py:359
  37.2 18.7 %collective-permute-start.10 = (bf16[128,512]{1,0:T(8,128)(2,1)}, bf16[128,512]{1,0:T(8,128)(2,1)S(1)}, u32[]{:S(2)}, u32[]{:S(2)}) collective-permute-start(bf16[128,512]{1,0:T(8,128)(2,1)} %get-tuple-element.39), channel_id=1, source_target_pairs={{0,4},{1,5},{2,6},{3,7},{4,0},{5,1},{6,2},{7,3},{8,12},{9,13},{10,... | collective-permute-start | bytes 393224 | tf_op jit(solution)/shard_map/ppermute | solution.py:359
  39.9 16.0 %collective-permute-start.11 = (bf16[128,512]{1,0:T(8,128)(2,1)}, bf16[128,512]{1,0:T(8,128)(2,1)S(1)}, u32[]{:S(2)}, u32[]{:S(2)}) collective-permute-start(bf16[128,512]{1,0:T(8,128)(2,1)} %get-tuple-element.40), channel_id=1, source_target_pairs={{0,5},{1,6},{2,7},{3,0},{4,1},{5,2},{6,3},{7,4},{8,13},{9,14},{10,... | collective-permute-start | bytes 393224 | tf_op jit(solution)/shard_map/ppermute | solution.py:359
  44.7 11.8 %collective-permute-start.12 = (bf16[128,512]{1,0:T(8,128)(2,1)}, bf16[128,512]{1,0:T(8,128)(2,1)S(1)}, u32[]{:S(2)}, u32[]{:S(2)}) collective-permute-start(bf16[128,512]{1,0:T(8,128)(2,1)} %get-tuple-element.41), channel_id=1, source_target_pairs={{0,6},{1,7},{2,0},{3,1},{4,2},{5,3},{6,4},{7,5},{8,14},{9,15},{10,... | collective-permute-start | bytes 393224 | tf_op jit(solution)/shard_map/ppermute | solution.py:359
  52.7 6.8 %collective-permute-start.13 = (bf16[128,512]{1,0:T(8,128)(2,1)}, bf16[128,512]{1,0:T(8,128)(2,1)S(1)}, u32[]{:S(2)}, u32[]{:S(2)}) collective-permute-start(bf16[128,512]{1,0:T(8,128)(2,1)} %get-tuple-element.42), channel_id=1, source_target_pairs={{0,7},{1,0},{2,1},{3,2},{4,3},{5,4},{6,5},{7,6},{8,15},{9,8},{10,9... | collective-permute-start | bytes 393224 | tf_op jit(solution)/shard_map/ppermute | solution.py:359
  59.4 0.9 copy-start.7
  61.4 1.2 copy-start.1
  65.4 28.4 %copy-start.2 = (bf16[8,128,512]{2,1,0:T(8,128)(2,1)S(1)}, bf16[8,128,512]{2,1,0:T(8,128)(2,1)}, u32[]{:S(2)}) copy-start(bf16[8,128,512]{2,1,0:T(8,128)(2,1)} %assemble.3.refs_0_.refs_1_) | copy-start | bytes 3145732
  65.4 73.1 %copy-start.8 = (bf16[128,384]{1,0:T(8,128)(2,1)S(1)}, bf16[128,384]{1,0:T(8,128)(2,1)}, u32[]{:S(2)}) copy-start(bf16[128,384]{1,0:T(8,128)(2,1)} %get-tuple-element.27.refs_0_) | copy-start | bytes 294916
  77.2 147.8 %all-to-all-start = ((bf16[32,128,512]{2,1,0:T(8,128)(2,1)}), bf16[32,128,512]{2,1,0:T(8,128)(2,1)}, u32[]{:S(2)}, u32[]{:S(2)}) async-start(bf16[32,128,512]{2,1,0:T(8,128)(2,1)} %select.5), calls=%async_computation | async-start | bytes 8388608 | tf_op jit(solution)/shard_map/all_to_all | solution.py:371
  86.7 18.9 %collective-permute-start = (bf16[128,384]{1,0:T(8,128)(2,1)}, bf16[128,384]{1,0:T(8,128)(2,1)}, u32[]{:S(2)}, u32[]{:S(2)}) collective-permute-start(bf16[128,384]{1,0:T(8,128)(2,1)} %get-tuple-element.28), channel_id=1, source_target_pairs={{0,1},{1,2},{2,3},{3,4},{4,5},{5,6},{6,7},{7,0},{8,9},{9,10},{10,1... | collective-permute-start | bytes 294920 | tf_op jit(solution)/shard_map/ppermute | solution.py:359
  90.3 17.1 %collective-permute-start.1 = (bf16[128,384]{1,0:T(8,128)(2,1)}, bf16[128,384]{1,0:T(8,128)(2,1)}, u32[]{:S(2)}, u32[]{:S(2)}) collective-permute-start(bf16[128,384]{1,0:T(8,128)(2,1)} %get-tuple-element.29), channel_id=1, source_target_pairs={{0,2},{1,3},{2,4},{3,5},{4,6},{5,7},{6,0},{7,1},{8,10},{9,11},{10,... | collective-permute-start | bytes 294920 | tf_op jit(solution)/shard_map/ppermute | solution.py:359
  91.2 18.7 %collective-permute-start.2 = (bf16[128,384]{1,0:T(8,128)(2,1)}, bf16[128,384]{1,0:T(8,128)(2,1)}, u32[]{:S(2)}, u32[]{:S(2)}) collective-permute-start(bf16[128,384]{1,0:T(8,128)(2,1)} %get-tuple-element.30), channel_id=1, source_target_pairs={{0,3},{1,4},{2,5},{3,6},{4,7},{5,0},{6,1},{7,2},{8,11},{9,12},{10,... | collective-permute-start | bytes 294920 | tf_op jit(solution)/shard_map/ppermute | solution.py:359
  93.8 112.7 %collective-permute-start.15 = (bf16[1024,512]{1,0:T(8,128)(2,1)S(1)}, bf16[1024,512]{1,0:T(8,128)(2,1)S(1)}, u32[]{:S(2)}, u32[]{:S(2)}) collective-permute-start(bf16[1024,512]{1,0:T(8,128)(2,1)S(1)} %bitcast.7), channel_id=1, source_target_pairs={{8,0},{16,8},{24,16},{32,24},{40,32},{48,40},{56,48},{64,56},{72,6... | collective-permute-start | bytes 3145736 | tf_op jit(solution)/shard_map/ppermute | solution.py:376
  98.0 108.5 %collective-permute-start.14 = (bf16[1024,512]{1,0:T(8,128)(2,1)S(1)}, bf16[1024,512]{1,0:T(8,128)(2,1)S(1)}, u32[]{:S(2)}, u32[]{:S(2)}) collective-permute-start(bf16[1024,512]{1,0:T(8,128)(2,1)S(1)} %bitcast.8), channel_id=1, source_target_pairs={{0,8},{8,16},{16,24},{24,32},{32,40},{40,48},{48,56},{56,64},{64,7... | collective-permute-start | bytes 3145736 | tf_op jit(solution)/shard_map/ppermute | solution.py:375
  105.6 88.5 %collective-permute-start.17 = (bf16[1024,256]{1,0:T(8,128)(2,1)}, bf16[1024,256]{1,0:T(8,128)(2,1)S(1)}, u32[]{:S(2)}, u32[]{:S(2)}) collective-permute-start(bf16[1024,256]{1,0:T(8,128)(2,1)} %bitcast.14), channel_id=1, source_target_pairs={{8,0},{16,8},{24,16},{32,24},{40,32},{48,40},{56,48},{64,56},{72,6... | collective-permute-start | bytes 1572872 | tf_op jit(solution)/shard_map/ppermute | solution.py:374
  107.5 90.1 %collective-permute-start.16 = (bf16[1024,256]{1,0:T(8,128)(2,1)}, bf16[1024,256]{1,0:T(8,128)(2,1)S(1)}, u32[]{:S(2)}, u32[]{:S(2)}) collective-permute-start(bf16[1024,256]{1,0:T(8,128)(2,1)} %bitcast.15), channel_id=1, source_target_pairs={{0,8},{8,16},{16,24},{24,32},{32,40},{40,48},{48,56},{56,64},{64,7... | collective-permute-start | bytes 1572872 | tf_op jit(solution)/shard_map/ppermute | solution.py:373
  109.9 7.2 %collective-permute-start.3 = (bf16[128,384]{1,0:T(8,128)(2,1)}, bf16[128,384]{1,0:T(8,128)(2,1)S(1)}, u32[]{:S(2)}, u32[]{:S(2)}) collective-permute-start(bf16[128,384]{1,0:T(8,128)(2,1)} %get-tuple-element.31), channel_id=1, source_target_pairs={{0,4},{1,5},{2,6},{3,7},{4,0},{5,1},{6,2},{7,3},{8,12},{9,13},{10,... | collective-permute-start | bytes 294920 | tf_op jit(solution)/shard_map/ppermute | solution.py:359
  117.2 8.5 %collective-permute-start.4 = (bf16[128,384]{1,0:T(8,128)(2,1)}, bf16[128,384]{1,0:T(8,128)(2,1)S(1)}, u32[]{:S(2)}, u32[]{:S(2)}) collective-permute-start(bf16[128,384]{1,0:T(8,128)(2,1)} %get-tuple-element.32), channel_id=1, source_target_pairs={{0,5},{1,6},{2,7},{3,0},{4,1},{5,2},{6,3},{7,4},{8,13},{9,14},{10,... | collective-permute-start | bytes 294920 | tf_op jit(solution)/shard_map/ppermute | solution.py:359
  125.7 4.8 %collective-permute-start.5 = (bf16[128,384]{1,0:T(8,128)(2,1)}, bf16[128,384]{1,0:T(8,128)(2,1)S(1)}, u32[]{:S(2)}, u32[]{:S(2)}) collective-permute-start(bf16[128,384]{1,0:T(8,128)(2,1)} %get-tuple-element.33), channel_id=1, source_target_pairs={{0,6},{1,7},{2,0},{3,1},{4,2},{5,3},{6,4},{7,5},{8,14},{9,15},{10,... | collective-permute-start | bytes 294920 | tf_op jit(solution)/shard_map/ppermute | solution.py:359
  130.5 8.0 %collective-permute-start.6 = (bf16[128,384]{1,0:T(8,128)(2,1)}, bf16[128,384]{1,0:T(8,128)(2,1)S(1)}, u32[]{:S(2)}, u32[]{:S(2)}) collective-permute-start(bf16[128,384]{1,0:T(8,128)(2,1)} %get-tuple-element.34), channel_id=1, source_target_pairs={{0,7},{1,0},{2,1},{3,2},{4,3},{5,4},{6,5},{7,6},{8,15},{9,8},{10,9... | collective-permute-start | bytes 294920 | tf_op jit(solution)/shard_map/ppermute | solution.py:359
  197.6 1.1 copy-start.3
  198.7 1.0 copy-start.6
  218.9 6.1 %copy-start.4 = (bf16[8,128,384]{2,1,0:T(8,128)(2,1)S(1)}, bf16[8,128,384]{2,1,0:T(8,128)(2,1)}, u32[]{:S(2)}) copy-start(bf16[8,128,384]{2,1,0:T(8,128)(2,1)} %assemble.2) | copy-start | bytes 2359300

commit v6 on v5

--- a/solution.py
+++ b/solution.py
@@ -18,7 +18,6 @@
 PACK_STEPS = 4
 LEAD_STEPS = 2
 JOIN_STEPS = 2
-SELECT_STEPS = 2
 PARAMS = pltpu.CompilerParams(vmem_limit_bytes=24 << 20)
 NEG = -1e30
 SCALE2 = math.log2(math.e) / math.sqrt(HDIM)
@@ -122,53 +121,61 @@
     )(me, *parts)
 
 
-def unpack_kernel(part_ref, out_ref):
-    peers, _, local = part_ref.shape
+def unpack_kernel(early_ref, late_ref, out_ref, sem):
+    peers = late_ref.shape[0]
+    copies, left = [], 0
     for j in range(peers):
-        out_ref[:, j * local : (j + 1) * local] = part_ref[j]
-
-
-def unpack(parts):
-    peers, rows, local = parts.shape
-    tile = rows // PACK_STEPS
+        for part, ref in enumerate((early_ref, late_ref)):
+            cols = slice(left, left + ref.shape[2])
+            left += ref.shape[2]
+            copies.append(
+                pltpu.make_async_copy(ref.at[j], out_ref.at[:, cols], sem.at[2 * j + part])
+            )
+    for copy in copies:
+        copy.start()
+    for copy in copies:
+        copy.wait()
+
+
+def unpack(early, late):
+    peers, rows, width = late.shape
     return pl.pallas_call(
         unpack_kernel,
-        grid=(PACK_STEPS,),
-        in_specs=[pl.BlockSpec((peers, tile, local), lambda i: (0, i, 0))],
-        out_specs=pl.BlockSpec((tile, peers * local), lambda i: (i, 0)),
-        out_shape=jax.ShapeDtypeStruct((rows, peers * local), parts.dtype),
+        in_specs=[pl.BlockSpec(memory_space=pltpu.VMEM)] * 2,
+        out_specs=pl.BlockSpec(memory_space=pl.ANY),
+        out_shape=pltpu.HBM((rows, peers * (early.shape[2] + width)), late.dtype),
+        scratch_shapes=[pltpu.SemaphoreType.DMA((2 * peers,))],
         compiler_params=PARAMS,
         name="unpack",
-    )(parts)
-
-
-def select_kernel(pick_ref, *refs):
-    out_ref = refs[-1]
-    base = pl.program_id(0) * out_ref.shape[0]
-    for i in range(out_ref.shape[0]):
-        for g, kv_ref in enumerate(refs[:-1]):
-            out_ref[i, :, 2 * g * HDIM : 2 * (g + 1) * HDIM] = kv_ref[pick_ref[base + i]]
+    )(early, late)
+
+
+def select_kernel(pick_ref, kv_ref, out_ref, sem):
+    copies = [
+        pltpu.make_async_copy(kv_ref.at[pick_ref[i]], out_ref.at[i], sem.at[i])
+        for i in range(out_ref.shape[0])
+    ]
+    for copy in copies:
+        copy.start()
+    for copy in copies:
+        copy.wait()
 
 
 def select_blocks(picks, blocks):
     frames = picks.shape[0]
-    step = frames // SELECT_STEPS
-    count, rows, width = blocks.shape
-    heads = range(width // (2 * HDIM))
+    _, rows, width = blocks.shape
     return pl.pallas_call(
         select_kernel,
-        grid_spec=pltpu.PrefetchScalarGridSpec(
-            num_scalar_prefetch=1,
-            grid=(SELECT_STEPS,),
-            in_specs=[
-                pl.BlockSpec((count, rows, 2 * HDIM), lambda i, p, h=h: (0, 0, h)) for h in heads
-            ],
-            out_specs=pl.BlockSpec((step, rows, width), lambda i, p: (i, 0, 0)),
-        ),
+        in_specs=[
+            pl.BlockSpec(memory_space=pltpu.SMEM),
+            pl.BlockSpec(memory_space=pltpu.VMEM),
+        ],
+        out_specs=pl.BlockSpec(memory_space=pl.ANY),
         out_shape=pltpu.HBM((frames, rows, width), blocks.dtype),
+        scratch_shapes=[pltpu.SemaphoreType.DMA((frames,))],
         compiler_params=PARAMS,
         name="select",
-    )(picks, *([blocks] * len(heads)))
+    )(picks, blocks)
 
 
 def near_kernel(on_ref, q_ref, own_ref, before_ref, after_ref, o_ref, m_ref, l_ref):
@@ -232,8 +239,8 @@
     )(near_on, query, own, before, after)
 
 
-def far_kernel(list_ref, rank_ref, count_ref, q_ref, kv_ref, o_ref, m_ref, l_ref, *refs):
-    out_ref, m_s, l_s, acc_s = refs[-4:]
+def far_kernel(list_ref, rank_ref, count_ref, me_ref, q_ref, kv_ref, o_ref, m_ref, l_ref, *refs):
+    out_refs, (m_s, l_s, acc_s) = refs[:-3], refs[-3:]
     m_s[...] = m_ref[...]
     l_s[...] = l_ref[...]
     acc_s[...] = o_ref[...]
@@ -274,38 +281,42 @@
     for lead in range(0, blocks, TEAM):
         trips = (count_ref[rank_ref[lead]] + GROUP - 1) // GROUP
         lax.fori_loop(0, trips, functools.partial(step, lead), 0)
-    total = jnp.sum(l_s[...], axis=1, keepdims=True)
-    out_ref[...] = (acc_s[...] / total).astype(out_ref.dtype)
-
-
-def far_attention(tables, query, heads, far, near, result):
+    peers = len(out_refs)
+    for d, out_ref in enumerate(out_refs):
+        rows = slice(None)
+        if peers > 1:
+            block = lax.rem(me_ref[0] + d, peers)
+            rows = pl.ds(pl.multiple_of(block * BLOCK, BLOCK), BLOCK)
+        total = jnp.sum(l_s[rows, :], axis=1, keepdims=True)
+        out_ref[...] = (acc_s[rows, :] / total).astype(out_ref.dtype)
+
+
+def far_attention(tables, me, query, heads, far, near, pieces):
     rows = query.shape[0]
     first = heads[0]
     frames = far.shape[0]
-    full = pl.BlockSpec((rows, HDIM), lambda g, a, b, c: (0, g))
-    operands = [*tables, query, far, *in_hbm(*near)] + ([] if result is None else [result])
+    full = pl.BlockSpec((rows, HDIM), lambda g, a, b, c, m: (0, g))
+    out = pl.BlockSpec((rows // pieces, HDIM), lambda g, a, b, c, m: (0, g))
     return pl.pallas_call(
         far_kernel,
         grid_spec=pltpu.PrefetchScalarGridSpec(
-            num_scalar_prefetch=3,
+            num_scalar_prefetch=4,
             grid=(len(heads),),
             in_specs=[
-                pl.BlockSpec((rows, HDIM), lambda g, a, b, c: (0, first + g)),
-                pl.BlockSpec((frames, BLOCK, 2 * HDIM), lambda g, a, b, c: (0, 0, g)),
+                pl.BlockSpec((rows, HDIM), lambda g, a, b, c, m: (0, first + g)),
+                pl.BlockSpec((frames, BLOCK, 2 * HDIM), lambda g, a, b, c, m: (0, 0, g)),
                 full,
                 full,
                 full,
-            ]
-            + ([] if result is None else [pl.BlockSpec(memory_space=pl.ANY)]),
-            out_specs=pl.BlockSpec((rows, HDIM), lambda g, a, b, c: (0, first + g)),
+            ],
+            out_specs=[out] * pieces,
             scratch_shapes=[
                 pltpu.VMEM((rows, HDIM), jnp.float32),
                 pltpu.VMEM((rows, HDIM), jnp.float32),
                 pltpu.VMEM((rows, HDIM), jnp.float32),
             ],
         ),
-        out_shape=pltpu.HBM((rows, HEADS_LOCAL * HDIM), query.dtype),
-        input_output_aliases={} if result is None else {8: 0},
+        out_shape=[pltpu.HBM((rows // pieces, len(heads) * HDIM), query.dtype)] * pieces,
         cost_estimate=pl.CostEstimate(
             flops=len(heads) * rows * frames * BLOCK * HDIM,
             bytes_accessed=len(heads) * frames * BLOCK * 2 * HDIM * 2,
@@ -313,7 +324,7 @@
         ),
         compiler_params=PARAMS,
         name="far",
-    )(*operands)
+    )(*tables, me, query, far, *in_hbm(*near))
 
 
 def mask_tables(block_mask, frame_id, frame_count):
@@ -378,10 +389,11 @@
     query = query.reshape(FT, query.shape[2])
     near_early = near_attention(near_on, query, early, flat, before_early, after_early)
     near_late = near_attention(near_on, query, late, pairs, before_late, after_late)
-    result = far_attention(tables, query, early, far_early, near_early, None)
-    result = far_attention(tables, query, late, far_late, near_late, result)
-    result = result.reshape(peers, BLOCK, HEADS_LOCAL * HDIM)
-    return unpack(exchange(result, "head"))
+    early_out = far_attention(tables, me, query, early, far_early, near_early, peers)
+    early_out = assemble(me, turned(early_out))
+    (late_out,) = far_attention(tables, me, query, late, far_late, near_late, 1)
+    late_out = exchange(late_out.reshape(peers, BLOCK, len(late) * HDIM), "head")
+    return unpack(early_out, late_out)
 
 
 def solution(mesh):

time: 253 us -> 276 us (1.091)
  starting transfers between devices: 73.2 us -> 93.2 us
  blocking collectives: 14.9 us -> 0 us
  waiting for transfers between devices: 106 us -> 118 us
  local copies, waits for them, and re-layouts: 5.23 us -> 8.16 us
  Pallas kernels: 50.4 us -> 53.2 us
    all_to_all x1, waiting for transfers between devices: 0.01 us -> 93.3 us  [body(): far_late = exchange(parcel, 'frame')]
    ppermute x1, waiting for transfers between devices: 53.8 us -> 0.01 us  [body(): after_early = lax.ppermute(flat, 'frame', down)]
    ppermute x1, starting transfers between devices: 2.41 us -> 18.3 us  [body(): before_early = lax.ppermute(flat, 'frame', up)]
    all_to_all x1 -> x0, blocking collectives: 14.9 us -> none  [body(): return unpack(exchange(result, 'head'))]
    ppermute x14 -> x21, waiting for transfers between devices: 27.4 us -> 13.5 us  [turned(): moved.append(lax.ppermute(parts[d], 'head', turn))]
    all_to_all x1, waiting for transfers between devices: 11.8 us -> 0.01 us  [body(): far_early = exchange(parcel, 'frame')]
    ppermute x1, waiting for transfers between devices: 0.01 us -> 10.9 us  [body(): before_late = lax.ppermute(pairs, 'frame', up)]
    all_to_all x1, waiting for transfers between devices: 9.21 us -> 0.01 us  [body(): lead = exchange(pack_lead(key_rows, value_rows, peers), 'head')]
  transfers between devices with their start and end apart: 21 -> 29, of which waited for: 12 -> 11; matrix products, arithmetic and copies ran while one was open for 1% -> 1% of each run, Pallas kernels for 14% -> 18%
where the time goes in v6:
time: 276 us; the launch traced here: 275 us
  waiting for transfers between devices  118 us (43%)
  starting transfers between devices  93.2 us (34%)
  Pallas kernels  53.2 us (19%)
  local copies, waits for them, and re-layouts  8.16 us (3%)
    all_to_all x1, waiting for transfers between devices, body(): far_late = exchange(parcel, 'frame')  93.3 us
    ppermute x21, starting transfers between devices, turned(): moved.append(lax.ppermute(parts[d], 'head', turn))  38.5 us
    pallas_call x2, Pallas kernels, near_attention(): pl.pallas_call(near_kernel, grid_spec=pltpu.PrefetchScalarGridSpec(num_sc...  20.2 us
    ppermute x1, starting transfers between devices, body(): before_early = lax.ppermute(flat, 'frame', up)  18.3 us
    pallas_call x2, Pallas kernels, far_attention(): pl.pallas_call(far_kernel, grid_spec=pltpu.PrefetchScalarGridSpec(num_sca...  16.3 us
    ppermute x21, waiting for transfers between devices, turned(): moved.append(lax.ppermute(parts[d], 'head', turn))  13.5 us
    all_to_all x1, starting transfers between devices, body(): far_late = exchange(parcel, 'frame')  11.1 us
    ppermute x1, waiting for transfers between devices, body(): before_late = lax.ppermute(pairs, 'frame', up)  10.9 us
  transfers between devices with their start and end apart: 29, of which 11 were waited for; matrix products, arithmetic and copies ran while one was open for 1% of the time, Pallas kernels for 18%

profile of v6, /device:TPU:32, one launch (start us, length us, event | category | flops | bytes accessed | tf_op | source)
XLA Modules:
  0.0 274.8 jit_solution(17052568634352961205)
XLA Ops:
  0.0 1.8 lead.1
  1.8 5.3 %all-to-all-start = ((bf16[8,128,256]{2,1,0:T(8,128)(2,1)}), bf16[8,128,256]{2,1,0:T(8,128)(2,1)S(1)}, u32[]{:S(2)}, u32[]{:S(2)}) async-start(bf16[8,128,256]{2,1,0:T(8,128)(2,1)} %lead.1), calls=%async_computation | async-start | bytes 1048576 | tf_op jit(solution)/shard_map/all_to_all | solution.py:375
  7.1 4.1 %rest.1 = (bf16[128,512]{1,0:T(8,128)(2,1)}, bf16[128,512]{1,0:T(8,128)(2,1)}, bf16[128,512]{1,0:T(8,128)(2,1)}, bf16[128,512]{1,0:T(8,128)(2,1)}, bf16[128,512]...) custom-call(s32[1]{0:T(128)} %bitcast.me_ref, ...), custom_call_target="tpu_custom_call" | custom-call | tf_op jit(solution)/shard_map/rest/pallas_call | solution.py:84
  11.3 2.1 collective-permute-start.16
  13.4 1.5 collective-permute-start.17
  14.8 2.1 collective-permute-start.18
  16.9 2.1 collective-permute-start.19
  19.0 3.0 %collective-permute-start.20 = (bf16[128,512]{1,0:T(8,128)(2,1)}, bf16[128,512]{1,0:T(8,128)(2,1)S(1)}, u32[]{:S(2)}, u32[]{:S(2)}) collective-permute-start(bf16[128,512]{1,0:T(8,128)(2,1)} %get-tuple-element.59), channel_id=1, source_target_pairs={{0,5},{1,6},{2,7},{3,0},{4,1},{5,2},{6,3},{7,4},{8,13},{9,14},{10,... | collective-permute-start | bytes 393224 | tf_op jit(solution)/shard_map/ppermute | solution.py:370
  22.2 1.5 collective-permute-start.21
  23.7 1.1 collective-permute-start.22
  24.9 2.4 collective-permute-done.18.refs_3_
  27.3 1.1 collective-permute-done.20.refs_5_
  29.3 1.5 collective-permute-done.22.refs_7_
  32.7 1.2 copy-done.3
  33.9 2.9 %select.6 = bf16[32,128,512]{2,1,0:T(8,128)(2,1)} custom-call(s32[32]{0:T(128)S(1)} %broadcast_minimum_fusion.pick_ref, bf16[8,128,512]{2,1,0:T(8,128)(2,1)S(1)} %copy-done.3), custom_call_target="tpu_custom_call" | custom-call | tf_op jit(solution)/shard_map/select/pallas_call | solution.py:167
  36.8 11.1 %all-to-all-start.2 = ((bf16[32,128,512]{2,1,0:T(8,128)(2,1)}), bf16[32,128,512]{2,1,0:T(8,128)(2,1)}, u32[]{:S(2)}, u32[]{:S(2)}) async-start(bf16[32,128,512]{2,1,0:T(8,128)(2,1)} %select.6), calls=%async_computation.2 | async-start | bytes 8388608 | tf_op jit(solution)/shard_map/all_to_all | solution.py:382
  48.0 2.1 select.5
  50.2 93.3 %all-to-all-done.2.kv_ref = bf16[32,128,512]{2,1,0:T(8,128)(2,1)} async-done(((bf16[32,128,512]{2,1,0:T(8,128)(2,1)}), bf16[32,128,512]{2,1,0:T(8,128)(2,1)}, u32[]{:S(2)}, u32[]{:S(2)}) %all-to-all-start.2) | async-done | bytes 4194336 | tf_op jit(solution)/shard_map/all_to_all | solution.py:382
  143.5 6.0 %all-to-all-start.1 = ((bf16[32,128,256]{2,1,0:T(8,128)(2,1)}), bf16[32,128,256]{2,1,0:T(8,128)(2,1)S(1)}, u32[]{:S(2)}, u32[]{:S(2)}) async-start(bf16[32,128,256]{2,1,0:T(8,128)(2,1)} %select.5), calls=%async_computation.1 | async-start | bytes 4194304 | tf_op jit(solution)/shard_map/all_to_all | solution.py:378
  150.4 1.4 collective-permute-start.1
  151.8 1.3 collective-permute-start.2
  155.1 1.9 collective-permute-start.23
  157.1 6.0 %collective-permute-start.24 = (bf16[1024,512]{1,0:T(8,128)(2,1)S(1)}, bf16[1024,512]{1,0:T(8,128)(2,1)S(1)}, u32[]{:S(2)}, u32[]{:S(2)}) collective-permute-start(bf16[1024,512]{1,0:T(8,128)(2,1)S(1)} %bitcast.12), channel_id=1, source_target_pairs={{8,0},{16,8},{24,16},{32,24},{40,32},{48,40},{56,48},{64,56},{72,6... | collective-permute-start | bytes 3145736 | tf_op jit(solution)/shard_map/ppermute | solution.py:387
  163.7 2.1 collective-permute-start.3
  165.9 3.8 %collective-permute-start.4 = (bf16[128,384]{1,0:T(8,128)(2,1)}, bf16[128,384]{1,0:T(8,128)(2,1)S(1)}, u32[]{:S(2)}, u32[]{:S(2)}) collective-permute-start(bf16[128,384]{1,0:T(8,128)(2,1)} %get-tuple-element.40), channel_id=1, source_target_pairs={{0,5},{1,6},{2,7},{3,0},{4,1},{5,2},{6,3},{7,4},{8,13},{9,14},{10,... | collective-permute-start | bytes 294920 | tf_op jit(solution)/shard_map/ppermute | solution.py:370
  170.4 2.9 %collective-permute-start.6 = (bf16[128,384]{1,0:T(8,128)(2,1)}, bf16[128,384]{1,0:T(8,128)(2,1)S(1)}, u32[]{:S(2)}, u32[]{:S(2)}) collective-permute-start(bf16[128,384]{1,0:T(8,128)(2,1)} %get-tuple-element.42), channel_id=1, source_target_pairs={{0,7},{1,0},{2,1},{3,2},{4,3},{5,4},{6,5},{7,6},{8,15},{9,8},{10,9... | collective-permute-start | bytes 294920 | tf_op jit(solution)/shard_map/ppermute | solution.py:370
  173.4 2.1 collective-permute-done.5.refs_6_
  175.4 1.5 collective-permute-done.6.refs_7_
  176.9 1.8 assemble.3
  178.7 18.3 %collective-permute-start.7 = (bf16[1024,256]{1,0:T(8,128)(2,1)}, bf16[1024,256]{1,0:T(8,128)(2,1)}, u32[]{:S(2)}, u32[]{:S(2)}) collective-permute-start(bf16[1024,256]{1,0:T(8,128)(2,1)} %bitcast.14), channel_id=1, source_target_pairs={{0,8},{8,16},{16,24},{24,32},{32,40},{40,48},{48,56},{56,64},{64,7... | collective-permute-start | bytes 1572872 | tf_op jit(solution)/shard_map/ppermute | solution.py:384
  196.9 1.9 collective-permute-start.8
  198.9 10.9 %collective-permute-done.23.before_ref = bf16[1024,512]{1,0:T(8,128)(2,1)S(1)} collective-permute-done((bf16[1024,512]{1,0:T(8,128)(2,1)S(1)}, bf16[1024,512]{1,0:T(8,128)(2,1)S(1)}, u32[]{:S(2)}, u32[]{:S(2)}) %collective-permute-start.23) | collective-permute-done | bytes 1048608 | tf_op jit(solution)/shard_map/ppermute | solution.py:386
  209.8 1.1 copy-done.1
  210.9 1.2 copy-done.5
  212.2 12.4 %near.3 = (f32[1024,256]{1,0:T(8,128)}, f32[1024,256]{1,0:T(8,128)}, f32[1024,256]{1,0:T(8,128)}) custom-call(s32[8,16]{1,0:T(8,128)S(1)} %pad_add_fusion.on_ref, bf16[1024,384]{1,0:T(8,128)(2,1)S(1)} %bitcast.7, bf16[1024,512]{1,0:T(8,128)(2,1)S(1)} %bitcast.13, bf16[1024,512]{1,0:T(8,128)(2,1)S(1)} %collective-permute-done.23.before_ref, ...), custom_call_target="tpu_custom_call" | custom-call | flops 3221225472 | bytes 4194304 | tf_op jit(solution)/shard_map/near/pallas_call | solution.py:218
  224.6 10.3 %far.3 = bf16[1024,256]{1,0:T(8,128)(2,1)} custom-call(s32[8,32]{1,0:T(8,128)S(1)} %select_reduce_fusion.list_ref, s32[8]{0:T(128)S(1)} %select_reduce_fusion.1.rank_ref, s32[8]{0:T(128)S(1)} %get-tuple-element.65.count_ref, s32[1]{0:T(128)} %bitcast.me_ref, bf16[1024,384]{1,0:T(8,128)(2,1)S(1)} %bitcast.8, bf16[32,128,512]{2,1,0:T(8,128)(2,1)} %all-to-all-done.2.kv_ref, ...), custom_call_target="tpu_custom_call" | custom-call | flops 1073741824 | bytes 4194304 | tf_op jit(solution)/shard_map/far/pallas_call | solution.py:300
  234.9 4.2 %all-to-all-start.3 = ((bf16[8,128,256]{2,1,0:T(8,128)(2,1)}), bf16[8,128,256]{2,1,0:T(8,128)(2,1)}, u32[]{:S(2)}, u32[]{:S(2)}) async-start(bf16[8,128,256]{2,1,0:T(8,128)(2,1)} %bitcast.17), calls=%async_computation.3 | async-start | bytes 1048576 | tf_op jit(solution)/shard_map/all_to_all | solution.py:395
  240.1 7.8 %near.2 = (f32[1024,128]{1,0:T(8,128)}, f32[1024,128]{1,0:T(8,128)}, f32[1024,128]{1,0:T(8,128)}) custom-call(s32[8,16]{1,0:T(8,128)S(1)} %pad_add_fusion.on_ref, bf16[1024,384]{1,0:T(8,128)(2,1)S(1)} %bitcast.9, bf16[1024,256]{1,0:T(8,128)(2,1)S(1)} %bitcast.16, bf16[1024,256]{1,0:T(8,128)(2,1)} %collective-permute-done.7.before_ref, ...), custom_call_target="tpu_custom_call" | custom-call | flops 1610612736 | bytes 2097152 | tf_op jit(solution)/shard_map/near/pallas_call | solution.py:218
  247.9 6.0 %far.2 = (bf16[128,128]{1,0:T(8,128)(2,1)}, bf16[128,128]{1,0:T(8,128)(2,1)}, bf16[128,128]{1,0:T(8,128)(2,1)}, bf16[128,128]{1,0:T(8,128)(2,1)}, bf16[128,128]{...) custom-call(s32[8,32]{1,0:T(8,128)S(1)} %select_reduce_fusion.list_ref, ...), custom_call_target="tpu_custom_call" | custom-call | flops 536870912 | bytes 2097152 | tf_op jit(solution)/shard_map/far/pallas_call | solution.py:300
  253.9 2.0 collective-permute-start.9
  255.9 1.5 collective-permute-start.10
  257.4 2.1 collective-permute-start.11
  259.5 2.1 collective-permute-start.12
  261.5 3.0 %collective-permute-start.13 = (bf16[128,128]{1,0:T(8,128)(2,1)}, bf16[128,128]{1,0:T(8,128)(2,1)S(1)}, u32[]{:S(2)}, u32[]{:S(2)}) collective-permute-start(bf16[128,128]{1,0:T(8,128)(2,1)} %get-tuple-element.51), channel_id=1, source_target_pairs={{0,5},{1,6},{2,7},{3,0},{4,1},{5,2},{6,3},{7,4},{8,13},{9,14},{10,... | collective-permute-start | bytes 98312 | tf_op jit(solution)/shard_map/ppermute | solution.py:370
  264.5 1.5 collective-permute-start.14
  266.6 2.1 collective-permute-done.14.refs_6_
  268.6 1.5 collective-permute-done.15.refs_7_
  272.5 2.0 unpack.1
  (63 shorter events, 11.4 us)
Async XLA Ops:
  0.0 22.0 %copy-start = (s32[256,256]{1,0:T(8,128)S(1)}, s32[256,256]{1,0:T(8,128)}, u32[]{:S(2)}) copy-start(s32[256,256]{1,0:T(8,128)} %param.7) | copy-start | bytes 786436
  1.8 35.0 %all-to-all-start = ((bf16[8,128,256]{2,1,0:T(8,128)(2,1)}), bf16[8,128,256]{2,1,0:T(8,128)(2,1)S(1)}, u32[]{:S(2)}, u32[]{:S(2)}) async-start(bf16[8,128,256]{2,1,0:T(8,128)(2,1)} %lead.1), calls=%async_computation | async-start | bytes 1048576 | tf_op jit(solution)/shard_map/all_to_all | solution.py:375
  11.3 10.9 %collective-permute-start.16 = (bf16[128,512]{1,0:T(8,128)(2,1)}, bf16[128,512]{1,0:T(8,128)(2,1)S(1)}, u32[]{:S(2)}, u32[]{:S(2)}) collective-permute-start(bf16[128,512]{1,0:T(8,128)(2,1)} %get-tuple-element.55), channel_id=1, source_target_pairs={{0,1},{1,2},{2,3},{3,4},{4,5},{5,6},{6,7},{7,0},{8,9},{9,10},{10,1... | collective-permute-start | bytes 393224 | tf_op jit(solution)/shard_map/ppermute | solution.py:370
  13.4 10.4 %collective-permute-start.17 = (bf16[128,512]{1,0:T(8,128)(2,1)}, bf16[128,512]{1,0:T(8,128)(2,1)S(1)}, u32[]{:S(2)}, u32[]{:S(2)}) collective-permute-start(bf16[128,512]{1,0:T(8,128)(2,1)} %get-tuple-element.56), channel_id=1, source_target_pairs={{0,2},{1,3},{2,4},{3,5},{4,6},{5,7},{6,0},{7,1},{8,10},{9,11},{10,... | collective-permute-start | bytes 393224 | tf_op jit(solution)/shard_map/ppermute | solution.py:370
  14.8 12.4 %collective-permute-start.18 = (bf16[128,512]{1,0:T(8,128)(2,1)}, bf16[128,512]{1,0:T(8,128)(2,1)S(1)}, u32[]{:S(2)}, u32[]{:S(2)}) collective-permute-start(bf16[128,512]{1,0:T(8,128)(2,1)} %get-tuple-element.57), channel_id=1, source_target_pairs={{0,3},{1,4},{2,5},{3,6},{4,7},{5,0},{6,1},{7,2},{8,11},{9,12},{10,... | collective-permute-start | bytes 393224 | tf_op jit(solution)/shard_map/ppermute | solution.py:370
  16.9 10.4 %collective-permute-start.19 = (bf16[128,512]{1,0:T(8,128)(2,1)}, bf16[128,512]{1,0:T(8,128)(2,1)S(1)}, u32[]{:S(2)}, u32[]{:S(2)}) collective-permute-start(bf16[128,512]{1,0:T(8,128)(2,1)} %get-tuple-element.58), channel_id=1, source_target_pairs={{0,4},{1,5},{2,6},{3,7},{4,0},{5,1},{6,2},{7,3},{8,12},{9,13},{10,... | collective-permute-start | bytes 393224 | tf_op jit(solution)/shard_map/ppermute | solution.py:370
  19.0 9.4 %collective-permute-start.20 = (bf16[128,512]{1,0:T(8,128)(2,1)}, bf16[128,512]{1,0:T(8,128)(2,1)S(1)}, u32[]{:S(2)}, u32[]{:S(2)}) collective-permute-start(bf16[128,512]{1,0:T(8,128)(2,1)} %get-tuple-element.59), channel_id=1, source_target_pairs={{0,5},{1,6},{2,7},{3,0},{4,1},{5,2},{6,3},{7,4},{8,13},{9,14},{10,... | collective-permute-start | bytes 393224 | tf_op jit(solution)/shard_map/ppermute | solution.py:370
  22.2 7.1 %collective-permute-start.21 = (bf16[128,512]{1,0:T(8,128)(2,1)}, bf16[128,512]{1,0:T(8,128)(2,1)S(1)}, u32[]{:S(2)}, u32[]{:S(2)}) collective-permute-start(bf16[128,512]{1,0:T(8,128)(2,1)} %get-tuple-element.60), channel_id=1, source_target_pairs={{0,6},{1,7},{2,0},{3,1},{4,2},{5,3},{6,4},{7,5},{8,14},{9,15},{10,... | collective-permute-start | bytes 393224 | tf_op jit(solution)/shard_map/ppermute | solution.py:370
  23.7 7.0 %collective-permute-start.22 = (bf16[128,512]{1,0:T(8,128)(2,1)}, bf16[128,512]{1,0:T(8,128)(2,1)S(1)}, u32[]{:S(2)}, u32[]{:S(2)}) collective-permute-start(bf16[128,512]{1,0:T(8,128)(2,1)} %get-tuple-element.61), channel_id=1, source_target_pairs={{0,7},{1,0},{2,1},{3,2},{4,3},{5,4},{6,5},{7,6},{8,15},{9,8},{10,9... | collective-permute-start | bytes 393224 | tf_op jit(solution)/shard_map/ppermute | solution.py:370
  30.7 0.9 copy-start.9
  32.7 1.2 copy-start.3
  36.8 13.3 %copy-start.6 = (bf16[8,128,256]{2,1,0:T(8,128)(2,1)}, bf16[8,128,256]{2,1,0:T(8,128)(2,1)S(1)}, u32[]{:S(2)}) copy-start(bf16[8,128,256]{2,1,0:T(8,128)(2,1)S(1)} %all-to-all-done.kv_ref) | copy-start | bytes 1572868
  36.8 106.6 %all-to-all-start.2 = ((bf16[32,128,512]{2,1,0:T(8,128)(2,1)}), bf16[32,128,512]{2,1,0:T(8,128)(2,1)}, u32[]{:S(2)}, u32[]{:S(2)}) async-start(bf16[32,128,512]{2,1,0:T(8,128)(2,1)} %select.6), calls=%async_computation.2 | async-start | bytes 8388608 | tf_op jit(solution)/shard_map/all_to_all | solution.py:382
  48.0 107.2 %copy-start.4 = (bf16[8,128,512]{2,1,0:T(8,128)(2,1)S(1)}, bf16[8,128,512]{2,1,0:T(8,128)(2,1)}, u32[]{:S(2)}) copy-start(bf16[8,128,512]{2,1,0:T(8,128)(2,1)} %assemble.5.kv_ref) | copy-start | bytes 3145732
  48.0 128.9 %copy-start.10 = (bf16[128,384]{1,0:T(8,128)(2,1)S(1)}, bf16[128,384]{1,0:T(8,128)(2,1)}, u32[]{:S(2)}) copy-start(bf16[128,384]{1,0:T(8,128)(2,1)} %get-tuple-element.35.refs_0_) | copy-start | bytes 294916
  143.5 91.4 %all-to-all-start.1 = ((bf16[32,128,256]{2,1,0:T(8,128)(2,1)}), bf16[32,128,256]{2,1,0:T(8,128)(2,1)S(1)}, u32[]{:S(2)}, u32[]{:S(2)}) async-start(bf16[32,128,256]{2,1,0:T(8,128)(2,1)} %select.5), calls=%async_computation.1 | async-start | bytes 4194304 | tf_op jit(solution)/shard_map/all_to_all | solution.py:378
  149.5 14.2 %collective-permute-start = (bf16[128,384]{1,0:T(8,128)(2,1)}, bf16[128,384]{1,0:T(8,128)(2,1)}, u32[]{:S(2)}, u32[]{:S(2)}) collective-permute-start(bf16[128,384]{1,0:T(8,128)(2,1)} %get-tuple-element.36), channel_id=1, source_target_pairs={{0,1},{1,2},{2,3},{3,4},{4,5},{5,6},{6,7},{7,0},{8,9},{9,10},{10,1... | collective-permute-start | bytes 294920 | tf_op jit(solution)/shard_map/ppermute | solution.py:370
  150.4 15.6 %collective-permute-start.1 = (bf16[128,384]{1,0:T(8,128)(2,1)}, bf16[128,384]{1,0:T(8,128)(2,1)}, u32[]{:S(2)}, u32[]{:S(2)}) collective-permute-start(bf16[128,384]{1,0:T(8,128)(2,1)} %get-tuple-element.37), channel_id=1, source_target_pairs={{0,2},{1,3},{2,4},{3,5},{4,6},{5,7},{6,0},{7,1},{8,10},{9,11},{10,... | collective-permute-start | bytes 294920 | tf_op jit(solution)/shard_map/ppermute | solution.py:370
  151.8 18.0 %collective-permute-start.2 = (bf16[128,384]{1,0:T(8,128)(2,1)}, bf16[128,384]{1,0:T(8,128)(2,1)}, u32[]{:S(2)}, u32[]{:S(2)}) collective-permute-start(bf16[128,384]{1,0:T(8,128)(2,1)} %get-tuple-element.38), channel_id=1, source_target_pairs={{0,3},{1,4},{2,5},{3,6},{4,7},{5,0},{6,1},{7,2},{8,11},{9,12},{10,... | collective-permute-start | bytes 294920 | tf_op jit(solution)/shard_map/ppermute | solution.py:370
  155.1 54.6 %collective-permute-start.23 = (bf16[1024,512]{1,0:T(8,128)(2,1)S(1)}, bf16[1024,512]{1,0:T(8,128)(2,1)S(1)}, u32[]{:S(2)}, u32[]{:S(2)}) collective-permute-start(bf16[1024,512]{1,0:T(8,128)(2,1)S(1)} %bitcast.11), channel_id=1, source_target_pairs={{0,8},{8,16},{16,24},{24,32},{32,40},{40,48},{48,56},{56,64},{64,7... | collective-permute-start | bytes 3145736 | tf_op jit(solution)/shard_map/ppermute | solution.py:386
  157.1 52.7 %collective-permute-start.24 = (bf16[1024,512]{1,0:T(8,128)(2,1)S(1)}, bf16[1024,512]{1,0:T(8,128)(2,1)S(1)}, u32[]{:S(2)}, u32[]{:S(2)}) collective-permute-start(bf16[1024,512]{1,0:T(8,128)(2,1)S(1)} %bitcast.12), channel_id=1, source_target_pairs={{8,0},{16,8},{24,16},{32,24},{40,32},{48,40},{56,48},{64,56},{72,6... | collective-permute-start | bytes 3145736 | tf_op jit(solution)/shard_map/ppermute | solution.py:387
  163.7 6.7 %collective-permute-start.3 = (bf16[128,384]{1,0:T(8,128)(2,1)}, bf16[128,384]{1,0:T(8,128)(2,1)S(1)}, u32[]{:S(2)}, u32[]{:S(2)}) collective-permute-start(bf16[128,384]{1,0:T(8,128)(2,1)} %get-tuple-element.39), channel_id=1, source_target_pairs={{0,4},{1,5},{2,6},{3,7},{4,0},{5,1},{6,2},{7,3},{8,12},{9,13},{10,... | collective-permute-start | bytes 294920 | tf_op jit(solution)/shard_map/ppermute | solution.py:370
  165.9 7.4 %collective-permute-start.4 = (bf16[128,384]{1,0:T(8,128)(2,1)}, bf16[128,384]{1,0:T(8,128)(2,1)S(1)}, u32[]{:S(2)}, u32[]{:S(2)}) collective-permute-start(bf16[128,384]{1,0:T(8,128)(2,1)} %get-tuple-element.40), channel_id=1, source_target_pairs={{0,5},{1,6},{2,7},{3,0},{4,1},{5,2},{6,3},{7,4},{8,13},{9,14},{10,... | collective-permute-start | bytes 294920 | tf_op jit(solution)/shard_map/ppermute | solution.py:370
  169.8 5.6 %collective-permute-start.5 = (bf16[128,384]{1,0:T(8,128)(2,1)}, bf16[128,384]{1,0:T(8,128)(2,1)S(1)}, u32[]{:S(2)}, u32[]{:S(2)}) collective-permute-start(bf16[128,384]{1,0:T(8,128)(2,1)} %get-tuple-element.41), channel_id=1, source_target_pairs={{0,6},{1,7},{2,0},{3,1},{4,2},{5,3},{6,4},{7,5},{8,14},{9,15},{10,... | collective-permute-start | bytes 294920 | tf_op jit(solution)/shard_map/ppermute | solution.py:370
  170.4 6.5 %collective-permute-start.6 = (bf16[128,384]{1,0:T(8,128)(2,1)}, bf16[128,384]{1,0:T(8,128)(2,1)S(1)}, u32[]{:S(2)}, u32[]{:S(2)}) collective-permute-start(bf16[128,384]{1,0:T(8,128)(2,1)} %get-tuple-element.42), channel_id=1, source_target_pairs={{0,7},{1,0},{2,1},{3,2},{4,3},{5,4},{6,5},{7,6},{8,15},{9,8},{10,9... | collective-permute-start | bytes 294920 | tf_op jit(solution)/shard_map/ppermute | solution.py:370
  178.7 60.3 %collective-permute-start.7 = (bf16[1024,256]{1,0:T(8,128)(2,1)}, bf16[1024,256]{1,0:T(8,128)(2,1)}, u32[]{:S(2)}, u32[]{:S(2)}) collective-permute-start(bf16[1024,256]{1,0:T(8,128)(2,1)} %bitcast.14), channel_id=1, source_target_pairs={{0,8},{8,16},{16,24},{24,32},{32,40},{40,48},{48,56},{56,64},{64,7... | collective-permute-start | bytes 1572872 | tf_op jit(solution)/shard_map/ppermute | solution.py:384
  196.9 42.1 %collective-permute-start.8 = (bf16[1024,256]{1,0:T(8,128)(2,1)}, bf16[1024,256]{1,0:T(8,128)(2,1)}, u32[]{:S(2)}, u32[]{:S(2)}) collective-permute-start(bf16[1024,256]{1,0:T(8,128)(2,1)} %bitcast.15), channel_id=1, source_target_pairs={{8,0},{16,8},{24,16},{32,24},{40,32},{48,40},{56,48},{64,56},{72,6... | collective-permute-start | bytes 1572872 | tf_op jit(solution)/shard_map/ppermute | solution.py:385
  209.8 1.1 copy-start.1
  210.9 1.2 copy-start.5
  212.2 12.4 %copy-start.2 = (bf16[8,128,384]{2,1,0:T(8,128)(2,1)S(1)}, bf16[8,128,384]{2,1,0:T(8,128)(2,1)}, u32[]{:S(2)}) copy-start(bf16[8,128,384]{2,1,0:T(8,128)(2,1)} %assemble.3) | copy-start | bytes 2359300
  234.9 36.7 %all-to-all-start.3 = ((bf16[8,128,256]{2,1,0:T(8,128)(2,1)}), bf16[8,128,256]{2,1,0:T(8,128)(2,1)}, u32[]{:S(2)}, u32[]{:S(2)}) async-start(bf16[8,128,256]{2,1,0:T(8,128)(2,1)} %bitcast.17), calls=%async_computation.3 | async-start | bytes 1048576 | tf_op jit(solution)/shard_map/all_to_all | solution.py:395
  239.0 1.0 copy-start.7
  253.9 10.6 %collective-permute-start.9 = (bf16[128,128]{1,0:T(8,128)(2,1)}, bf16[128,128]{1,0:T(8,128)(2,1)S(1)}, u32[]{:S(2)}, u32[]{:S(2)}) collective-permute-start(bf16[128,128]{1,0:T(8,128)(2,1)} %get-tuple-element.47), channel_id=1, source_target_pairs={{0,1},{1,2},{2,3},{3,4},{4,5},{5,6},{6,7},{7,0},{8,9},{9,10},{10,1... | collective-permute-start | bytes 98312 | tf_op jit(solution)/shard_map/ppermute | solution.py:370
  255.9 10.0 %collective-permute-start.10 = (bf16[128,128]{1,0:T(8,128)(2,1)}, bf16[128,128]{1,0:T(8,128)(2,1)S(1)}, u32[]{:S(2)}, u32[]{:S(2)}) collective-permute-start(bf16[128,128]{1,0:T(8,128)(2,1)} %get-tuple-element.48), channel_id=1, source_target_pairs={{0,2},{1,3},{2,4},{3,5},{4,6},{5,7},{6,0},{7,1},{8,10},{9,11},{10,... | collective-permute-start | bytes 98312 | tf_op jit(solution)/shard_map/ppermute | solution.py:370
  257.4 8.6 %collective-permute-start.11 = (bf16[128,128]{1,0:T(8,128)(2,1)}, bf16[128,128]{1,0:T(8,128)(2,1)S(1)}, u32[]{:S(2)}, u32[]{:S(2)}) collective-permute-start(bf16[128,128]{1,0:T(8,128)(2,1)} %get-tuple-element.49), channel_id=1, source_target_pairs={{0,3},{1,4},{2,5},{3,6},{4,7},{5,0},{6,1},{7,2},{8,11},{9,12},{10,... | collective-permute-start | bytes 98312 | tf_op jit(solution)/shard_map/ppermute | solution.py:370
  259.5 6.5 %collective-permute-start.12 = (bf16[128,128]{1,0:T(8,128)(2,1)}, bf16[128,128]{1,0:T(8,128)(2,1)S(1)}, u32[]{:S(2)}, u32[]{:S(2)}) collective-permute-start(bf16[128,128]{1,0:T(8,128)(2,1)} %get-tuple-element.50), channel_id=1, source_target_pairs={{0,4},{1,5},{2,6},{3,7},{4,0},{5,1},{6,2},{7,3},{8,12},{9,13},{10,... | collective-permute-start | bytes 98312 | tf_op jit(solution)/shard_map/ppermute | solution.py:370
  261.5 5.0 %collective-permute-start.13 = (bf16[128,128]{1,0:T(8,128)(2,1)}, bf16[128,128]{1,0:T(8,128)(2,1)S(1)}, u32[]{:S(2)}, u32[]{:S(2)}) collective-permute-start(bf16[128,128]{1,0:T(8,128)(2,1)} %get-tuple-element.51), channel_id=1, source_target_pairs={{0,5},{1,6},{2,7},{3,0},{4,1},{5,2},{6,3},{7,4},{8,13},{9,14},{10,... | collective-permute-start | bytes 98312 | tf_op jit(solution)/shard_map/ppermute | solution.py:370
  264.5 4.1 %collective-permute-start.14 = (bf16[128,128]{1,0:T(8,128)(2,1)}, bf16[128,128]{1,0:T(8,128)(2,1)S(1)}, u32[]{:S(2)}, u32[]{:S(2)}) collective-permute-start(bf16[128,128]{1,0:T(8,128)(2,1)} %get-tuple-element.52), channel_id=1, source_target_pairs={{0,6},{1,7},{2,0},{3,1},{4,2},{5,3},{6,4},{7,5},{8,14},{9,15},{10,... | collective-permute-start | bytes 98312 | tf_op jit(solution)/shard_map/ppermute | solution.py:370
  266.0 4.1 %collective-permute-start.15 = (bf16[128,128]{1,0:T(8,128)(2,1)}, bf16[128,128]{1,0:T(8,128)(2,1)S(1)}, u32[]{:S(2)}, u32[]{:S(2)}) collective-permute-start(bf16[128,128]{1,0:T(8,128)(2,1)} %get-tuple-element.53), channel_id=1, source_target_pairs={{0,7},{1,0},{2,1},{3,2},{4,3},{5,4},{6,5},{7,6},{8,15},{9,8},{10,9... | collective-permute-start | bytes 98312 | tf_op jit(solution)/shard_map/ppermute | solution.py:370
  270.1 0.8 copy-start.11
  271.6 1.0 copy-start.8

commit v7 on v6

--- a/solution.py
+++ b/solution.py
@@ -14,6 +14,7 @@
 FT = BF * BLOCK
 HEADS_LOCAL = 3
 GROUP = 4
+SLAB = 4
 TEAM = 4
 PACK_STEPS = 4
 LEAD_STEPS = 2
@@ -94,6 +95,37 @@
         name="rest",
     )(me, *in_hbm(queries, keys, values))
     return outs[:peers], outs[peers:]
+
+
+def cross_kernel(me_ref, k_ref, v_ref, *out_refs):
+    peers = len(out_refs)
+    local = k_ref.shape[1] // peers
+    for d, out_ref in enumerate(out_refs):
+        base = lax.rem(me_ref[0] + d, peers) * local
+        for h in range(local // HDIM):
+            cols = pl.ds(pl.multiple_of(base + h * HDIM, HDIM), HDIM)
+            left = 2 * h * HDIM
+            out_ref[:, left : left + HDIM] = k_ref[:, cols]
+            out_ref[:, left + HDIM : left + 2 * HDIM] = v_ref[:, cols]
+
+
+def pack_cross(me, keys, values, peers):
+    rows, width = keys.shape
+    size = 2 * width // peers
+    tile = rows // PACK_STEPS
+    spec = pl.BlockSpec((tile, width), lambda i, m: (i, 0))
+    return pl.pallas_call(
+        cross_kernel,
+        grid_spec=pltpu.PrefetchScalarGridSpec(
+            num_scalar_prefetch=1,
+            grid=(PACK_STEPS,),
+            in_specs=[spec] * 2,
+            out_specs=[pl.BlockSpec((tile, size), lambda i, m: (i, 0))] * peers,
+        ),
+        out_shape=[pltpu.HBM((rows, size), keys.dtype)] * peers,
+        compiler_params=PARAMS,
+        name="cross",
+    )(me, *in_hbm(keys, values))
 
 
 def gather_kernel(me_ref, *refs):
@@ -360,8 +392,14 @@
     frame_id = lax.axis_index("frame")
     me = lax.axis_index("head").astype(jnp.int32).reshape(1)
     exchange = functools.partial(lax.all_to_all, split_axis=0, concat_axis=0, tiled=True)
-    up = [(i, i + 1) for i in range(frame_count - 1)]
+    slabs = range(frame_count // SLAB)
+    last = SLAB - 1
+    up = [(i, i + 1) for i in range(frame_count - 1) if i % SLAB != last]
     down = [(j, i) for i, j in up]
+    ahead = [(z * SLAB + last, (z + 1) * SLAB + last) for z in slabs[:-1]]
+    behind = [(z * SLAB, (z - 1) * SLAB) for z in slabs[1:]]
+    inward = [(z * SLAB + last, z * SLAB) for z in slabs[1:]]
+    inward += [(z * SLAB, z * SLAB + last) for z in slabs[:-1]]
 
     def turned(parts):
         moved = [parts[0]]
@@ -373,9 +411,12 @@
     early, late = [0], list(range(1, HEADS_LOCAL))
     outgoing, near_on, tables = mask_tables(block_mask, frame_id, frame_count)
     lead = exchange(pack_lead(key_rows, value_rows, peers), "head")
+    cross_keys = lax.ppermute(key_rows, "frame", ahead + behind)
+    cross_values = lax.ppermute(value_rows, "frame", ahead + behind)
     pair_parts, query_parts = pack_rest(me, queries, key_rows, value_rows, peers)
     parcel = select_blocks(outgoing, lead)
     far_early = exchange(parcel, "frame")
+    cross_parts = pack_cross(me, cross_keys, cross_values, peers)
     flat = lead.reshape(FT, lead.shape[2])
     pairs = assemble(me, turned(pair_parts))
     parcel = select_blocks(outgoing, pairs)
@@ -385,6 +426,20 @@
     after_early = lax.ppermute(flat, "frame", down)
     before_late = lax.ppermute(pairs, "frame", up)
     after_late = lax.ppermute(pairs, "frame", down)
+    folded = []
+    for d in range(peers):
+        pairs_of = [
+            (i * peers + j, k * peers + (j + d) % peers) for i, k in inward for j in range(peers)
+        ]
+        folded.append(lax.ppermute(cross_parts[d], ("frame", "head"), pairs_of))
+    cross = assemble(me, folded)
+    cross = cross.reshape(FT, cross.shape[2])
+    place = lax.rem(frame_id, SLAB)
+    split = flat.shape[1]
+    before_early = jnp.where(place == 0, cross[:, :split], before_early)
+    before_late = jnp.where(place == 0, cross[:, split:], before_late)
+    after_early = jnp.where(place == last, cross[:, :split], after_early)
+    after_late = jnp.where(place == last, cross[:, split:], after_late)
     query = assemble(me, turned(query_parts))
     query = query.reshape(FT, query.shape[2])
     near_early = near_attention(near_on, query, early, flat, before_early, after_early)

time: 276 us -> 336 us (1.22)
  waiting for transfers between devices: 118 us -> 155 us
  starting transfers between devices: 93.2 us -> 110 us
  Pallas kernels: 53.2 us -> 58.7 us
    ppermute x0 -> x10, waiting for transfers between devices: none -> 44.3 us  [the longest x1 36.8 us: body(): cross_keys = lax.ppermute(key_rows, 'frame', ahead + behind)]
    ppermute x0 -> x10, starting transfers between devices: none -> 34.2 us  [the longest x8 30.1 us: body(): folded.append(lax.ppermute(cross_parts[d], ('frame', 'head'), pairs_of))]
    ppermute x1, starting transfers between devices: 18.3 us -> 3.86 us  [body(): before_early = lax.ppermute(flat, 'frame', up)]
    ppermute x1, waiting for transfers between devices: 10.9 us -> 0.01 us  [body(): before_late = lax.ppermute(pairs, 'frame', up)]
    ppermute x1, starting transfers between devices: 6.05 us -> 1.29 us  [body(): after_late = lax.ppermute(pairs, 'frame', down)]
    ppermute x21, waiting for transfers between devices: 13.5 us -> 18.2 us  [turned(): moved.append(lax.ppermute(parts[d], 'head', turn))]
    pallas_call x0 -> x1, Pallas kernels: none -> 3.77 us  [pack_cross(): pl.pallas_call(cross_kernel, grid_spec=pltpu.PrefetchScalarGridSpec(num_s...]
    unnamed x24 -> x18, local copies, waits for them, and re-layouts: 7.25 us -> 4.07 us
  transfers between devices with their start and end apart: 29 -> 39, of which waited for: 11 -> 12; matrix products, arithmetic and copies ran while one was open for 1% -> 2% of each run, Pallas kernels for 18% -> 16%
where the time goes in v7:
time: 336 us; the launch traced here: 334 us
  waiting for transfers between devices  155 us (46%)
  starting transfers between devices  110 us (33%)
  Pallas kernels  58.7 us (17%)
  other arithmetic  5.19 us (2%)
  local copies, waits for them, and re-layouts  4.98 us (1%)
    all_to_all x1, waiting for transfers between devices, body(): far_late = exchange(parcel, 'frame')  92.7 us
    ppermute x1, waiting for transfers between devices, body(): cross_keys = lax.ppermute(key_rows, 'frame', ahead + behind)  36.8 us
    ppermute x21, starting transfers between devices, turned(): moved.append(lax.ppermute(parts[d], 'head', turn))  36.7 us
    ppermute x8, starting transfers between devices, body(): folded.append(lax.ppermute(cross_parts[d], ('frame', 'head'), pairs_of))  30.1 us
    pallas_call x2, Pallas kernels, near_attention(): pl.pallas_call(near_kernel, grid_spec=pltpu.PrefetchScalarGridSpec(num_sc...  20.2 us
    ppermute x21, waiting for transfers between devices, turned(): moved.append(lax.ppermute(parts[d], 'head', turn))  18.2 us
    pallas_call x2, Pallas kernels, far_attention(): pl.pallas_call(far_kernel, grid_spec=pltpu.PrefetchScalarGridSpec(num_sca...  16.5 us
    all_to_all x1, starting transfers between devices, body(): far_late = exchange(parcel, 'frame')  11.1 us
  transfers between devices with their start and end apart: 39, of which 12 were waited for; matrix products, arithmetic and copies ran while one was open for 2% of the time, Pallas kernels for 16%

profile of v7, /device:TPU:32, one launch (start us, length us, event | category | flops | bytes accessed | tf_op | source)
XLA Modules:
  0.0 334.2 jit_solution(11834724669028349270)
XLA Ops:
  0.0 1.8 lead.1
  1.8 5.3 %all-to-all-start = ((bf16[8,128,256]{2,1,0:T(8,128)(2,1)}), bf16[8,128,256]{2,1,0:T(8,128)(2,1)}, u32[]{:S(2)}, u32[]{:S(2)}) async-start(bf16[8,128,256]{2,1,0:T(8,128)(2,1)} %lead.1), calls=%async_computation | async-start | bytes 1048576 | tf_op jit(solution)/shard_map/all_to_all | solution.py:413
  7.1 4.0 %rest.1 = (bf16[128,512]{1,0:T(8,128)(2,1)}, bf16[128,512]{1,0:T(8,128)(2,1)}, bf16[128,512]{1,0:T(8,128)(2,1)}, bf16[128,512]{1,0:T(8,128)(2,1)}, bf16[128,512]...) custom-call(s32[1]{0:T(128)} %bitcast.me_ref, ...), custom_call_target="tpu_custom_call" | custom-call | tf_op jit(solution)/shard_map/rest/pallas_call | solution.py:85
  11.1 2.1 collective-permute-start.26
  14.7 2.1 collective-permute-start.28
  16.7 2.1 collective-permute-start.29
  18.8 3.0 collective-permute-start.30
  22.0 1.5 collective-permute-start.31
  24.7 2.6 collective-permute-done.28.refs_3_
  29.1 1.6 collective-permute-done.32.refs_7_
  33.9 2.9 select.8
  36.8 11.1 %all-to-all-start.2 = ((bf16[32,128,512]{2,1,0:T(8,128)(2,1)}), bf16[32,128,512]{2,1,0:T(8,128)(2,1)}, u32[]{:S(2)}, u32[]{:S(2)}) async-start(bf16[32,128,512]{2,1,0:T(8,128)(2,1)} %select.8), calls=%async_computation.2 | async-start | bytes 8388608 | tf_op jit(solution)/shard_map/all_to_all | solution.py:423
  47.9 2.7 select.7
  50.7 92.7 %all-to-all-done.2.kv_ref = bf16[32,128,512]{2,1,0:T(8,128)(2,1)} async-done(((bf16[32,128,512]{2,1,0:T(8,128)(2,1)}), bf16[32,128,512]{2,1,0:T(8,128)(2,1)}, u32[]{:S(2)}, u32[]{:S(2)}) %all-to-all-start.2) | async-done | bytes 4194336 | tf_op jit(solution)/shard_map/all_to_all | solution.py:423
  143.4 6.0 %all-to-all-start.1 = ((bf16[32,128,256]{2,1,0:T(8,128)(2,1)}), bf16[32,128,256]{2,1,0:T(8,128)(2,1)S(1)}, u32[]{:S(2)}, u32[]{:S(2)}) async-start(bf16[32,128,256]{2,1,0:T(8,128)(2,1)} %select.7), calls=%async_computation.1 | async-start | bytes 4194304 | tf_op jit(solution)/shard_map/all_to_all | solution.py:418
  149.4 2.1 collective-permute-start.7
  151.6 1.9 collective-permute-start.8
  157.5 4.0 %collective-permute-start.33 = (bf16[1024,512]{1,0:T(8,128)(2,1)S(1)}, bf16[1024,512]{1,0:T(8,128)(2,1)}, u32[]{:S(2)}, u32[]{:S(2)}) collective-permute-start(bf16[1024,512]{1,0:T(8,128)(2,1)S(1)} %bitcast.13), channel_id=1, source_target_pairs={{0,8},{8,16},{16,24},{32,40},{40,48},{48,56},{64,72},{72,80},{80,8... | collective-permute-start | bytes 3145736 | tf_op jit(solution)/shard_map/ppermute | solution.py:427
  163.2 5.6 %collective-permute-done.1.refs_2_ = bf16[128,384]{1,0:T(8,128)(2,1)} collective-permute-done((bf16[128,384]{1,0:T(8,128)(2,1)}, bf16[128,384]{1,0:T(8,128)(2,1)}, u32[]{:S(2)}, u32[]{:S(2)}) %collective-permute-start.1) | collective-permute-done | bytes 98336 | tf_op jit(solution)/shard_map/ppermute | solution.py:408
  168.8 36.8 %collective-permute-done.7.k_ref = bf16[128,3072]{1,0:T(8,128)(2,1)} collective-permute-done((bf16[128,3072]{1,0:T(8,128)(2,1)}, bf16[128,3072]{1,0:T(8,128)(2,1)}, u32[]{:S(2)}, u32[]{:S(2)}) %collective-permute-start.7) | collective-permute-done | bytes 786464 | tf_op jit(solution)/shard_map/ppermute | solution.py:414
  206.6 7.5 %collective-permute-done.8.v_ref = bf16[128,3072]{1,0:T(8,128)(2,1)} collective-permute-done((bf16[128,3072]{1,0:T(8,128)(2,1)}, bf16[128,3072]{1,0:T(8,128)(2,1)}, u32[]{:S(2)}, u32[]{:S(2)}) %collective-permute-start.8) | collective-permute-done | bytes 786464 | tf_op jit(solution)/shard_map/ppermute | solution.py:415
  214.1 2.0 collective-permute-start.4
  216.2 3.8 %cross.1 = (bf16[128,768]{1,0:T(8,128)(2,1)}, bf16[128,768]{1,0:T(8,128)(2,1)}, bf16[128,768]{1,0:T(8,128)(2,1)}, bf16[128,768]{1,0:T(8,128)(2,1)}, bf16[128,768...) custom-call(s32[1]{0:T(128)} %bitcast.me_ref, ...), custom_call_target="tpu_custom_call" | custom-call | tf_op jit(solution)/shard_map/cross/pallas_call | solution.py:117
  220.0 2.3 collective-permute-start.5
  222.3 3.5 %collective-permute-start.9 = (bf16[128,768]{1,0:T(8,128)(2,1)}, bf16[128,768]{1,0:T(8,128)(2,1)S(1)}, u32[]{:S(2)}, u32[]{:S(2)}) collective-permute-start(bf16[128,768]{1,0:T(8,128)(2,1)} %get-tuple-element.51), channel_id=1, source_target_pairs={{56,32},{57,33},{58,34},{59,35},{60,36},{61,37},{62,38},{63,39},{8... | collective-permute-start | bytes 589832 | tf_op jit(solution)/shard_map/ppermute | solution.py:434
  225.8 1.9 collective-permute-start.10
  227.8 3.8 %collective-permute-start.6 = (bf16[128,384]{1,0:T(8,128)(2,1)}, bf16[128,384]{1,0:T(8,128)(2,1)S(1)}, u32[]{:S(2)}, u32[]{:S(2)}) collective-permute-start(bf16[128,384]{1,0:T(8,128)(2,1)} %get-tuple-element.50), channel_id=1, source_target_pairs={{0,7},{1,0},{2,1},{3,2},{4,3},{5,4},{6,5},{7,6},{8,15},{9,8},{10,9... | collective-permute-start | bytes 294920 | tf_op jit(solution)/shard_map/ppermute | solution.py:408
  231.7 2.5 collective-permute-done.6.refs_7_
  234.1 2.3 collective-permute-start.11
  236.4 4.8 %collective-permute-start.12 = (bf16[128,768]{1,0:T(8,128)(2,1)}, bf16[128,768]{1,0:T(8,128)(2,1)S(1)}, u32[]{:S(2)}, u32[]{:S(2)}) collective-permute-start(bf16[128,768]{1,0:T(8,128)(2,1)} %get-tuple-element.54), channel_id=1, source_target_pairs={{56,35},{57,36},{58,37},{59,38},{60,39},{61,32},{62,33},{63,34},{8... | collective-permute-start | bytes 589832 | tf_op jit(solution)/shard_map/ppermute | solution.py:434
  241.2 5.8 %collective-permute-start.13 = (bf16[128,768]{1,0:T(8,128)(2,1)}, bf16[128,768]{1,0:T(8,128)(2,1)S(1)}, u32[]{:S(2)}, u32[]{:S(2)}) collective-permute-start(bf16[128,768]{1,0:T(8,128)(2,1)} %get-tuple-element.55), channel_id=1, source_target_pairs={{56,36},{57,37},{58,38},{59,39},{60,32},{61,33},{62,34},{63,35},{8... | collective-permute-start | bytes 589832 | tf_op jit(solution)/shard_map/ppermute | solution.py:434
  247.1 4.0 %collective-permute-start.14 = (bf16[128,768]{1,0:T(8,128)(2,1)}, bf16[128,768]{1,0:T(8,128)(2,1)S(1)}, u32[]{:S(2)}, u32[]{:S(2)}) collective-permute-start(bf16[128,768]{1,0:T(8,128)(2,1)} %get-tuple-element.56), channel_id=1, source_target_pairs={{56,37},{57,38},{58,39},{59,32},{60,33},{61,34},{62,35},{63,36},{8... | collective-permute-start | bytes 589832 | tf_op jit(solution)/shard_map/ppermute | solution.py:434
  251.1 5.2 %collective-permute-start.15 = (bf16[128,768]{1,0:T(8,128)(2,1)}, bf16[128,768]{1,0:T(8,128)(2,1)S(1)}, u32[]{:S(2)}, u32[]{:S(2)}) collective-permute-start(bf16[128,768]{1,0:T(8,128)(2,1)} %get-tuple-element.57), channel_id=1, source_target_pairs={{56,38},{57,39},{58,32},{59,33},{60,34},{61,35},{62,36},{63,37},{8... | collective-permute-start | bytes 589832 | tf_op jit(solution)/shard_map/ppermute | solution.py:434
  256.3 2.7 collective-permute-start.16
  259.2 1.8 assemble.4
  262.3 3.9 %collective-permute-start.17 = (bf16[1024,256]{1,0:T(8,128)(2,1)}, bf16[1024,256]{1,0:T(8,128)(2,1)}, u32[]{:S(2)}, u32[]{:S(2)}) collective-permute-start(bf16[1024,256]{1,0:T(8,128)(2,1)} %bitcast.3.own_ref), channel_id=1, source_target_pairs={{0,8},{8,16},{16,24},{32,40},{40,48},{48,56},{64,72},{72,80},{80,8... | collective-permute-start | bytes 1572872 | tf_op jit(solution)/shard_map/ppermute | solution.py:425
  267.5 1.9 broadcast_select_fusion
  269.5 12.4 %near.3 = (f32[1024,256]{1,0:T(8,128)}, f32[1024,256]{1,0:T(8,128)}, f32[1024,256]{1,0:T(8,128)}) custom-call(s32[8,16]{1,0:T(8,128)S(1)} %pad_add_fusion.on_ref, bf16[1024,384]{1,0:T(8,128)(2,1)S(1)} %bitcast.8, bf16[1024,512]{1,0:T(8,128)(2,1)S(1)} %bitcast.14, bf16[1024,512]{1,0:T(8,128)(2,1)S(1)} %get-tuple-element.84.before_ref, ...), custom_call_target="tpu_custom_call" | custom-call | flops 3221225472 | bytes 4194304 | tf_op jit(solution)/shard_map/near/pallas_call | solution.py:250
  282.0 10.5 %far.3 = bf16[1024,256]{1,0:T(8,128)(2,1)} custom-call(s32[8,32]{1,0:T(8,128)S(1)} %select_reduce_fusion.list_ref, s32[8]{0:T(128)S(1)} %select_reduce_fusion.1.rank_ref, s32[8]{0:T(128)S(1)} %get-tuple-element.81.count_ref, s32[1]{0:T(128)} %bitcast.me_ref, bf16[1024,384]{1,0:T(8,128)(2,1)S(1)} %bitcast.9, bf16[32,128,512]{2,1,0:T(8,128)(2,1)} %all-to-all-done.2.kv_ref, ...), custom_call_target="tpu_custom_call" | custom-call | flops 1073741824 | bytes 4194304 | tf_op jit(solution)/shard_map/far/pallas_call | solution.py:332
  292.4 5.7 %all-to-all-start.3 = ((bf16[8,128,256]{2,1,0:T(8,128)(2,1)}), bf16[8,128,256]{2,1,0:T(8,128)(2,1)}, u32[]{:S(2)}, u32[]{:S(2)}) async-start(bf16[8,128,256]{2,1,0:T(8,128)(2,1)} %bitcast.17), calls=%async_computation.3 | async-start | bytes 1048576 | tf_op jit(solution)/shard_map/all_to_all | solution.py:450
  299.5 7.8 %near.2 = (f32[1024,128]{1,0:T(8,128)}, f32[1024,128]{1,0:T(8,128)}, f32[1024,128]{1,0:T(8,128)}) custom-call(s32[8,16]{1,0:T(8,128)S(1)} %pad_add_fusion.on_ref, bf16[1024,384]{1,0:T(8,128)(2,1)S(1)} %bitcast.10, bf16[1024,256]{1,0:T(8,128)(2,1)} %bitcast.3.own_ref, bf16[1024,256]{1,0:T(8,128)(2,1)S(1)} %get-tuple-element.86.before_ref, ...), custom_call_target="tpu_custom_call" | custom-call | flops 1610612736 | bytes 2097152 | tf_op jit(solution)/shard_map/near/pallas_call | solution.py:250
  307.3 6.1 %far.2 = (bf16[128,128]{1,0:T(8,128)(2,1)}, bf16[128,128]{1,0:T(8,128)(2,1)}, bf16[128,128]{1,0:T(8,128)(2,1)}, bf16[128,128]{1,0:T(8,128)(2,1)}, bf16[128,128]{...) custom-call(s32[8,32]{1,0:T(8,128)S(1)} %select_reduce_fusion.list_ref, ...), custom_call_target="tpu_custom_call" | custom-call | flops 536870912 | bytes 2097152 | tf_op jit(solution)/shard_map/far/pallas_call | solution.py:332
  313.4 2.0 collective-permute-start.19
  316.8 2.1 collective-permute-start.21
  318.9 2.1 collective-permute-start.22
  321.0 3.0 collective-permute-start.23
  326.0 2.0 collective-permute-done.24.refs_6_
  332.0 2.0 unpack.1
  (81 shorter events, 26.6 us)
Async XLA Ops:
  0.0 21.8 %copy-start = (s32[256,256]{1,0:T(8,128)S(1)}, s32[256,256]{1,0:T(8,128)}, u32[]{:S(2)}) copy-start(s32[256,256]{1,0:T(8,128)} %param.7) | copy-start | bytes 786436
  1.8 34.9 %all-to-all-start = ((bf16[8,128,256]{2,1,0:T(8,128)(2,1)}), bf16[8,128,256]{2,1,0:T(8,128)(2,1)}, u32[]{:S(2)}, u32[]{:S(2)}) async-start(bf16[8,128,256]{2,1,0:T(8,128)(2,1)} %lead.1), calls=%async_computation | async-start | bytes 1048576 | tf_op jit(solution)/shard_map/all_to_all | solution.py:413
  11.1 10.9 %collective-permute-start.26 = (bf16[128,512]{1,0:T(8,128)(2,1)}, bf16[128,512]{1,0:T(8,128)(2,1)S(1)}, u32[]{:S(2)}, u32[]{:S(2)}) collective-permute-start(bf16[128,512]{1,0:T(8,128)(2,1)} %get-tuple-element.71), channel_id=1, source_target_pairs={{0,1},{1,2},{2,3},{3,4},{4,5},{5,6},{6,7},{7,0},{8,9},{9,10},{10,1... | collective-permute-start | bytes 393224 | tf_op jit(solution)/shard_map/ppermute | solution.py:408
  13.2 10.4 %collective-permute-start.27 = (bf16[128,512]{1,0:T(8,128)(2,1)}, bf16[128,512]{1,0:T(8,128)(2,1)S(1)}, u32[]{:S(2)}, u32[]{:S(2)}) collective-permute-start(bf16[128,512]{1,0:T(8,128)(2,1)} %get-tuple-element.72), channel_id=1, source_target_pairs={{0,2},{1,3},{2,4},{3,5},{4,6},{5,7},{6,0},{7,1},{8,10},{9,11},{10,... | collective-permute-start | bytes 393224 | tf_op jit(solution)/shard_map/ppermute | solution.py:408
  14.7 12.6 %collective-permute-start.28 = (bf16[128,512]{1,0:T(8,128)(2,1)}, bf16[128,512]{1,0:T(8,128)(2,1)S(1)}, u32[]{:S(2)}, u32[]{:S(2)}) collective-permute-start(bf16[128,512]{1,0:T(8,128)(2,1)} %get-tuple-element.73), channel_id=1, source_target_pairs={{0,3},{1,4},{2,5},{3,6},{4,7},{5,0},{6,1},{7,2},{8,11},{9,12},{10,... | collective-permute-start | bytes 393224 | tf_op jit(solution)/shard_map/ppermute | solution.py:408
  16.7 10.5 %collective-permute-start.29 = (bf16[128,512]{1,0:T(8,128)(2,1)}, bf16[128,512]{1,0:T(8,128)(2,1)S(1)}, u32[]{:S(2)}, u32[]{:S(2)}) collective-permute-start(bf16[128,512]{1,0:T(8,128)(2,1)} %get-tuple-element.74), channel_id=1, source_target_pairs={{0,4},{1,5},{2,6},{3,7},{4,0},{5,1},{6,2},{7,3},{8,12},{9,13},{10,... | collective-permute-start | bytes 393224 | tf_op jit(solution)/shard_map/ppermute | solution.py:408
  18.8 9.4 %collective-permute-start.30 = (bf16[128,512]{1,0:T(8,128)(2,1)}, bf16[128,512]{1,0:T(8,128)(2,1)S(1)}, u32[]{:S(2)}, u32[]{:S(2)}) collective-permute-start(bf16[128,512]{1,0:T(8,128)(2,1)} %get-tuple-element.75), channel_id=1, source_target_pairs={{0,5},{1,6},{2,7},{3,0},{4,1},{5,2},{6,3},{7,4},{8,13},{9,14},{10,... | collective-permute-start | bytes 393224 | tf_op jit(solution)/shard_map/ppermute | solution.py:408
  22.0 7.1 %collective-permute-start.31 = (bf16[128,512]{1,0:T(8,128)(2,1)}, bf16[128,512]{1,0:T(8,128)(2,1)S(1)}, u32[]{:S(2)}, u32[]{:S(2)}) collective-permute-start(bf16[128,512]{1,0:T(8,128)(2,1)} %get-tuple-element.76), channel_id=1, source_target_pairs={{0,6},{1,7},{2,0},{3,1},{4,2},{5,3},{6,4},{7,5},{8,14},{9,15},{10,... | collective-permute-start | bytes 393224 | tf_op jit(solution)/shard_map/ppermute | solution.py:408
  23.6 7.1 %collective-permute-start.32 = (bf16[128,512]{1,0:T(8,128)(2,1)}, bf16[128,512]{1,0:T(8,128)(2,1)S(1)}, u32[]{:S(2)}, u32[]{:S(2)}) collective-permute-start(bf16[128,512]{1,0:T(8,128)(2,1)} %get-tuple-element.77), channel_id=1, source_target_pairs={{0,7},{1,0},{2,1},{3,2},{4,3},{5,4},{6,5},{7,6},{8,15},{9,8},{10,9... | collective-permute-start | bytes 393224 | tf_op jit(solution)/shard_map/ppermute | solution.py:408
  30.7 0.9 copy-start.6
  32.7 1.2 copy-start.2
  36.8 106.6 %all-to-all-start.2 = ((bf16[32,128,512]{2,1,0:T(8,128)(2,1)}), bf16[32,128,512]{2,1,0:T(8,128)(2,1)}, u32[]{:S(2)}, u32[]{:S(2)}) async-start(bf16[32,128,512]{2,1,0:T(8,128)(2,1)} %select.8), calls=%async_computation.2 | async-start | bytes 8388608 | tf_op jit(solution)/shard_map/all_to_all | solution.py:423
  50.6 105.6 %copy-start.3 = (bf16[8,128,512]{2,1,0:T(8,128)(2,1)S(1)}, bf16[8,128,512]{2,1,0:T(8,128)(2,1)}, u32[]{:S(2)}) copy-start(bf16[8,128,512]{2,1,0:T(8,128)(2,1)} %assemble.7.kv_ref) | copy-start | bytes 3145732
  50.6 208.6 %copy-start.7 = (bf16[128,384]{1,0:T(8,128)(2,1)S(1)}, bf16[128,384]{1,0:T(8,128)(2,1)}, u32[]{:S(2)}) copy-start(bf16[128,384]{1,0:T(8,128)(2,1)} %get-tuple-element.43.refs_0_) | copy-start | bytes 294916
  143.4 149.0 %all-to-all-start.1 = ((bf16[32,128,256]{2,1,0:T(8,128)(2,1)}), bf16[32,128,256]{2,1,0:T(8,128)(2,1)S(1)}, u32[]{:S(2)}, u32[]{:S(2)}) async-start(bf16[32,128,256]{2,1,0:T(8,128)(2,1)} %select.7), calls=%async_computation.1 | async-start | bytes 4194304 | tf_op jit(solution)/shard_map/all_to_all | solution.py:418
  149.4 56.2 %collective-permute-start.7 = (bf16[128,3072]{1,0:T(8,128)(2,1)}, bf16[128,3072]{1,0:T(8,128)(2,1)}, u32[]{:S(2)}, u32[]{:S(2)}) collective-permute-start(bf16[128,3072]{1,0:T(8,128)(2,1)} %refs_3_.1), channel_id=1, source_target_pairs={{24,56},{56,88},{88,120},{120,152},{152,184},{184,216},{216,248},{... | collective-permute-start | bytes 2359304 | tf_op jit(solution)/shard_map/ppermute | solution.py:414
  151.6 62.5 %collective-permute-start.8 = (bf16[128,3072]{1,0:T(8,128)(2,1)}, bf16[128,3072]{1,0:T(8,128)(2,1)}, u32[]{:S(2)}, u32[]{:S(2)}) collective-permute-start(bf16[128,3072]{1,0:T(8,128)(2,1)} %refs_7_.1), channel_id=1, source_target_pairs={{24,56},{56,88},{88,120},{120,152},{152,184},{184,216},{216,248},{... | collective-permute-start | bytes 2359304 | tf_op jit(solution)/shard_map/ppermute | solution.py:415
  153.5 8.2 %collective-permute-start = (bf16[128,384]{1,0:T(8,128)(2,1)}, bf16[128,384]{1,0:T(8,128)(2,1)}, u32[]{:S(2)}, u32[]{:S(2)}) collective-permute-start(bf16[128,384]{1,0:T(8,128)(2,1)} %get-tuple-element.44), channel_id=1, source_target_pairs={{0,1},{1,2},{2,3},{3,4},{4,5},{5,6},{6,7},{7,0},{8,9},{9,10},{10,1... | collective-permute-start | bytes 294920 | tf_op jit(solution)/shard_map/ppermute | solution.py:408
  156.2 111.2 %collective-permute-start.34 = (bf16[1024,512]{1,0:T(8,128)(2,1)S(1)}, bf16[1024,512]{1,0:T(8,128)(2,1)}, u32[]{:S(2)}, u32[]{:S(2)}) collective-permute-start(bf16[1024,512]{1,0:T(8,128)(2,1)S(1)} %bitcast.12), channel_id=1, source_target_pairs={{8,0},{16,8},{24,16},{40,32},{48,40},{56,48},{72,64},{80,72},{88,8... | collective-permute-start | bytes 3145736 | tf_op jit(solution)/shard_map/ppermute | solution.py:428
  157.5 109.9 %collective-permute-start.33 = (bf16[1024,512]{1,0:T(8,128)(2,1)S(1)}, bf16[1024,512]{1,0:T(8,128)(2,1)}, u32[]{:S(2)}, u32[]{:S(2)}) collective-permute-start(bf16[1024,512]{1,0:T(8,128)(2,1)S(1)} %bitcast.13), channel_id=1, source_target_pairs={{0,8},{8,16},{16,24},{32,40},{40,48},{48,56},{64,72},{72,80},{80,8... | collective-permute-start | bytes 3145736 | tf_op jit(solution)/shard_map/ppermute | solution.py:427
  161.7 7.1 %collective-permute-start.1 = (bf16[128,384]{1,0:T(8,128)(2,1)}, bf16[128,384]{1,0:T(8,128)(2,1)}, u32[]{:S(2)}, u32[]{:S(2)}) collective-permute-start(bf16[128,384]{1,0:T(8,128)(2,1)} %get-tuple-element.45), channel_id=1, source_target_pairs={{0,2},{1,3},{2,4},{3,5},{4,6},{5,7},{6,0},{7,1},{8,10},{9,11},{10,... | collective-permute-start | bytes 294920 | tf_op jit(solution)/shard_map/ppermute | solution.py:408
  168.8 51.2 %collective-permute-start.2 = (bf16[128,384]{1,0:T(8,128)(2,1)}, bf16[128,384]{1,0:T(8,128)(2,1)S(1)}, u32[]{:S(2)}, u32[]{:S(2)}) collective-permute-start(bf16[128,384]{1,0:T(8,128)(2,1)} %get-tuple-element.46), channel_id=1, source_target_pairs={{0,3},{1,4},{2,5},{3,6},{4,7},{5,0},{6,1},{7,2},{8,11},{9,12},{10,... | collective-permute-start | bytes 294920 | tf_op jit(solution)/shard_map/ppermute | solution.py:408
  205.6 16.7 %collective-permute-start.3 = (bf16[128,384]{1,0:T(8,128)(2,1)}, bf16[128,384]{1,0:T(8,128)(2,1)S(1)}, u32[]{:S(2)}, u32[]{:S(2)}) collective-permute-start(bf16[128,384]{1,0:T(8,128)(2,1)} %get-tuple-element.47), channel_id=1, source_target_pairs={{0,4},{1,5},{2,6},{3,7},{4,0},{5,1},{6,2},{7,3},{8,12},{9,13},{10,... | collective-permute-start | bytes 294920 | tf_op jit(solution)/shard_map/ppermute | solution.py:408
  214.1 11.7 %collective-permute-start.4 = (bf16[128,384]{1,0:T(8,128)(2,1)}, bf16[128,384]{1,0:T(8,128)(2,1)S(1)}, u32[]{:S(2)}, u32[]{:S(2)}) collective-permute-start(bf16[128,384]{1,0:T(8,128)(2,1)} %get-tuple-element.48), channel_id=1, source_target_pairs={{0,5},{1,6},{2,7},{3,0},{4,1},{5,2},{6,3},{7,4},{8,13},{9,14},{10,... | collective-permute-start | bytes 294920 | tf_op jit(solution)/shard_map/ppermute | solution.py:408
  220.0 7.8 %collective-permute-start.5 = (bf16[128,384]{1,0:T(8,128)(2,1)}, bf16[128,384]{1,0:T(8,128)(2,1)S(1)}, u32[]{:S(2)}, u32[]{:S(2)}) collective-permute-start(bf16[128,384]{1,0:T(8,128)(2,1)} %get-tuple-element.49), channel_id=1, source_target_pairs={{0,6},{1,7},{2,0},{3,1},{4,2},{5,3},{6,4},{7,5},{8,14},{9,15},{10,... | collective-permute-start | bytes 294920 | tf_op jit(solution)/shard_map/ppermute | solution.py:408
  222.3 14.1 %collective-permute-start.9 = (bf16[128,768]{1,0:T(8,128)(2,1)}, bf16[128,768]{1,0:T(8,128)(2,1)S(1)}, u32[]{:S(2)}, u32[]{:S(2)}) collective-permute-start(bf16[128,768]{1,0:T(8,128)(2,1)} %get-tuple-element.51), channel_id=1, source_target_pairs={{56,32},{57,33},{58,34},{59,35},{60,36},{61,37},{62,38},{63,39},{8... | collective-permute-start | bytes 589832 | tf_op jit(solution)/shard_map/ppermute | solution.py:434
  225.8 15.4 %collective-permute-start.10 = (bf16[128,768]{1,0:T(8,128)(2,1)}, bf16[128,768]{1,0:T(8,128)(2,1)S(1)}, u32[]{:S(2)}, u32[]{:S(2)}) collective-permute-start(bf16[128,768]{1,0:T(8,128)(2,1)} %get-tuple-element.52), channel_id=1, source_target_pairs={{56,33},{57,34},{58,35},{59,36},{60,37},{61,38},{62,39},{63,32},{8... | collective-permute-start | bytes 589832 | tf_op jit(solution)/shard_map/ppermute | solution.py:434
  227.8 6.3 %collective-permute-start.6 = (bf16[128,384]{1,0:T(8,128)(2,1)}, bf16[128,384]{1,0:T(8,128)(2,1)S(1)}, u32[]{:S(2)}, u32[]{:S(2)}) collective-permute-start(bf16[128,384]{1,0:T(8,128)(2,1)} %get-tuple-element.50), channel_id=1, source_target_pairs={{0,7},{1,0},{2,1},{3,2},{4,3},{5,4},{6,5},{7,6},{8,15},{9,8},{10,9... | collective-permute-start | bytes 294920 | tf_op jit(solution)/shard_map/ppermute | solution.py:408
  234.1 12.9 %collective-permute-start.11 = (bf16[128,768]{1,0:T(8,128)(2,1)}, bf16[128,768]{1,0:T(8,128)(2,1)S(1)}, u32[]{:S(2)}, u32[]{:S(2)}) collective-permute-start(bf16[128,768]{1,0:T(8,128)(2,1)} %get-tuple-element.53), channel_id=1, source_target_pairs={{56,34},{57,35},{58,36},{59,37},{60,38},{61,39},{62,32},{63,33},{8... | collective-permute-start | bytes 589832 | tf_op jit(solution)/shard_map/ppermute | solution.py:434
  236.4 14.6 %collective-permute-start.12 = (bf16[128,768]{1,0:T(8,128)(2,1)}, bf16[128,768]{1,0:T(8,128)(2,1)S(1)}, u32[]{:S(2)}, u32[]{:S(2)}) collective-permute-start(bf16[128,768]{1,0:T(8,128)(2,1)} %get-tuple-element.54), channel_id=1, source_target_pairs={{56,35},{57,36},{58,37},{59,38},{60,39},{61,32},{62,33},{63,34},{8... | collective-permute-start | bytes 589832 | tf_op jit(solution)/shard_map/ppermute | solution.py:434
  241.2 15.1 %collective-permute-start.13 = (bf16[128,768]{1,0:T(8,128)(2,1)}, bf16[128,768]{1,0:T(8,128)(2,1)S(1)}, u32[]{:S(2)}, u32[]{:S(2)}) collective-permute-start(bf16[128,768]{1,0:T(8,128)(2,1)} %get-tuple-element.55), channel_id=1, source_target_pairs={{56,36},{57,37},{58,38},{59,39},{60,32},{61,33},{62,34},{63,35},{8... | collective-permute-start | bytes 589832 | tf_op jit(solution)/shard_map/ppermute | solution.py:434
  247.1 13.9 %collective-permute-start.14 = (bf16[128,768]{1,0:T(8,128)(2,1)}, bf16[128,768]{1,0:T(8,128)(2,1)S(1)}, u32[]{:S(2)}, u32[]{:S(2)}) collective-permute-start(bf16[128,768]{1,0:T(8,128)(2,1)} %get-tuple-element.56), channel_id=1, source_target_pairs={{56,37},{57,38},{58,39},{59,32},{60,33},{61,34},{62,35},{63,36},{8... | collective-permute-start | bytes 589832 | tf_op jit(solution)/shard_map/ppermute | solution.py:434
  251.1 11.2 %collective-permute-start.15 = (bf16[128,768]{1,0:T(8,128)(2,1)}, bf16[128,768]{1,0:T(8,128)(2,1)S(1)}, u32[]{:S(2)}, u32[]{:S(2)}) collective-permute-start(bf16[128,768]{1,0:T(8,128)(2,1)} %get-tuple-element.57), channel_id=1, source_target_pairs={{56,38},{57,39},{58,32},{59,33},{60,34},{61,35},{62,36},{63,37},{8... | collective-permute-start | bytes 589832 | tf_op jit(solution)/shard_map/ppermute | solution.py:434
  256.3 9.9 %collective-permute-start.16 = (bf16[128,768]{1,0:T(8,128)(2,1)}, bf16[128,768]{1,0:T(8,128)(2,1)S(1)}, u32[]{:S(2)}, u32[]{:S(2)}) collective-permute-start(bf16[128,768]{1,0:T(8,128)(2,1)} %get-tuple-element.58), channel_id=1, source_target_pairs={{56,39},{57,32},{58,33},{59,34},{60,35},{61,36},{62,37},{63,38},{8... | collective-permute-start | bytes 589832 | tf_op jit(solution)/shard_map/ppermute | solution.py:434
  261.0 37.2 %collective-permute-start.18 = (bf16[1024,256]{1,0:T(8,128)(2,1)}, bf16[1024,256]{1,0:T(8,128)(2,1)}, u32[]{:S(2)}, u32[]{:S(2)}) collective-permute-start(bf16[1024,256]{1,0:T(8,128)(2,1)} %bitcast.3.own_ref), channel_id=1, source_target_pairs={{8,0},{16,8},{24,16},{40,32},{48,40},{56,48},{72,64},{80,72},{88,8... | collective-permute-start | bytes 1572872 | tf_op jit(solution)/shard_map/ppermute | solution.py:426
  262.3 35.9 %collective-permute-start.17 = (bf16[1024,256]{1,0:T(8,128)(2,1)}, bf16[1024,256]{1,0:T(8,128)(2,1)}, u32[]{:S(2)}, u32[]{:S(2)}) collective-permute-start(bf16[1024,256]{1,0:T(8,128)(2,1)} %bitcast.3.own_ref), channel_id=1, source_target_pairs={{0,8},{8,16},{16,24},{32,40},{40,48},{48,56},{64,72},{72,80},{80,8... | collective-permute-start | bytes 1572872 | tf_op jit(solution)/shard_map/ppermute | solution.py:425
  267.4 1.9 copy-start.1
  267.4 2.1 copy-start.4
  292.4 38.6 %all-to-all-start.3 = ((bf16[8,128,256]{2,1,0:T(8,128)(2,1)}), bf16[8,128,256]{2,1,0:T(8,128)(2,1)}, u32[]{:S(2)}, u32[]{:S(2)}) async-start(bf16[8,128,256]{2,1,0:T(8,128)(2,1)} %bitcast.17), calls=%async_computation.3 | async-start | bytes 1048576 | tf_op jit(solution)/shard_map/all_to_all | solution.py:450
  313.4 10.6 %collective-permute-start.19 = (bf16[128,128]{1,0:T(8,128)(2,1)}, bf16[128,128]{1,0:T(8,128)(2,1)S(1)}, u32[]{:S(2)}, u32[]{:S(2)}) collective-permute-start(bf16[128,128]{1,0:T(8,128)(2,1)} %get-tuple-element.63), channel_id=1, source_target_pairs={{0,1},{1,2},{2,3},{3,4},{4,5},{5,6},{6,7},{7,0},{8,9},{9,10},{10,1... | collective-permute-start | bytes 98312 | tf_op jit(solution)/shard_map/ppermute | solution.py:408
  315.4 10.0 %collective-permute-start.20 = (bf16[128,128]{1,0:T(8,128)(2,1)}, bf16[128,128]{1,0:T(8,128)(2,1)S(1)}, u32[]{:S(2)}, u32[]{:S(2)}) collective-permute-start(bf16[128,128]{1,0:T(8,128)(2,1)} %get-tuple-element.64), channel_id=1, source_target_pairs={{0,2},{1,3},{2,4},{3,5},{4,6},{5,7},{6,0},{7,1},{8,10},{9,11},{10,... | collective-permute-start | bytes 98312 | tf_op jit(solution)/shard_map/ppermute | solution.py:408
  316.8 8.6 %collective-permute-start.21 = (bf16[128,128]{1,0:T(8,128)(2,1)}, bf16[128,128]{1,0:T(8,128)(2,1)S(1)}, u32[]{:S(2)}, u32[]{:S(2)}) collective-permute-start(bf16[128,128]{1,0:T(8,128)(2,1)} %get-tuple-element.65), channel_id=1, source_target_pairs={{0,3},{1,4},{2,5},{3,6},{4,7},{5,0},{6,1},{7,2},{8,11},{9,12},{10,... | collective-permute-start | bytes 98312 | tf_op jit(solution)/shard_map/ppermute | solution.py:408
  318.9 6.5 %collective-permute-start.22 = (bf16[128,128]{1,0:T(8,128)(2,1)}, bf16[128,128]{1,0:T(8,128)(2,1)S(1)}, u32[]{:S(2)}, u32[]{:S(2)}) collective-permute-start(bf16[128,128]{1,0:T(8,128)(2,1)} %get-tuple-element.66), channel_id=1, source_target_pairs={{0,4},{1,5},{2,6},{3,7},{4,0},{5,1},{6,2},{7,3},{8,12},{9,13},{10,... | collective-permute-start | bytes 98312 | tf_op jit(solution)/shard_map/ppermute | solution.py:408
  321.0 5.1 %collective-permute-start.23 = (bf16[128,128]{1,0:T(8,128)(2,1)}, bf16[128,128]{1,0:T(8,128)(2,1)S(1)}, u32[]{:S(2)}, u32[]{:S(2)}) collective-permute-start(bf16[128,128]{1,0:T(8,128)(2,1)} %get-tuple-element.67), channel_id=1, source_target_pairs={{0,5},{1,6},{2,7},{3,0},{4,1},{5,2},{6,3},{7,4},{8,13},{9,14},{10,... | collective-permute-start | bytes 98312 | tf_op jit(solution)/shard_map/ppermute | solution.py:408
  323.9 4.1 %collective-permute-start.24 = (bf16[128,128]{1,0:T(8,128)(2,1)}, bf16[128,128]{1,0:T(8,128)(2,1)S(1)}, u32[]{:S(2)}, u32[]{:S(2)}) collective-permute-start(bf16[128,128]{1,0:T(8,128)(2,1)} %get-tuple-element.68), channel_id=1, source_target_pairs={{0,6},{1,7},{2,0},{3,1},{4,2},{5,3},{6,4},{7,5},{8,14},{9,15},{10,... | collective-permute-start | bytes 98312 | tf_op jit(solution)/shard_map/ppermute | solution.py:408
  325.4 4.1 %collective-permute-start.25 = (bf16[128,128]{1,0:T(8,128)(2,1)}, bf16[128,128]{1,0:T(8,128)(2,1)S(1)}, u32[]{:S(2)}, u32[]{:S(2)}) collective-permute-start(bf16[128,128]{1,0:T(8,128)(2,1)} %get-tuple-element.69), channel_id=1, source_target_pairs={{0,7},{1,0},{2,1},{3,2},{4,3},{5,4},{6,5},{7,6},{8,15},{9,8},{10,9... | collective-permute-start | bytes 98312 | tf_op jit(solution)/shard_map/ppermute | solution.py:408
  329.5 0.8 copy-start.8
  331.0 1.0 copy-start.5

commit v8 on v6

--- a/solution.py
+++ b/solution.py
@@ -60,40 +60,40 @@
     )(*([keys] * group), *([values] * group))
 
 
-def rest_kernel(me_ref, q_ref, k_ref, v_ref, *out_refs):
-    peers = len(out_refs) // 2
-    local = q_ref.shape[1] // peers
-    heads = local // HDIM
-    for d in range(peers):
-        pair_ref, query_ref = out_refs[d], out_refs[peers + d]
+def pairs_kernel(me_ref, k_ref, v_ref, *out_refs):
+    peers = len(out_refs)
+    local = k_ref.shape[1] // peers
+    for d, out_ref in enumerate(out_refs):
         base = lax.rem(me_ref[0] + d, peers) * local
-        for h in range(1, heads):
+        for h in range(1, local // HDIM):
             cols = pl.ds(pl.multiple_of(base + h * HDIM, HDIM), HDIM)
             left = 2 * (h - 1) * HDIM
-            pair_ref[:, left : left + HDIM] = k_ref[:, cols]
-            pair_ref[:, left + HDIM : left + 2 * HDIM] = v_ref[:, cols]
-        query_ref[...] = q_ref[:, pl.ds(pl.multiple_of(base, HDIM), local)]
-
-
-def pack_rest(me, queries, keys, values, peers):
-    rows, width = queries.shape
-    local = width // peers
+            out_ref[:, left : left + HDIM] = k_ref[:, cols]
+            out_ref[:, left + HDIM : left + 2 * HDIM] = v_ref[:, cols]
+
+
+def queries_kernel(me_ref, q_ref, *out_refs):
+    peers = len(out_refs)
+    local = q_ref.shape[1] // peers
+    for d, out_ref in enumerate(out_refs):
+        base = lax.rem(me_ref[0] + d, peers) * local
+        out_ref[...] = q_ref[:, pl.ds(pl.multiple_of(base, HDIM), local)]
+
+
+def pack_turned(kernel, me, arrays, size, peers):
+    rows, width = arrays[0].shape
     tile = rows // PACK_STEPS
-    spec = pl.BlockSpec((tile, width), lambda i, m: (i, 0))
-    sizes = [2 * local - 2 * HDIM] * peers + [local] * peers
-    outs = pl.pallas_call(
-        rest_kernel,
+    return pl.pallas_call(
+        kernel,
         grid_spec=pltpu.PrefetchScalarGridSpec(
             num_scalar_prefetch=1,
             grid=(PACK_STEPS,),
-            in_specs=[spec] * 3,
-            out_specs=[pl.BlockSpec((tile, size), lambda i, m: (i, 0)) for size in sizes],
-        ),
-        out_shape=[pltpu.HBM((rows, size), queries.dtype) for size in sizes],
-        compiler_params=PARAMS,
-        name="rest",
-    )(me, *in_hbm(queries, keys, values))
-    return outs[:peers], outs[peers:]
+            in_specs=[pl.BlockSpec((tile, width), lambda i, m: (i, 0))] * len(arrays),
+            out_specs=[pl.BlockSpec((tile, size), lambda i, m: (i, 0))] * peers,
+        ),
+        out_shape=[pltpu.HBM((rows, size), arrays[0].dtype)] * peers,
+        compiler_params=PARAMS,
+    )(me, *in_hbm(*arrays))
 
 
 def gather_kernel(me_ref, *refs):
@@ -373,7 +373,9 @@
     early, late = [0], list(range(1, HEADS_LOCAL))
     outgoing, near_on, tables = mask_tables(block_mask, frame_id, frame_count)
     lead = exchange(pack_lead(key_rows, value_rows, peers), "head")
-    pair_parts, query_parts = pack_rest(me, queries, key_rows, value_rows, peers)
+    local = queries.shape[1] // peers
+    pair_parts = pack_turned(pairs_kernel, me, (key_rows, value_rows), 2 * local - 2 * HDIM, peers)
+    query_parts = pack_turned(queries_kernel, me, (queries,), local, peers)
     parcel = select_blocks(outgoing, lead)
     far_early = exchange(parcel, "frame")
     flat = lead.reshape(FT, lead.shape[2])

time: 276 us -> 289 us (1.047)
  the two profiles are of different devices: /device:TPU:32 before, /device:TPU:80 now
where the time goes in v8:
time: 289 us; the launch traced here: 287 us
  waiting for transfers between devices  140 us (48%)
  starting transfers between devices  80.1 us (28%)
  Pallas kernels  56 us (19%)
  local copies, waits for them, and re-layouts  9.05 us (3%)
    all_to_all x1, waiting for transfers between devices, body(): far_late = exchange(parcel, 'frame')  92.4 us
    ppermute x21, waiting for transfers between devices, turned(): moved.append(lax.ppermute(parts[d], 'head', turn))  47.4 us
    ppermute x21, starting transfers between devices, turned(): moved.append(lax.ppermute(parts[d], 'head', turn))  39.2 us
    pallas_call x2, Pallas kernels, near_attention(): pl.pallas_call(near_kernel, grid_spec=pltpu.PrefetchScalarGridSpec(num_sc...  20.2 us
    pallas_call x2, Pallas kernels, far_attention(): pl.pallas_call(far_kernel, grid_spec=pltpu.PrefetchScalarGridSpec(num_sca...  16.3 us
    all_to_all x1, starting transfers between devices, body(): far_late = exchange(parcel, 'frame')  10.8 us
    unnamed x24, local copies, waits for them, and re-layouts  8.13 us
    pallas_call x2, Pallas kernels, pack_turned(): pl.pallas_call(kernel, grid_spec=pltpu.PrefetchScalarGridSpec(num_scalar_...  6.96 us
  transfers between devices with their start and end apart: 29, of which 10 were waited for; matrix products, arithmetic and copies ran while one was open for 1% of the time, Pallas kernels for 18%

profile of v8, /device:TPU:80, one launch (start us, length us, event | category | flops | bytes accessed | tf_op | source)
XLA Modules:
  0.0 287.4 jit_solution(9875019729669510656)
XLA Ops:
  0.0 1.8 lead.1
  1.8 5.0 %all-to-all-start = ((bf16[8,128,256]{2,1,0:T(8,128)(2,1)}), bf16[8,128,256]{2,1,0:T(8,128)(2,1)S(1)}, u32[]{:S(2)}, u32[]{:S(2)}) async-start(bf16[8,128,256]{2,1,0:T(8,128)(2,1)} %lead.1), calls=%async_computation | async-start | bytes 1048576 | tf_op jit(solution)/shard_map/all_to_all | solution.py:375
  6.8 3.6 %shard_map.47 = (bf16[128,512]{1,0:T(8,128)(2,1)}, bf16[128,512]{1,0:T(8,128)(2,1)}, bf16[128,512]{1,0:T(8,128)(2,1)}, bf16[128,512]{1,0:T(8,128)(2,1)}, bf16[12...) custom-call(s32[1]{0:T(128)} %bitcast.me_ref, ...), custom_call_target="tpu_custom_call" | custom-call | tf_op jit(solution)/shard_map/pallas_call | solution.py:86
  10.5 2.1 collective-permute-start.16
  12.6 1.5 collective-permute-start.17
  14.0 2.1 collective-permute-start.18
  16.1 2.1 collective-permute-start.19
  18.2 3.0 %collective-permute-start.20 = (bf16[128,512]{1,0:T(8,128)(2,1)}, bf16[128,512]{1,0:T(8,128)(2,1)S(1)}, u32[]{:S(2)}, u32[]{:S(2)}) collective-permute-start(bf16[128,512]{1,0:T(8,128)(2,1)} %get-tuple-element.59), channel_id=1, source_target_pairs={{0,5},{1,6},{2,7},{3,0},{4,1},{5,2},{6,3},{7,4},{8,13},{9,14},{10,... | collective-permute-start | bytes 393224 | tf_op jit(solution)/shard_map/ppermute | solution.py:370
  21.4 1.5 collective-permute-start.21
  22.9 1.5 collective-permute-start.22
  24.4 2.5 collective-permute-done.18.refs_3_
  28.5 1.8 collective-permute-done.22.refs_7_
  31.2 1.1 assemble.5.kv_ref
  32.3 1.2 copy-done.3
  33.5 2.8 select.6
  36.4 10.8 %all-to-all-start.2 = ((bf16[32,128,512]{2,1,0:T(8,128)(2,1)}), bf16[32,128,512]{2,1,0:T(8,128)(2,1)}, u32[]{:S(2)}, u32[]{:S(2)}) async-start(bf16[32,128,512]{2,1,0:T(8,128)(2,1)} %select.6), calls=%async_computation.2 | async-start | bytes 8388608 | tf_op jit(solution)/shard_map/all_to_all | solution.py:384
  47.1 2.2 select.5
  49.3 92.4 %all-to-all-done.2.kv_ref = bf16[32,128,512]{2,1,0:T(8,128)(2,1)} async-done(((bf16[32,128,512]{2,1,0:T(8,128)(2,1)}), bf16[32,128,512]{2,1,0:T(8,128)(2,1)}, u32[]{:S(2)}, u32[]{:S(2)}) %all-to-all-start.2) | async-done | bytes 4194336 | tf_op jit(solution)/shard_map/all_to_all | solution.py:384
  141.8 6.8 %all-to-all-start.1 = ((bf16[32,128,256]{2,1,0:T(8,128)(2,1)}), bf16[32,128,256]{2,1,0:T(8,128)(2,1)S(1)}, u32[]{:S(2)}, u32[]{:S(2)}) async-start(bf16[32,128,256]{2,1,0:T(8,128)(2,1)} %select.5), calls=%async_computation.1 | async-start | bytes 4194304 | tf_op jit(solution)/shard_map/all_to_all | solution.py:380
  148.6 3.3 %shard_map.46 = (bf16[128,384]{1,0:T(8,128)(2,1)}, bf16[128,384]{1,0:T(8,128)(2,1)}, bf16[128,384]{1,0:T(8,128)(2,1)}, bf16[128,384]{1,0:T(8,128)(2,1)}, bf16[12...) custom-call(s32[1]{0:T(128)} %bitcast.me_ref, ...), custom_call_target="tpu_custom_call" | custom-call | tf_op jit(solution)/shard_map/pallas_call | solution.py:86
  152.0 1.1 collective-permute-start
  153.1 1.4 collective-permute-start.1
  157.2 1.9 collective-permute-start.23
  159.2 5.1 %collective-permute-start.24 = (bf16[1024,512]{1,0:T(8,128)(2,1)S(1)}, bf16[1024,512]{1,0:T(8,128)(2,1)S(1)}, u32[]{:S(2)}, u32[]{:S(2)}) collective-permute-start(bf16[1024,512]{1,0:T(8,128)(2,1)S(1)} %bitcast.12), channel_id=1, source_target_pairs={{8,0},{16,8},{24,16},{32,24},{40,32},{48,40},{56,48},{64,56},{72,6... | collective-permute-start | bytes 3145736 | tf_op jit(solution)/shard_map/ppermute | solution.py:389
  164.9 2.5 collective-permute-start.3
  167.5 4.1 %collective-permute-start.4 = (bf16[128,384]{1,0:T(8,128)(2,1)}, bf16[128,384]{1,0:T(8,128)(2,1)S(1)}, u32[]{:S(2)}, u32[]{:S(2)}) collective-permute-start(bf16[128,384]{1,0:T(8,128)(2,1)} %get-tuple-element.40), channel_id=1, source_target_pairs={{0,5},{1,6},{2,7},{3,0},{4,1},{5,2},{6,3},{7,4},{8,13},{9,14},{10,... | collective-permute-start | bytes 294920 | tf_op jit(solution)/shard_map/ppermute | solution.py:370
  172.2 3.1 %collective-permute-start.6 = (bf16[128,384]{1,0:T(8,128)(2,1)}, bf16[128,384]{1,0:T(8,128)(2,1)S(1)}, u32[]{:S(2)}, u32[]{:S(2)}) collective-permute-start(bf16[128,384]{1,0:T(8,128)(2,1)} %get-tuple-element.42), channel_id=1, source_target_pairs={{0,7},{1,0},{2,1},{3,2},{4,3},{5,4},{6,5},{7,6},{8,15},{9,8},{10,9... | collective-permute-start | bytes 294920 | tf_op jit(solution)/shard_map/ppermute | solution.py:370
  175.4 1.4 collective-permute-done.5.refs_6_
  176.7 36.1 %collective-permute-done.6.refs_7_ = bf16[128,384]{1,0:T(8,128)(2,1)S(1)} collective-permute-done((bf16[128,384]{1,0:T(8,128)(2,1)}, bf16[128,384]{1,0:T(8,128)(2,1)S(1)}, u32[]{:S(2)}, u32[]{:S(2)}) %collective-permute-start.6) | collective-permute-done | bytes 98336 | tf_op jit(solution)/shard_map/ppermute | solution.py:370
  213.7 1.8 assemble.3
  215.5 1.9 collective-permute-start.7
  217.4 5.1 %collective-permute-start.8 = (bf16[1024,256]{1,0:T(8,128)(2,1)}, bf16[1024,256]{1,0:T(8,128)(2,1)}, u32[]{:S(2)}, u32[]{:S(2)}) collective-permute-start(bf16[1024,256]{1,0:T(8,128)(2,1)} %bitcast.15), channel_id=1, source_target_pairs={{8,0},{16,8},{24,16},{32,24},{40,32},{48,40},{56,48},{64,56},{72,6... | collective-permute-start | bytes 1572872 | tf_op jit(solution)/shard_map/ppermute | solution.py:387
  222.6 1.1 copy-done.1
  223.7 1.2 copy-done.5
  225.0 12.4 %near.3 = (f32[1024,256]{1,0:T(8,128)}, f32[1024,256]{1,0:T(8,128)}, f32[1024,256]{1,0:T(8,128)}) custom-call(s32[8,16]{1,0:T(8,128)S(1)} %pad_add_fusion.on_ref, bf16[1024,384]{1,0:T(8,128)(2,1)S(1)} %bitcast.7, bf16[1024,512]{1,0:T(8,128)(2,1)S(1)} %bitcast.13, bf16[1024,512]{1,0:T(8,128)(2,1)S(1)} %collective-permute-done.23.before_ref, ...), custom_call_target="tpu_custom_call" | custom-call | flops 3221225472 | bytes 4194304 | tf_op jit(solution)/shard_map/near/pallas_call | solution.py:218
  237.4 10.3 %far.3 = bf16[1024,256]{1,0:T(8,128)(2,1)} custom-call(s32[8,32]{1,0:T(8,128)S(1)} %select_reduce_fusion.list_ref, s32[8]{0:T(128)S(1)} %select_reduce_fusion.1.rank_ref, s32[8]{0:T(128)S(1)} %get-tuple-element.65.count_ref, s32[1]{0:T(128)} %bitcast.me_ref, bf16[1024,384]{1,0:T(8,128)(2,1)S(1)} %bitcast.8, bf16[32,128,512]{2,1,0:T(8,128)(2,1)} %all-to-all-done.2.kv_ref, ...), custom_call_target="tpu_custom_call" | custom-call | flops 1073741824 | bytes 4194304 | tf_op jit(solution)/shard_map/far/pallas_call | solution.py:300
  247.6 4.1 %all-to-all-start.3 = ((bf16[8,128,256]{2,1,0:T(8,128)(2,1)}), bf16[8,128,256]{2,1,0:T(8,128)(2,1)}, u32[]{:S(2)}, u32[]{:S(2)}) async-start(bf16[8,128,256]{2,1,0:T(8,128)(2,1)} %bitcast.17), calls=%async_computation.3 | async-start | bytes 1048576 | tf_op jit(solution)/shard_map/all_to_all | solution.py:397
  252.9 7.8 %near.2 = (f32[1024,128]{1,0:T(8,128)}, f32[1024,128]{1,0:T(8,128)}, f32[1024,128]{1,0:T(8,128)}) custom-call(s32[8,16]{1,0:T(8,128)S(1)} %pad_add_fusion.on_ref, bf16[1024,384]{1,0:T(8,128)(2,1)S(1)} %bitcast.9, bf16[1024,256]{1,0:T(8,128)(2,1)S(1)} %bitcast.16, bf16[1024,256]{1,0:T(8,128)(2,1)} %collective-permute-done.7.before_ref, ...), custom_call_target="tpu_custom_call" | custom-call | flops 1610612736 | bytes 2097152 | tf_op jit(solution)/shard_map/near/pallas_call | solution.py:218
  260.7 6.0 %far.2 = (bf16[128,128]{1,0:T(8,128)(2,1)}, bf16[128,128]{1,0:T(8,128)(2,1)}, bf16[128,128]{1,0:T(8,128)(2,1)}, bf16[128,128]{1,0:T(8,128)(2,1)}, bf16[128,128]{...) custom-call(s32[8,32]{1,0:T(8,128)S(1)} %select_reduce_fusion.list_ref, ...), custom_call_target="tpu_custom_call" | custom-call | flops 536870912 | bytes 2097152 | tf_op jit(solution)/shard_map/far/pallas_call | solution.py:300
  266.7 1.9 collective-permute-start.9
  268.6 1.5 collective-permute-start.10
  270.1 2.1 collective-permute-start.11
  272.2 2.0 collective-permute-start.12
  274.2 3.0 %collective-permute-start.13 = (bf16[128,128]{1,0:T(8,128)(2,1)}, bf16[128,128]{1,0:T(8,128)(2,1)S(1)}, u32[]{:S(2)}, u32[]{:S(2)}) collective-permute-start(bf16[128,128]{1,0:T(8,128)(2,1)} %get-tuple-element.51), channel_id=1, source_target_pairs={{0,5},{1,6},{2,7},{3,0},{4,1},{5,2},{6,3},{7,4},{8,13},{9,14},{10,... | collective-permute-start | bytes 98312 | tf_op jit(solution)/shard_map/ppermute | solution.py:370
  277.2 1.4 collective-permute-start.14
  279.2 2.1 collective-permute-done.14.refs_6_
  281.3 1.4 collective-permute-done.15.refs_7_
  285.2 2.0 unpack.1
  (64 shorter events, 11.6 us)
Async XLA Ops:
  0.0 21.1 %copy-start = (s32[256,256]{1,0:T(8,128)S(1)}, s32[256,256]{1,0:T(8,128)}, u32[]{:S(2)}) copy-start(s32[256,256]{1,0:T(8,128)} %param.7) | copy-start | bytes 786436
  1.8 34.5 %all-to-all-start = ((bf16[8,128,256]{2,1,0:T(8,128)(2,1)}), bf16[8,128,256]{2,1,0:T(8,128)(2,1)S(1)}, u32[]{:S(2)}, u32[]{:S(2)}) async-start(bf16[8,128,256]{2,1,0:T(8,128)(2,1)} %lead.1), calls=%async_computation | async-start | bytes 1048576 | tf_op jit(solution)/shard_map/all_to_all | solution.py:375
  10.5 10.9 %collective-permute-start.16 = (bf16[128,512]{1,0:T(8,128)(2,1)}, bf16[128,512]{1,0:T(8,128)(2,1)S(1)}, u32[]{:S(2)}, u32[]{:S(2)}) collective-permute-start(bf16[128,512]{1,0:T(8,128)(2,1)} %get-tuple-element.55), channel_id=1, source_target_pairs={{0,1},{1,2},{2,3},{3,4},{4,5},{5,6},{6,7},{7,0},{8,9},{9,10},{10,1... | collective-permute-start | bytes 393224 | tf_op jit(solution)/shard_map/ppermute | solution.py:370
  12.6 10.4 %collective-permute-start.17 = (bf16[128,512]{1,0:T(8,128)(2,1)}, bf16[128,512]{1,0:T(8,128)(2,1)S(1)}, u32[]{:S(2)}, u32[]{:S(2)}) collective-permute-start(bf16[128,512]{1,0:T(8,128)(2,1)} %get-tuple-element.56), channel_id=1, source_target_pairs={{0,2},{1,3},{2,4},{3,5},{4,6},{5,7},{6,0},{7,1},{8,10},{9,11},{10,... | collective-permute-start | bytes 393224 | tf_op jit(solution)/shard_map/ppermute | solution.py:370
  14.0 12.9 %collective-permute-start.18 = (bf16[128,512]{1,0:T(8,128)(2,1)}, bf16[128,512]{1,0:T(8,128)(2,1)S(1)}, u32[]{:S(2)}, u32[]{:S(2)}) collective-permute-start(bf16[128,512]{1,0:T(8,128)(2,1)} %get-tuple-element.57), channel_id=1, source_target_pairs={{0,3},{1,4},{2,5},{3,6},{4,7},{5,0},{6,1},{7,2},{8,11},{9,12},{10,... | collective-permute-start | bytes 393224 | tf_op jit(solution)/shard_map/ppermute | solution.py:370
  16.1 10.9 %collective-permute-start.19 = (bf16[128,512]{1,0:T(8,128)(2,1)}, bf16[128,512]{1,0:T(8,128)(2,1)S(1)}, u32[]{:S(2)}, u32[]{:S(2)}) collective-permute-start(bf16[128,512]{1,0:T(8,128)(2,1)} %get-tuple-element.58), channel_id=1, source_target_pairs={{0,4},{1,5},{2,6},{3,7},{4,0},{5,1},{6,2},{7,3},{8,12},{9,13},{10,... | collective-permute-start | bytes 393224 | tf_op jit(solution)/shard_map/ppermute | solution.py:370
  18.2 9.4 %collective-permute-start.20 = (bf16[128,512]{1,0:T(8,128)(2,1)}, bf16[128,512]{1,0:T(8,128)(2,1)S(1)}, u32[]{:S(2)}, u32[]{:S(2)}) collective-permute-start(bf16[128,512]{1,0:T(8,128)(2,1)} %get-tuple-element.59), channel_id=1, source_target_pairs={{0,5},{1,6},{2,7},{3,0},{4,1},{5,2},{6,3},{7,4},{8,13},{9,14},{10,... | collective-permute-start | bytes 393224 | tf_op jit(solution)/shard_map/ppermute | solution.py:370
  21.4 7.1 %collective-permute-start.21 = (bf16[128,512]{1,0:T(8,128)(2,1)}, bf16[128,512]{1,0:T(8,128)(2,1)S(1)}, u32[]{:S(2)}, u32[]{:S(2)}) collective-permute-start(bf16[128,512]{1,0:T(8,128)(2,1)} %get-tuple-element.60), channel_id=1, source_target_pairs={{0,6},{1,7},{2,0},{3,1},{4,2},{5,3},{6,4},{7,5},{8,14},{9,15},{10,... | collective-permute-start | bytes 393224 | tf_op jit(solution)/shard_map/ppermute | solution.py:370
  22.9 7.3 %collective-permute-start.22 = (bf16[128,512]{1,0:T(8,128)(2,1)}, bf16[128,512]{1,0:T(8,128)(2,1)S(1)}, u32[]{:S(2)}, u32[]{:S(2)}) collective-permute-start(bf16[128,512]{1,0:T(8,128)(2,1)} %get-tuple-element.61), channel_id=1, source_target_pairs={{0,7},{1,0},{2,1},{3,2},{4,3},{5,4},{6,5},{7,6},{8,15},{9,8},{10,9... | collective-permute-start | bytes 393224 | tf_op jit(solution)/shard_map/ppermute | solution.py:370
  30.2 0.9 copy-start.9
  32.3 1.2 copy-start.3
  36.3 13.0 %copy-start.6 = (bf16[8,128,256]{2,1,0:T(8,128)(2,1)}, bf16[8,128,256]{2,1,0:T(8,128)(2,1)S(1)}, u32[]{:S(2)}) copy-start(bf16[8,128,256]{2,1,0:T(8,128)(2,1)S(1)} %all-to-all-done.kv_ref) | copy-start | bytes 1572868
  36.4 105.4 %all-to-all-start.2 = ((bf16[32,128,512]{2,1,0:T(8,128)(2,1)}), bf16[32,128,512]{2,1,0:T(8,128)(2,1)}, u32[]{:S(2)}, u32[]{:S(2)}) async-start(bf16[32,128,512]{2,1,0:T(8,128)(2,1)} %select.6), calls=%async_computation.2 | async-start | bytes 8388608 | tf_op jit(solution)/shard_map/all_to_all | solution.py:384
  47.1 110.1 %copy-start.4 = (bf16[8,128,512]{2,1,0:T(8,128)(2,1)S(1)}, bf16[8,128,512]{2,1,0:T(8,128)(2,1)}, u32[]{:S(2)}) copy-start(bf16[8,128,512]{2,1,0:T(8,128)(2,1)} %assemble.5.kv_ref) | copy-start | bytes 3145732
  141.8 105.9 %all-to-all-start.1 = ((bf16[32,128,256]{2,1,0:T(8,128)(2,1)}), bf16[32,128,256]{2,1,0:T(8,128)(2,1)S(1)}, u32[]{:S(2)}, u32[]{:S(2)}) async-start(bf16[32,128,256]{2,1,0:T(8,128)(2,1)} %select.5), calls=%async_computation.1 | async-start | bytes 4194304 | tf_op jit(solution)/shard_map/all_to_all | solution.py:380
  152.0 12.9 %collective-permute-start = (bf16[128,384]{1,0:T(8,128)(2,1)}, bf16[128,384]{1,0:T(8,128)(2,1)S(1)}, u32[]{:S(2)}, u32[]{:S(2)}) collective-permute-start(bf16[128,384]{1,0:T(8,128)(2,1)} %get-tuple-element.36), channel_id=1, source_target_pairs={{0,1},{1,2},{2,3},{3,4},{4,5},{5,6},{6,7},{7,0},{8,9},{9,10},{10,1... | collective-permute-start | bytes 294920 | tf_op jit(solution)/shard_map/ppermute | solution.py:370
  153.1 14.4 %collective-permute-start.1 = (bf16[128,384]{1,0:T(8,128)(2,1)}, bf16[128,384]{1,0:T(8,128)(2,1)}, u32[]{:S(2)}, u32[]{:S(2)}) collective-permute-start(bf16[128,384]{1,0:T(8,128)(2,1)} %get-tuple-element.37), channel_id=1, source_target_pairs={{0,2},{1,3},{2,4},{3,5},{4,6},{5,7},{6,0},{7,1},{8,10},{9,11},{10,... | collective-permute-start | bytes 294920 | tf_op jit(solution)/shard_map/ppermute | solution.py:370
  154.5 17.1 %collective-permute-start.2 = (bf16[128,384]{1,0:T(8,128)(2,1)}, bf16[128,384]{1,0:T(8,128)(2,1)}, u32[]{:S(2)}, u32[]{:S(2)}) collective-permute-start(bf16[128,384]{1,0:T(8,128)(2,1)} %get-tuple-element.38), channel_id=1, source_target_pairs={{0,3},{1,4},{2,5},{3,6},{4,7},{5,0},{6,1},{7,2},{8,11},{9,12},{10,... | collective-permute-start | bytes 294920 | tf_op jit(solution)/shard_map/ppermute | solution.py:370
  157.2 65.3 %collective-permute-start.23 = (bf16[1024,512]{1,0:T(8,128)(2,1)S(1)}, bf16[1024,512]{1,0:T(8,128)(2,1)S(1)}, u32[]{:S(2)}, u32[]{:S(2)}) collective-permute-start(bf16[1024,512]{1,0:T(8,128)(2,1)S(1)} %bitcast.11), channel_id=1, source_target_pairs={{0,8},{8,16},{16,24},{24,32},{32,40},{40,48},{48,56},{56,64},{64,7... | collective-permute-start | bytes 3145736 | tf_op jit(solution)/shard_map/ppermute | solution.py:388
  159.2 63.4 %collective-permute-start.24 = (bf16[1024,512]{1,0:T(8,128)(2,1)S(1)}, bf16[1024,512]{1,0:T(8,128)(2,1)S(1)}, u32[]{:S(2)}, u32[]{:S(2)}) collective-permute-start(bf16[1024,512]{1,0:T(8,128)(2,1)S(1)} %bitcast.12), channel_id=1, source_target_pairs={{8,0},{16,8},{24,16},{32,24},{40,32},{48,40},{56,48},{64,56},{72,6... | collective-permute-start | bytes 3145736 | tf_op jit(solution)/shard_map/ppermute | solution.py:389
  164.9 7.3 %collective-permute-start.3 = (bf16[128,384]{1,0:T(8,128)(2,1)}, bf16[128,384]{1,0:T(8,128)(2,1)S(1)}, u32[]{:S(2)}, u32[]{:S(2)}) collective-permute-start(bf16[128,384]{1,0:T(8,128)(2,1)} %get-tuple-element.39), channel_id=1, source_target_pairs={{0,4},{1,5},{2,6},{3,7},{4,0},{5,1},{6,2},{7,3},{8,12},{9,13},{10,... | collective-permute-start | bytes 294920 | tf_op jit(solution)/shard_map/ppermute | solution.py:370
  167.5 7.9 %collective-permute-start.4 = (bf16[128,384]{1,0:T(8,128)(2,1)}, bf16[128,384]{1,0:T(8,128)(2,1)S(1)}, u32[]{:S(2)}, u32[]{:S(2)}) collective-permute-start(bf16[128,384]{1,0:T(8,128)(2,1)} %get-tuple-element.40), channel_id=1, source_target_pairs={{0,5},{1,6},{2,7},{3,0},{4,1},{5,2},{6,3},{7,4},{8,13},{9,14},{10,... | collective-permute-start | bytes 294920 | tf_op jit(solution)/shard_map/ppermute | solution.py:370
  171.6 5.2 %collective-permute-start.5 = (bf16[128,384]{1,0:T(8,128)(2,1)}, bf16[128,384]{1,0:T(8,128)(2,1)S(1)}, u32[]{:S(2)}, u32[]{:S(2)}) collective-permute-start(bf16[128,384]{1,0:T(8,128)(2,1)} %get-tuple-element.41), channel_id=1, source_target_pairs={{0,6},{1,7},{2,0},{3,1},{4,2},{5,3},{6,4},{7,5},{8,14},{9,15},{10,... | collective-permute-start | bytes 294920 | tf_op jit(solution)/shard_map/ppermute | solution.py:370
  172.2 40.7 %collective-permute-start.6 = (bf16[128,384]{1,0:T(8,128)(2,1)}, bf16[128,384]{1,0:T(8,128)(2,1)S(1)}, u32[]{:S(2)}, u32[]{:S(2)}) collective-permute-start(bf16[128,384]{1,0:T(8,128)(2,1)} %get-tuple-element.42), channel_id=1, source_target_pairs={{0,7},{1,0},{2,1},{3,2},{4,3},{5,4},{6,5},{7,6},{8,15},{9,8},{10,9... | collective-permute-start | bytes 294920 | tf_op jit(solution)/shard_map/ppermute | solution.py:370
  212.8 0.9 copy-start.10
  215.5 36.3 %collective-permute-start.7 = (bf16[1024,256]{1,0:T(8,128)(2,1)}, bf16[1024,256]{1,0:T(8,128)(2,1)}, u32[]{:S(2)}, u32[]{:S(2)}) collective-permute-start(bf16[1024,256]{1,0:T(8,128)(2,1)} %bitcast.14), channel_id=1, source_target_pairs={{0,8},{8,16},{16,24},{24,32},{32,40},{40,48},{48,56},{56,64},{64,7... | collective-permute-start | bytes 1572872 | tf_op jit(solution)/shard_map/ppermute | solution.py:386
  217.4 34.4 %collective-permute-start.8 = (bf16[1024,256]{1,0:T(8,128)(2,1)}, bf16[1024,256]{1,0:T(8,128)(2,1)}, u32[]{:S(2)}, u32[]{:S(2)}) collective-permute-start(bf16[1024,256]{1,0:T(8,128)(2,1)} %bitcast.15), channel_id=1, source_target_pairs={{8,0},{16,8},{24,16},{32,24},{40,32},{48,40},{56,48},{64,56},{72,6... | collective-permute-start | bytes 1572872 | tf_op jit(solution)/shard_map/ppermute | solution.py:387
  222.6 1.1 copy-start.1
  223.7 1.2 copy-start.5
  225.0 12.4 %copy-start.2 = (bf16[8,128,384]{2,1,0:T(8,128)(2,1)S(1)}, bf16[8,128,384]{2,1,0:T(8,128)(2,1)}, u32[]{:S(2)}) copy-start(bf16[8,128,384]{2,1,0:T(8,128)(2,1)} %assemble.3) | copy-start | bytes 2359300
  247.6 36.6 %all-to-all-start.3 = ((bf16[8,128,256]{2,1,0:T(8,128)(2,1)}), bf16[8,128,256]{2,1,0:T(8,128)(2,1)}, u32[]{:S(2)}, u32[]{:S(2)}) async-start(bf16[8,128,256]{2,1,0:T(8,128)(2,1)} %bitcast.17), calls=%async_computation.3 | async-start | bytes 1048576 | tf_op jit(solution)/shard_map/all_to_all | solution.py:397
  251.8 1.0 copy-start.7
  266.7 10.5 %collective-permute-start.9 = (bf16[128,128]{1,0:T(8,128)(2,1)}, bf16[128,128]{1,0:T(8,128)(2,1)S(1)}, u32[]{:S(2)}, u32[]{:S(2)}) collective-permute-start(bf16[128,128]{1,0:T(8,128)(2,1)} %get-tuple-element.47), channel_id=1, source_target_pairs={{0,1},{1,2},{2,3},{3,4},{4,5},{5,6},{6,7},{7,0},{8,9},{9,10},{10,1... | collective-permute-start | bytes 98312 | tf_op jit(solution)/shard_map/ppermute | solution.py:370
  268.6 10.1 %collective-permute-start.10 = (bf16[128,128]{1,0:T(8,128)(2,1)}, bf16[128,128]{1,0:T(8,128)(2,1)S(1)}, u32[]{:S(2)}, u32[]{:S(2)}) collective-permute-start(bf16[128,128]{1,0:T(8,128)(2,1)} %get-tuple-element.48), channel_id=1, source_target_pairs={{0,2},{1,3},{2,4},{3,5},{4,6},{5,7},{6,0},{7,1},{8,10},{9,11},{10,... | collective-permute-start | bytes 98312 | tf_op jit(solution)/shard_map/ppermute | solution.py:370
  270.1 8.6 %collective-permute-start.11 = (bf16[128,128]{1,0:T(8,128)(2,1)}, bf16[128,128]{1,0:T(8,128)(2,1)S(1)}, u32[]{:S(2)}, u32[]{:S(2)}) collective-permute-start(bf16[128,128]{1,0:T(8,128)(2,1)} %get-tuple-element.49), channel_id=1, source_target_pairs={{0,3},{1,4},{2,5},{3,6},{4,7},{5,0},{6,1},{7,2},{8,11},{9,12},{10,... | collective-permute-start | bytes 98312 | tf_op jit(solution)/shard_map/ppermute | solution.py:370
  272.2 6.5 %collective-permute-start.12 = (bf16[128,128]{1,0:T(8,128)(2,1)}, bf16[128,128]{1,0:T(8,128)(2,1)S(1)}, u32[]{:S(2)}, u32[]{:S(2)}) collective-permute-start(bf16[128,128]{1,0:T(8,128)(2,1)} %get-tuple-element.50), channel_id=1, source_target_pairs={{0,4},{1,5},{2,6},{3,7},{4,0},{5,1},{6,2},{7,3},{8,12},{9,13},{10,... | collective-permute-start | bytes 98312 | tf_op jit(solution)/shard_map/ppermute | solution.py:370
  274.2 5.0 %collective-permute-start.13 = (bf16[128,128]{1,0:T(8,128)(2,1)}, bf16[128,128]{1,0:T(8,128)(2,1)S(1)}, u32[]{:S(2)}, u32[]{:S(2)}) collective-permute-start(bf16[128,128]{1,0:T(8,128)(2,1)} %get-tuple-element.51), channel_id=1, source_target_pairs={{0,5},{1,6},{2,7},{3,0},{4,1},{5,2},{6,3},{7,4},{8,13},{9,14},{10,... | collective-permute-start | bytes 98312 | tf_op jit(solution)/shard_map/ppermute | solution.py:370
  277.2 4.1 %collective-permute-start.14 = (bf16[128,128]{1,0:T(8,128)(2,1)}, bf16[128,128]{1,0:T(8,128)(2,1)S(1)}, u32[]{:S(2)}, u32[]{:S(2)}) collective-permute-start(bf16[128,128]{1,0:T(8,128)(2,1)} %get-tuple-element.52), channel_id=1, source_target_pairs={{0,6},{1,7},{2,0},{3,1},{4,2},{5,3},{6,4},{7,5},{8,14},{9,15},{10,... | collective-permute-start | bytes 98312 | tf_op jit(solution)/shard_map/ppermute | solution.py:370
  278.7 4.1 %collective-permute-start.15 = (bf16[128,128]{1,0:T(8,128)(2,1)}, bf16[128,128]{1,0:T(8,128)(2,1)S(1)}, u32[]{:S(2)}, u32[]{:S(2)}) collective-permute-start(bf16[128,128]{1,0:T(8,128)(2,1)} %get-tuple-element.53), channel_id=1, source_target_pairs={{0,7},{1,0},{2,1},{3,2},{4,3},{5,4},{6,5},{7,6},{8,15},{9,8},{10,9... | collective-permute-start | bytes 98312 | tf_op jit(solution)/shard_map/ppermute | solution.py:370
  282.8 0.8 copy-start.11
  284.3 1.0 copy-start.8
